TPU v7x, 128 devices: a whole 4x4x4 slice. The times are simulated.
128 devices in a mesh: wide: 16 (over x, y_lo, core), narrow: 8 (over y_hi, z).
Axes of the slice: x: 4, y: 4 (y_hi: 2, y_lo: 2; y = y_hi * 2 + y_lo), z: 4, core: 2. Of those that a mesh axis runs over, the one named last changes fastest.
Arguments:
- fit_rows: bfloat16 [3072, 49152], P('narrow', 'wide'), may hold values from -0.0546875 to 0.0546875
- trials: bfloat16 [32, 49152], P(None, 'wide'), may hold values from -6 to 6
- occ_energy: float32 [64], replicated, may hold values from -1.2 to -0.3
- vir_energy: float32 [768], replicated, may hold values from 0.1 to 2
Outputs:
- sigma: float32 [32, 49152], P(None, 'wide')
All inputs are finite; a program needn't handle non-finite values.
Results may differ from a plain program's by a relative error of at most 0.004.
Values may be sent and summed in bfloat16 or wider, within the bound.
No kernel may reach another device: no remote copies, remote signals or barrier semaphores. Data moves between devices by JAX's collectives and lax.ppermute only.
A program may use at most 64 MiB of HBM per device.

v0:
```python
import math

import jax
import jax.numpy as jnp
from jax import lax
from jax.sharding import PartitionSpec as P

NOCC = 64
NVIR = 768
NVEC = 32


def local(fit_rows, trials, occ_energy, vir_energy):
    wide_count = lax.axis_size("wide")
    pair_local = fit_rows.shape[1]
    fitvec = lax.dot_general(
        fit_rows, trials, (((1,), (1,)), ((), ())), preferred_element_type=jnp.float32
    )
    fitvec = lax.psum(fitvec, "wide")
    fitvec_b = fitvec.astype(jnp.bfloat16)
    coulomb = 2.0 * lax.dot_general(
        fitvec_b, fit_rows, (((0,), (0,)), ((), ())), preferred_element_type=jnp.float32
    )
    full_trials = lax.all_gather(trials, "wide", axis=1, tiled=True)
    aux_rows = lax.all_to_all(fit_rows, "wide", split_axis=0, concat_axis=1, tiled=True)
    aux_count = aux_rows.shape[0]
    block = math.gcd(aux_count, 8)
    blocks = aux_rows.reshape(aux_count // block, block, NOCC, NVIR)
    vectors = full_trials.reshape(NVEC, NOCC, NVIR)

    def step(carry, rows):
        inter = jnp.einsum(
            "pib,njb->pnij", rows, vectors, preferred_element_type=jnp.float32
        ).astype(jnp.bfloat16)
        term = jnp.einsum("pnij,pja->nia", inter, rows, preferred_element_type=jnp.float32)
        return (carry + term, None)

    exchange, _ = lax.scan(step, jnp.zeros((NVEC, NOCC, NVIR), jnp.float32), blocks)
    negated = -exchange.reshape(NVEC, NOCC * NVIR)
    wide_index = lax.axis_index("wide")
    occ_local = NOCC // wide_count
    occ_slice = lax.dynamic_slice_in_dim(occ_energy, wide_index * occ_local, occ_local)
    delta = (vir_energy[None, :] - occ_slice[:, None]).reshape(pair_local)
    diagonal_term = delta[None, :] * trials.astype(jnp.float32)
    share = lax.psum_scatter(negated, ("wide", "narrow"), scatter_dimension=1, tiled=True)
    combined = lax.all_gather(share.astype(jnp.bfloat16), "narrow", axis=1, tiled=True).astype(
        share.dtype
    )
    combined = combined + lax.psum(coulomb, "narrow")
    return diagonal_term + combined


def solution(mesh):
    in_specs = (P("narrow", "wide"), P(None, "wide"), P(), P())
    out_specs = P(None, "wide")
    return jax.shard_map(local, mesh=mesh, in_specs=in_specs, out_specs=out_specs, check_vma=False)
```

profile of v0, /device:TPU:0, one launch (start us, length us, event | category | flops | bytes accessed | tf_op | source)
XLA Modules:
  0.0 805.7 jit_solution(1953897362560750049)
XLA Ops:
  7.4 0.0 all-gather.2.cloned.1.call-start
  7.4 0.7 all-gather.2.cloned.1.call-update
  8.1 5.5 all-to-all-start
  13.6 0.0 reduce-scatter.2.cloned.1.call-start
  13.7 35.1 %all-to-all-done = bf16[16,24,3072]{2,1,0:T(8,128)(2,1)S(1)} async-done(((bf16[16,24,3072]{2,1,0:T(8,128)(2,1)}), bf16[16,24,3072]{2,1,0:T(8,128)(2,1)S(1)}, u32[]{:S(2)}, u32[]{:S(2)}) %all-to-all-start) | async-done | bytes 2359328 | tf_op jit(solution)/shard_map/all_to_all | solution.py:25
  48.8 2.8 copy.6
  51.5 4.9 reshape.28
  56.4 9.0 %all-gather.2.cloned.1.call-done = bf16[32,49152]{1,0:T(8,128)(2,1)} async-done(((bf16[32,3072]{1,0:T(8,128)(2,1)}), bf16[32,49152]{1,0:T(8,128)(2,1)}) %all-gather.2.cloned.1.call-update) | async-done | bytes 3145744 | tf_op jit(solution)/shard_map/all_gather | solution.py:24
  65.4 2.6 copy.9
  68.0 26.7 %while.11 = (s32[]{:T(128)}, f32[32,64,768]{2,1,0:T(8,128)}, bf16[3,8,64,768]{3,2,1,0:T(8,128)(2,1)}, bf16[32,64,768]{2,1,0:T(8,128)(2,1)S(1)}, s32[]{:T(128)}, /*index=5*/s32[]{:T(128)}) while((s32[]{:T(128)}, f32[32,64,768]{2,1,0:T(8,128)}, bf16[3,8,64,768]{3,2,1,0:T(8,128)(2,1)}, bf16[32,64,768]{2,1,0:T(8,128)(2,1)S(1)}, ...), condition=%wide.region_1.2_spmd.clone, body=%wide.region_0.0_spmd.clone.sunk | while | flops 3225419776 | bytes 17302604 | solution.py:38
  68.0 8.3 %bitcast_add_fusion.2 = f32[32,64,768]{2,1,0:T(8,128)} fusion(f32[32,64,768]{2,1,0:T(8,128)} %get-tuple-element.83, pred[]{:T(512)S(6)} %compare.3, bf16[32,64,768]{2,1,0:T(8,128)(2,1)S(1)} %get-tuple-element.91, bf16[3,8,64,768]{3,2,1,0:T(8,128)(2,1)} %get-tuple-element.90, s32[]{:T(128)} %get-tuple-element.82), kind=kOutput, calls=%fused_computation.clone.1 | convolution fusion | flops 3225419776 | bytes 17302528 | tf_op jit(solution)/shard_map/while/body/eval_jaxpr/pnij,pja->nia/dot_general | solution.py:35
  76.3 9.2 %bitcast_add_fusion.2 = f32[32,64,768]{2,1,0:T(8,128)} fusion(f32[32,64,768]{2,1,0:T(8,128)} %get-tuple-element.83, pred[]{:T(512)S(6)} %compare.3, bf16[32,64,768]{2,1,0:T(8,128)(2,1)S(1)} %get-tuple-element.91, bf16[3,8,64,768]{3,2,1,0:T(8,128)(2,1)} %get-tuple-element.90, s32[]{:T(128)} %get-tuple-element.82), kind=kOutput, calls=%fused_computation.clone.1 | convolution fusion | flops 3225419776 | bytes 17302528 | tf_op jit(solution)/shard_map/while/body/eval_jaxpr/pnij,pja->nia/dot_general | solution.py:35
  85.5 9.2 %bitcast_add_fusion.2 = f32[32,64,768]{2,1,0:T(8,128)} fusion(f32[32,64,768]{2,1,0:T(8,128)} %get-tuple-element.83, pred[]{:T(512)S(6)} %compare.3, bf16[32,64,768]{2,1,0:T(8,128)(2,1)S(1)} %get-tuple-element.91, bf16[3,8,64,768]{3,2,1,0:T(8,128)(2,1)} %get-tuple-element.90, s32[]{:T(128)} %get-tuple-element.82), kind=kOutput, calls=%fused_computation.clone.1 | convolution fusion | flops 3225419776 | bytes 17302528 | tf_op jit(solution)/shard_map/while/body/eval_jaxpr/pnij,pja->nia/dot_general | solution.py:35
  94.7 3.5 neg.6
  98.2 6.3 copy.10
  104.5 0.0 copy-start
  104.5 0.0 copy-start.1
  104.5 0.0 reduce-scatter.2.cloned.1.call-update
  104.5 0.0 copy-start.3
  104.5 0.0 copy-start.2
  104.5 0.0 all-reduce.2.cloned.1.call-start
  104.6 1.6 copy-done
  106.2 0.0 copy-done.1
  106.2 0.8 fusion.18
  106.9 54.7 %psum.14 = bf16[384,32]{0,1:T(8,128)(2,1)S(1)} all-reduce(f32[384,32]{0,1:T(8,128)S(1)} %fusion.18), channel_id=1, replica_groups=mesh['wide'=16,'narrow'=8] {'wide'}, use_global_device_ids=true, to_apply=%region_3.4 | all-reduce | flops 12288 | bytes 73728 | tf_op jit(solution)/shard_map/psum | solution.py:19
  161.6 1.3 convolution_multiply_fusion
  162.9 0.0 all-reduce.2.cloned.1.call-update
  162.9 0.0 copy-done.3
  162.9 0.1 dynamic_slice.7
  163.0 0.0 copy-done.2
  163.0 0.1 broadcast_subtract_fusion
  163.1 598.3 %reduce-scatter.2.cloned.1.call-done = f32[32,384]{1,0:T(8,128)} async-done(((f32[32,49152]{1,0:T(8,128)}), f32[32,384]{1,0:T(8,128)}) %reduce-scatter.2.cloned.1.call-update) | async-done | bytes 49168 | tf_op jit(solution)/shard_map/reduce_scatter | solution.py:45
  761.4 0.8 convert_element_type.19
  762.2 34.3 %all_gather.7 = bf16[32,3072]{1,0:T(8,128)(2,1)S(1)} all-gather(bf16[32,384]{1,0:T(8,128)(2,1)S(1)} %convert_element_type.19), channel_id=1, replica_groups=mesh['wide'=16,'narrow'=8] {'narrow'}, dimensions={1}, use_global_device_ids=true | all-gather | bytes 221184 | tf_op jit(solution)/shard_map/all_gather | solution.py:46
  796.5 0.0 all-reduce.2.cloned.1.call-done
  796.5 1.8 add_add_fusion
  (2 shorter events, 0.0 us)
Async XLA Ops:
  7.4 58.0 %all-gather.2.cloned.1.call-start = ((), (), s32[]{:S(2)}) async-start(), calls=%async_computation.2 | async-start | bytes 3342336 | tf_op jit(solution)/shard_map/all_gather | solution.py:24
  8.1 40.7 %all-to-all-start = ((bf16[16,24,3072]{2,1,0:T(8,128)(2,1)}), bf16[16,24,3072]{2,1,0:T(8,128)(2,1)S(1)}, u32[]{:S(2)}, u32[]{:S(2)}) async-start(bf16[16,24,3072]{2,1,0:T(8,128)(2,1)} %bitcast.43), calls=%async_computation | async-start | bytes 4718592 | tf_op jit(solution)/shard_map/all_to_all | solution.py:25
  13.6 747.7 %reduce-scatter.2.cloned.1.call-start = ((), (), s32[]{:S(2)}) async-start(), calls=%async_computation.3 | async-start | bytes 6340608 | tf_op jit(solution)/shard_map/reduce_scatter | solution.py:45
  104.5 1.7 copy-start
  104.5 1.7 copy-start.1
  104.5 58.4 %copy-start.3 = (f32[64]{0:T(128)S(1)}, f32[64]{0:T(128)}, u32[]{:S(2)}) copy-start(f32[64]{0:T(128)} %param.8) | copy-start | bytes 772
  104.5 58.5 %copy-start.2 = (f32[768]{0:T(1024)S(1)}, f32[768]{0:T(1024)}, u32[]{:S(2)}) copy-start(f32[768]{0:T(1024)} %param.9) | copy-start | bytes 9220
  104.5 692.0 %all-reduce.2.cloned.1.call-start = ((), (), s32[]{:S(2)}) async-start(), calls=%async_computation.4 | async-start | bytes 786432 | tf_op jit(solution)/shard_map/psum | solution.py:49
Sparse Core Ops, SparseCore 0:
  9.8 55.5 all-gather.1
  104.6 656.6 reduce-scatter.1
Sparse Core Ops, SparseCore 1:
  163.0 87.1 all-reduce.1
where the time goes:
time: 806 us
  waiting for transfers between devices  643 us (80%)
  blocking collectives  89 us (11%)
  matrix products  28.7 us (4%)
  local copies, waits for them, and re-layouts  18.2 us (2%)
  between operations  14.9 us (2%)
    reduce_scatter x1, waiting for transfers between devices, local(): lax.psum_scatter(negated, ('wide', 'narrow'), scatter_dimension=1, tiled=...  598 us
    psum x1, blocking collectives, local(): fitvec = lax.psum(fitvec, 'wide')  54.7 us
    all_to_all x1, waiting for transfers between devices, local(): lax.all_to_all(fit_rows, 'wide', split_axis=0, concat_axis=1, tiled=True)  35.1 us
    all_gather x1, blocking collectives, local(): lax.all_gather(share.astype(jnp.bfloat16), 'narrow', axis=1, tiled=True)  34.3 us
    dot_general x3, matrix products, step(): jnp.einsum('pnij,pja->nia', inter, rows, preferred_element_type=jnp.float32)  26.6 us
  transfers between devices with their start and end apart: 4, of which 3 were waited for; matrix products, arithmetic and copies ran while one was open for 1% of the time, Pallas kernels for 0%

commit v1 on v0

v1 whole, which is shorter than its diff:
```python
import jax
import jax.numpy as jnp
from jax import lax
from jax.experimental import pallas as pl
from jax.experimental.pallas import tpu as pltpu
from jax.sharding import Mesh, PartitionSpec as P

NOCC = 64
NVIR = 768
NVEC = 32
NCHIP = 8
OCC_DEV = 4
HALF = 16
CHUNKS = 3
ROWS = NOCC * HALF

F32 = jnp.float32
BF16 = jnp.bfloat16


def swap_blocks(tile):
    v = [tile[j * 16 : (j + 1) * 16] for j in range(8)]
    lane = lax.broadcasted_iota(jnp.int32, (16, 128), 1)
    for s in (4, 2, 1):
        bit = (lane & (16 * s)) != 0
        new = list(v)
        for j in range(8):
            if j & s:
                continue
            lo, hi = v[j], v[j + s]
            new[j] = jnp.where(bit, pltpu.roll(hi, 16 * s, 1), lo)
            new[j + s] = jnp.where(bit, hi, pltpu.roll(lo, 128 - 16 * s, 1))
        v = new
    return v


def chunk_kernel(first, last, *refs):
    if first:
        core, xg, b_own, b_other, out, x2, b2, d, c_buf, fit, sems = refs
        acc = out
    elif last:
        core, xg, b_own, b_other, acc, out, x2, b2, d, c_buf, fit, sems = refs
    else:
        core, xg, b_own, b_other, acc, out, x2, b2, d, c_buf, fit, sems = refs
    c = core[0]
    copies = []
    for rel in range(2):
        src_b = b_own if rel == 0 else b_other
        for chip in range(NCHIP):
            for q in range(OCC_DEV):
                row = ((rel * NCHIP + chip) * OCC_DEV + q) * 16
                copies.append(pltpu.make_async_copy(src_b.at[chip, :, pl.ds(q * NVIR, NVIR)], b2.at[pl.ds(row, 16), :], sems.at[0]))
                w = chip * 2 + (c ^ rel)
                copies.append(pltpu.make_async_copy(xg.at[w, :, pl.ds(q * NVIR, NVIR)], x2.at[pl.ds(row, 16), :], sems.at[0]))
    for cp in copies:
        cp.start()
    for cp in copies:
        cp.wait()
    row_i = lax.broadcasted_iota(jnp.int32, (128, 128), 0) // 16
    lane_i = lax.broadcasted_iota(jnp.int32, (128, 128), 1) // 16
    diag = row_i == lane_i
    fit[...] = jnp.zeros_like(fit)

    @pl.loop(0, 4)
    def _(ig2):
        rhs = b2[pl.ds(pl.multiple_of(ig2 * 256, 256), 256), :]
        c_buf[...] = lax.dot_general(x2[...], rhs, (((1,), (1,)), ((), ())), preferred_element_type=F32)
        for half in range(2):
            ig = ig2 * 2 + half
            own = c_buf[pl.ds(pl.multiple_of(ig * 128, 128), 128), half * 128 : (half + 1) * 128]
            fit[...] += jnp.where(diag, own, 0.0)
            for jg in range(8):
                tile = c_buf[jg * 128 : (jg + 1) * 128, half * 128 : (half + 1) * 128]
                t = swap_blocks(tile)
                d[pl.ds(pl.multiple_of(ig * 128, 128), 128), jg * 128 : (jg + 1) * 128] = jnp.concatenate(t, 0).astype(BF16)

    total = fit[0:16, :]
    for j in range(1, 8):
        total = total + fit[j * 16 : (j + 1) * 16, :]
    for s in (64, 32, 16):
        total = total + pltpu.roll(total, s, 1)
    fit_b = 2.0 * total.astype(BF16).astype(F32)
    sub = jnp.where(diag, jnp.concatenate([fit_b] * 8, 0), 0.0)
    for g in range(8):
        s = slice(g * 128, (g + 1) * 128)
        d[s, s] = (d[s, s].astype(F32) - sub).astype(BF16)

    for rb in range(4):
        rows = slice(rb * 256, (rb + 1) * 256)
        term = jnp.dot(d[rows, :], b2[...], preferred_element_type=F32)
        if not first:
            term = term + acc[rows, :]
        if not last:
            out[rows, :] = term
        else:
            for k in range(16):
                i = rb * 16 + k
                rel, chip, q = i // 32, (i // 4) % 8, i % 4
                w = chip * 2 + (c ^ rel)
                out[w, :, q * NVIR : (q + 1) * NVIR] = term[k * 16 : (k + 1) * 16, :].astype(BF16)


def chunk(core, xg, b_own, b_other, acc, last):
    first = acc is None
    hbm = pl.BlockSpec(memory_space=pl.ANY)
    vmem = pl.BlockSpec(memory_space=pltpu.VMEM)
    args = [core, xg, b_own, b_other] + ([] if first else [acc])
    specs = [pl.BlockSpec(memory_space=pltpu.SMEM), hbm, hbm, hbm] + ([] if first else [vmem])
    out = jax.ShapeDtypeStruct((16, HALF, OCC_DEV * NVIR), BF16) if last else jax.ShapeDtypeStruct((ROWS, NVIR), F32)
    flops = 2 * 2 * ROWS * ROWS * NVIR
    return pl.pallas_call(
        lambda *refs: chunk_kernel(first, last, *refs),
        out_shape=out,
        in_specs=specs,
        out_specs=vmem,
        scratch_shapes=[
            pltpu.VMEM((ROWS, NVIR), BF16),
            pltpu.VMEM((ROWS, NVIR), BF16),
            pltpu.VMEM((ROWS, ROWS), BF16),
            pltpu.VMEM((ROWS, 256), F32),
            pltpu.VMEM((128, 128), F32),
            pltpu.SemaphoreType.DMA((1,)),
        ],
        cost_estimate=pl.CostEstimate(flops=flops, bytes_accessed=4 * ROWS * NVIR * 2, transcendentals=0),
        compiler_params=pltpu.CompilerParams(vmem_limit_bytes=40 << 20),
        name="terms_last" if last else "terms_first" if first else "terms_mid",
    )(*args)


CHIPS = ("x", "yl")
WIDE = ("x", "yl", "c")
NARROW = ("yh", "z")


def local(fit_rows, trials, occ_energy, vir_energy):
    core = lax.axis_index("c").astype(jnp.int32).reshape(1)
    blocks = fit_rows.reshape(CHUNKS, NCHIP, HALF, OCC_DEV * NVIR)
    own = [lax.all_to_all(blocks[t], CHIPS, 0, 0, tiled=True) for t in range(CHUNKS)]
    other = [lax.ppermute(own[t], "c", [(0, 1), (1, 0)]) for t in range(CHUNKS)]
    halves = trials.reshape(1, 2, HALF, OCC_DEV * NVIR)
    send = jnp.broadcast_to(halves, (NCHIP, 2, HALF, OCC_DEV * NVIR)).reshape(16, HALF, OCC_DEV * NVIR)
    xg = lax.all_to_all(send, WIDE, 0, 0, tiled=True)
    acc = None
    for t in range(CHUNKS):
        acc = chunk(core, xg, own[t], other[t], acc, t == CHUNKS - 1)
    parts = lax.all_to_all(acc, WIDE, 0, 0, tiled=True)
    part = jnp.sum(parts.reshape(NCHIP, 2 * HALF, OCC_DEV * NVIR).astype(F32), 0).astype(BF16)
    every = lax.all_to_all(jnp.broadcast_to(part[None], (8, NVEC, OCC_DEV * NVIR)), NARROW, 0, 0, tiled=True)
    total = jnp.sum(every.astype(F32), 0)
    w = lax.axis_index(WIDE)
    occ = lax.dynamic_slice_in_dim(occ_energy, w * OCC_DEV, OCC_DEV)
    delta = (vir_energy[None, :] - occ[:, None]).reshape(OCC_DEV * NVIR)
    return delta[None, :] * trials.astype(F32) - total


def solution(mesh):
    fine = Mesh(mesh.devices.reshape(4, 2, 2, 2, 4), ("x", "yl", "c", "yh", "z"))
    in_specs = (P(NARROW, WIDE), P(None, WIDE), P(), P())
    return jax.shard_map(local, mesh=fine, in_specs=in_specs, out_specs=P(None, WIDE), check_vma=False)
```

time: 806 us -> 158 us (0.20)
  waiting for transfers between devices: 643 us -> 41.3 us
  matrix products: 28.7 us -> 0 us
  Pallas kernels: 0 us -> 24.7 us
  blocking collectives: 89 us -> 71.6 us
  between operations: 14.9 us -> 0.07 us
  local copies, waits for them, and re-layouts: 18.2 us -> 5.66 us
    reduce_scatter x1 -> x0, waiting for transfers between devices: 598 us -> none  [local(): lax.psum_scatter(negated, ('wide', 'narrow'), scatter_dimension=1, tiled=...]
    all_to_all x0 -> x4, blocking collectives: none -> 71.6 us  [the longest x3 45.8 us: local(): lax.all_to_all(blocks[t], CHIPS, 0, 0, tiled=True)]
    psum x1 -> x0, blocking collectives: 54.7 us -> none  [local(): fitvec = lax.psum(fitvec, 'wide')]
    all_gather x1 -> x0, blocking collectives: 34.3 us -> none  [local(): lax.all_gather(share.astype(jnp.bfloat16), 'narrow', axis=1, tiled=True)]
    dot_general x5 -> x0, matrix products: 28.7 us -> none  [the longest x3 26.6 us: step(): jnp.einsum('pnij,pja->nia', inter, rows, preferred_element_type=jnp.float32)]
    pallas_call x0 -> x3, Pallas kernels: none -> 24.7 us  [chunk(): pl.pallas_call(lambda *refs: chunk_kernel(first, last, *refs), out_shape=...]
    unnamed x10 -> x8, local copies, waits for them, and re-layouts: 10.5 us -> 1.14 us
    all_gather x1 -> x0, waiting for transfers between devices: 8.96 us -> none  [local(): full_trials = lax.all_gather(trials, 'wide', axis=1, tiled=True)]
  transfers between devices with their start and end apart: 4 -> 5, of which waited for: 3 -> 3; matrix products, arithmetic and copies ran while one was open for 1% -> 0% of each run, Pallas kernels for 0% -> 10%
where the time goes in v1:
time: 158 us; the launch traced here: 157 us
  blocking collectives  71.6 us (45%)
  waiting for transfers between devices  41.3 us (26%)
  Pallas kernels  24.7 us (16%)
  starting transfers between devices  12.3 us (8%)
  local copies, waits for them, and re-layouts  5.66 us (4%)
    all_to_all x3, blocking collectives, local(): lax.all_to_all(blocks[t], CHIPS, 0, 0, tiled=True)  45.8 us
    all_to_all x1, blocking collectives, local(): parts = lax.all_to_all(acc, WIDE, 0, 0, tiled=True)  25.7 us
    pallas_call x3, Pallas kernels, chunk(): pl.pallas_call(lambda *refs: chunk_kernel(first, last, *refs), out_shape=...  24.7 us
    all_to_all x1, waiting for transfers between devices, local(): lax.all_to_all(jnp.broadcast_to(part[None], (8, NVEC, OCC_DEV * NVIR)), N...  20.1 us
    all_to_all x1, waiting for transfers between devices, local(): xg = lax.all_to_all(send, WIDE, 0, 0, tiled=True)  19.3 us
    all_to_all x1, starting transfers between devices, local(): lax.all_to_all(jnp.broadcast_to(part[None], (8, NVEC, OCC_DEV * NVIR)), N...  7.78 us
    all_to_all x1, starting transfers between devices, local(): xg = lax.all_to_all(send, WIDE, 0, 0, tiled=True)  3.71 us
  transfers between devices with their start and end apart: 5, of which 3 were waited for; matrix products, arithmetic and copies ran while one was open for 0% of the time, Pallas kernels for 10%

profile of v1, /device:TPU:0, one launch (start us, length us, event | category | flops | bytes accessed | tf_op | source)
XLA Modules:
  0.0 156.9 jit_solution(10665410753685255231)
XLA Ops:
  0.0 1.8 %fusion = (bf16[128,3072]{1,0:T(8,128)(2,1)S(1)}, bf16[128,3072]{1,0:T(8,128)(2,1)S(1)}, bf16[128,3072]{1,0:T(8,128)(2,1)S(1)}) fusion(bf16[384,3072]{1,0:T(8,128)(2,1)} %param.4), kind=kLoop, calls=%fused_computation.4 | loop fusion | bytes 4718592 | tf_op jit(solution)/shard_map/slice | solution.py:138
  1.8 17.9 %all_to_all.30.refs_2_ = bf16[8,16,3072]{2,1,0:T(8,128)(2,1)} all-to-all(bf16[8,16,3072]{2,1,0:T(8,128)(2,1)S(1)} %bitcast.13), channel_id=1, replica_groups=mesh['x'=4,'yl'=2,'c'=2,'yh'=2,'z'=4] {'x','yl'}, dimensions={0} | all-to-all | bytes 1572864 | tf_op jit(solution)/shard_map/all_to_all | solution.py:138
  19.6 0.0 copy-start.1
  19.6 14.5 %all_to_all.31.refs_2_ = bf16[8,16,3072]{2,1,0:T(8,128)(2,1)S(1)} all-to-all(bf16[8,16,3072]{2,1,0:T(8,128)(2,1)S(1)} %bitcast.12), channel_id=1, replica_groups=mesh['x'=4,'yl'=2,'c'=2,'yh'=2,'z'=4] {'x','yl'}, dimensions={0} | all-to-all | bytes 1572864 | tf_op jit(solution)/shard_map/all_to_all | solution.py:138
  34.1 13.5 %all_to_all.32.refs_2_ = bf16[8,16,3072]{2,1,0:T(8,128)(2,1)S(1)} all-to-all(bf16[8,16,3072]{2,1,0:T(8,128)(2,1)S(1)} %bitcast.11), channel_id=1, replica_groups=mesh['x'=4,'yl'=2,'c'=2,'yh'=2,'z'=4] {'x','yl'}, dimensions={0} | all-to-all | bytes 1572864 | tf_op jit(solution)/shard_map/all_to_all | solution.py:138
  47.6 0.0 copy-done.1
  47.6 1.3 broadcast_in_dim.7
  48.9 3.7 %all-to-all-start = ((bf16[16,16,3072]{2,1,0:T(8,128)(2,1)}), bf16[16,16,3072]{2,1,0:T(8,128)(2,1)S(1)}, u32[]{:S(2)}, u32[]{:S(2)}) async-start(bf16[16,16,3072]{2,1,0:T(8,128)(2,1)} %bitcast.9), calls=%async_computation | async-start | bytes 3145728 | tf_op jit(solution)/shard_map/all_to_all | solution.py:142
  52.6 0.3 collective-permute-start.2
  52.9 0.3 collective-permute-start.1
  53.2 0.2 collective-permute-start
  53.4 1.9 %collective-permute-done.2.refs_3_ = bf16[8,16,3072]{2,1,0:T(8,128)(2,1)} collective-permute-done((bf16[8,16,3072]{2,1,0:T(8,128)(2,1)}, bf16[8,16,3072]{2,1,0:T(8,128)(2,1)}, u32[]{:S(2)}, u32[]{:S(2)}) %collective-permute-start.2) | collective-permute-done | bytes 786464 | tf_op jit(solution)/shard_map/ppermute | solution.py:139
  55.3 19.3 %all-to-all-done.refs_1_ = bf16[16,16,3072]{2,1,0:T(8,128)(2,1)S(1)} async-done(((bf16[16,16,3072]{2,1,0:T(8,128)(2,1)}), bf16[16,16,3072]{2,1,0:T(8,128)(2,1)S(1)}, u32[]{:S(2)}, u32[]{:S(2)}) %all-to-all-start) | async-done | bytes 1572896 | tf_op jit(solution)/shard_map/all_to_all | solution.py:142
  74.7 0.0 copy-start
  74.7 1.1 copy-done
  75.8 8.2 %terms_first.1.refs_4_ = f32[1024,768]{1,0:T(8,128)S(1)} custom-call(s32[1]{0:T(128)} %bitcast.refs_0_, bf16[16,16,3072]{2,1,0:T(8,128)(2,1)S(1)} %all-to-all-done.refs_1_, bf16[8,16,3072]{2,1,0:T(8,128)(2,1)S(1)} %copy-done, bf16[8,16,3072]{2,1,0:T(8,128)(2,1)} %collective-permute-done.2.refs_3_), custom_call_target="tpu_custom_call" | custom-call | flops 3221225472 | bytes 6291456 | tf_op jit(solution)/shard_map/terms_first/pallas_call | solution.py:111
  84.0 0.0 collective-permute-done.1.refs_3_
  84.0 8.2 %terms_mid.1.refs_4_ = f32[1024,768]{1,0:T(8,128)S(1)} custom-call(s32[1]{0:T(128)} %bitcast.refs_0_, bf16[16,16,3072]{2,1,0:T(8,128)(2,1)S(1)} %all-to-all-done.refs_1_, bf16[8,16,3072]{2,1,0:T(8,128)(2,1)S(1)} %all_to_all.31.refs_2_, bf16[8,16,3072]{2,1,0:T(8,128)(2,1)} %collective-permute-done.1.refs_3_, f32[1024,768]{1,0:T(8,128)S(1)} %terms_first.1.refs_4_), custom_call_target="tpu_custom_call" | custom-call | flops 3221225472 | bytes 6291456 | tf_op jit(solution)/shard_map/terms_mid/pallas_call | solution.py:111
  92.3 0.0 collective-permute-done.refs_3_
  92.3 8.2 %terms_last.1 = bf16[16,16,3072]{2,1,0:T(8,128)(2,1)S(1)} custom-call(s32[1]{0:T(128)} %bitcast.refs_0_, bf16[16,16,3072]{2,1,0:T(8,128)(2,1)S(1)} %all-to-all-done.refs_1_, bf16[8,16,3072]{2,1,0:T(8,128)(2,1)S(1)} %all_to_all.32.refs_2_, bf16[8,16,3072]{2,1,0:T(8,128)(2,1)} %collective-permute-done.refs_3_, f32[1024,768]{1,0:T(8,128)S(1)} %terms_mid.1.refs_4_), custom_call_target="tpu_custom_call" | custom-call | flops 3221225472 | bytes 6291456 | tf_op jit(solution)/shard_map/terms_last/pallas_call | solution.py:111
  100.5 25.7 %all_to_all.33 = bf16[16,16,3072]{2,1,0:T(8,128)(2,1)S(1)} all-to-all(bf16[16,16,3072]{2,1,0:T(8,128)(2,1)S(1)} %terms_last.1), channel_id=1, replica_groups=mesh['x'=4,'yl'=2,'c'=2,'yh'=2,'z'=4] {'x','yl','c'}, dimensions={0} | all-to-all | bytes 3145728 | tf_op jit(solution)/shard_map/all_to_all | solution.py:146
  126.3 0.2 bitcast_reduce_fusion
  126.5 1.3 broadcast_in_dim.8
  127.8 0.0 copy-start.3
  127.8 0.0 copy-start.2
  127.8 7.8 %all-to-all-start.5 = ((bf16[8,32,3072]{2,1,0:T(8,128)(2,1)}), bf16[8,32,3072]{2,1,0:T(8,128)(2,1)S(1)}, u32[]{:S(2)}, u32[]{:S(2)}) async-start(bf16[8,32,3072]{2,1,0:T(8,128)(2,1)} %broadcast_in_dim.8), calls=%async_computation.5 | async-start | bytes 3145728 | tf_op jit(solution)/shard_map/all_to_all | solution.py:148
  135.6 0.0 copy-done.3
  135.6 0.1 dynamic_slice.3
  135.7 0.0 copy-done.2
  135.7 0.1 broadcast_subtract_fusion
  135.8 20.1 %all-to-all-done.5 = bf16[8,32,3072]{2,1,0:T(8,128)(2,1)S(1)} async-done(((bf16[8,32,3072]{2,1,0:T(8,128)(2,1)}), bf16[8,32,3072]{2,1,0:T(8,128)(2,1)S(1)}, u32[]{:S(2)}, u32[]{:S(2)}) %all-to-all-start.5) | async-done | bytes 1572896 | tf_op jit(solution)/shard_map/all_to_all | solution.py:148
  155.8 0.2 convert_reduce_fusion
  156.1 0.8 multiply_subtract_fusion
  (1 shorter events, 0.0 us)
Async XLA Ops:
  19.6 28.0 %copy-start.1 = (bf16[32,3072]{1,0:T(8,128)(2,1)S(1)}, bf16[32,3072]{1,0:T(8,128)(2,1)}, u32[]{:S(2)}) copy-start(bf16[32,3072]{1,0:T(8,128)(2,1)} %param.5) | copy-start | bytes 589828
  48.9 25.7 %all-to-all-start = ((bf16[16,16,3072]{2,1,0:T(8,128)(2,1)}), bf16[16,16,3072]{2,1,0:T(8,128)(2,1)S(1)}, u32[]{:S(2)}, u32[]{:S(2)}) async-start(bf16[16,16,3072]{2,1,0:T(8,128)(2,1)} %bitcast.9), calls=%async_computation | async-start | bytes 3145728 | tf_op jit(solution)/shard_map/all_to_all | solution.py:142
  52.6 2.7 %collective-permute-start.2 = (bf16[8,16,3072]{2,1,0:T(8,128)(2,1)}, bf16[8,16,3072]{2,1,0:T(8,128)(2,1)}, u32[]{:S(2)}, u32[]{:S(2)}) collective-permute-start(bf16[8,16,3072]{2,1,0:T(8,128)(2,1)} %all_to_all.30.refs_2_), channel_id=1, source_target_pairs={{0,8},{8,0},{1,9},{9,1},{2,10},{10,2},{3,11},{11,3},{4,12},{12,4},... | collective-permute-start | bytes 2359304 | tf_op jit(solution)/shard_map/ppermute | solution.py:139
  52.9 31.1 %collective-permute-start.1 = (bf16[8,16,3072]{2,1,0:T(8,128)(2,1)S(1)}, bf16[8,16,3072]{2,1,0:T(8,128)(2,1)}, u32[]{:S(2)}, u32[]{:S(2)}) collective-permute-start(bf16[8,16,3072]{2,1,0:T(8,128)(2,1)S(1)} %all_to_all.31.refs_2_), channel_id=1, source_target_pairs={{0,8},{8,0},{1,9},{9,1},{2,10},{10,2},{3,11},{11,3},{4,12},{12,4},... | collective-permute-start | bytes 2359304 | tf_op jit(solution)/shard_map/ppermute | solution.py:139
  53.2 39.0 %collective-permute-start = (bf16[8,16,3072]{2,1,0:T(8,128)(2,1)S(1)}, bf16[8,16,3072]{2,1,0:T(8,128)(2,1)}, u32[]{:S(2)}, u32[]{:S(2)}) collective-permute-start(bf16[8,16,3072]{2,1,0:T(8,128)(2,1)S(1)} %all_to_all.32.refs_2_), channel_id=1, source_target_pairs={{0,8},{8,0},{1,9},{9,1},{2,10},{10,2},{3,11},{11,3},{4,12},{12,4},... | collective-permute-start | bytes 2359304 | tf_op jit(solution)/shard_map/ppermute | solution.py:139
  74.7 1.1 copy-start
  127.8 7.8 %copy-start.3 = (f32[64]{0:T(128)S(1)}, f32[64]{0:T(128)}, u32[]{:S(2)}) copy-start(f32[64]{0:T(128)} %param.6) | copy-start | bytes 772
  127.8 7.9 %copy-start.2 = (f32[768]{0:T(1024)S(1)}, f32[768]{0:T(1024)}, u32[]{:S(2)}) copy-start(f32[768]{0:T(1024)} %param.7) | copy-start | bytes 9220
  127.8 28.0 %all-to-all-start.5 = ((bf16[8,32,3072]{2,1,0:T(8,128)(2,1)}), bf16[8,32,3072]{2,1,0:T(8,128)(2,1)S(1)}, u32[]{:S(2)}, u32[]{:S(2)}) async-start(bf16[8,32,3072]{2,1,0:T(8,128)(2,1)} %broadcast_in_dim.8), calls=%async_computation.5 | async-start | bytes 3145728 | tf_op jit(solution)/shard_map/all_to_all | solution.py:148

commit v2 on v1

--- a/solution.py
+++ b/solution.py
@@ -13,6 +13,7 @@
 HALF = 16
 CHUNKS = 3
 ROWS = NOCC * HALF
+PIECE = NVIR // 2
 
 F32 = jnp.float32
 BF16 = jnp.bfloat16
@@ -35,23 +36,21 @@
 
 
 def chunk_kernel(first, last, *refs):
-    if first:
-        core, xg, b_own, b_other, out, x2, b2, d, c_buf, fit, sems = refs
-        acc = out
-    elif last:
-        core, xg, b_own, b_other, acc, out, x2, b2, d, c_buf, fit, sems = refs
-    else:
-        core, xg, b_own, b_other, acc, out, x2, b2, d, c_buf, fit, sems = refs
-    c = core[0]
+    where, xq, b_own, b_other = refs[0], refs[1:5], refs[5], refs[6]
+    acc = None if first else refs[7]
+    out, x2, b2, d, c_buf, fit, sems = refs[-7:]
+    c, z = where[0], where[1]
     copies = []
     for rel in range(2):
         src_b = b_own if rel == 0 else b_other
         for chip in range(NCHIP):
+            w = chip * 2 + (c ^ rel)
             for q in range(OCC_DEV):
-                row = ((rel * NCHIP + chip) * OCC_DEV + q) * 16
+                base = (rel * NCHIP + chip) * OCC_DEV
+                row = (base + q) * 16
                 copies.append(pltpu.make_async_copy(src_b.at[chip, :, pl.ds(q * NVIR, NVIR)], b2.at[pl.ds(row, 16), :], sems.at[0]))
-                w = chip * 2 + (c ^ rel)
-                copies.append(pltpu.make_async_copy(xg.at[w, :, pl.ds(q * NVIR, NVIR)], x2.at[pl.ds(row, 16), :], sems.at[0]))
+                row = pl.multiple_of((base + ((z - q) & 3)) * 16, 16)
+                copies.append(pltpu.make_async_copy(xq[q].at[w], x2.at[pl.ds(row, 16), :], sems.at[0]))
     for cp in copies:
         cp.start()
     for cp in copies:
@@ -97,16 +96,17 @@
                 i = rb * 16 + k
                 rel, chip, q = i // 32, (i // 4) % 8, i % 4
                 w = chip * 2 + (c ^ rel)
-                out[w, :, q * NVIR : (q + 1) * NVIR] = term[k * 16 : (k + 1) * 16, :].astype(BF16)
+                for h in range(2):
+                    out[h * OCC_DEV + q, w] = term[k * 16 : (k + 1) * 16, h * PIECE : (h + 1) * PIECE].astype(BF16)
 
 
-def chunk(core, xg, b_own, b_other, acc, last):
+def chunk(where, xq, b_own, b_other, acc, last):
     first = acc is None
     hbm = pl.BlockSpec(memory_space=pl.ANY)
     vmem = pl.BlockSpec(memory_space=pltpu.VMEM)
-    args = [core, xg, b_own, b_other] + ([] if first else [acc])
-    specs = [pl.BlockSpec(memory_space=pltpu.SMEM), hbm, hbm, hbm] + ([] if first else [vmem])
-    out = jax.ShapeDtypeStruct((16, HALF, OCC_DEV * NVIR), BF16) if last else jax.ShapeDtypeStruct((ROWS, NVIR), F32)
+    args = [where, *xq, b_own, b_other] + ([] if first else [acc])
+    specs = [pl.BlockSpec(memory_space=pltpu.SMEM)] + [hbm] * 6 + ([] if first else [vmem])
+    out = jax.ShapeDtypeStruct((8, 16, HALF, PIECE), BF16) if last else jax.ShapeDtypeStruct((ROWS, NVIR), F32)
     flops = 2 * 2 * ROWS * ROWS * NVIR
     return pl.pallas_call(
         lambda *refs: chunk_kernel(first, last, *refs),
@@ -122,7 +122,7 @@
             pltpu.SemaphoreType.DMA((1,)),
         ],
         cost_estimate=pl.CostEstimate(flops=flops, bytes_accessed=4 * ROWS * NVIR * 2, transcendentals=0),
-        compiler_params=pltpu.CompilerParams(vmem_limit_bytes=40 << 20),
+        compiler_params=pltpu.CompilerParams(vmem_limit_bytes=24 << 20),
         name="terms_last" if last else "terms_first" if first else "terms_mid",
     )(*args)
 
@@ -132,28 +132,36 @@
 NARROW = ("yh", "z")
 
 
-def local(fit_rows, trials, occ_energy, vir_energy):
-    core = lax.axis_index("c").astype(jnp.int32).reshape(1)
+def body(fit_rows, trials, occ_energy, vir_energy):
+    core = lax.axis_index("c").astype(jnp.int32)
+    z = lax.axis_index("z").astype(jnp.int32)
+    where = jnp.stack([core, z])
+    mine = lax.dynamic_slice_in_dim(trials, z * NVIR, NVIR, 1).reshape(1, 2, HALF, NVIR)
+    send = jnp.broadcast_to(mine, (NCHIP, 2, HALF, NVIR)).reshape(16, HALF, NVIR)
+    xq = [lax.all_to_all(send, WIDE, 0, 0, tiled=True)]
+    for s in (1, 2, 3):
+        xq.append(lax.ppermute(xq[0], "z", [(i, (i + s) % 4) for i in range(4)]))
     blocks = fit_rows.reshape(CHUNKS, NCHIP, HALF, OCC_DEV * NVIR)
-    own = [lax.all_to_all(blocks[t], CHIPS, 0, 0, tiled=True) for t in range(CHUNKS)]
-    other = [lax.ppermute(own[t], "c", [(0, 1), (1, 0)]) for t in range(CHUNKS)]
-    halves = trials.reshape(1, 2, HALF, OCC_DEV * NVIR)
-    send = jnp.broadcast_to(halves, (NCHIP, 2, HALF, OCC_DEV * NVIR)).reshape(16, HALF, OCC_DEV * NVIR)
-    xg = lax.all_to_all(send, WIDE, 0, 0, tiled=True)
+    own, other = [], []
+    for t in range(CHUNKS):
+        own.append(lax.all_to_all(blocks[t], CHIPS, 0, 0, tiled=True))
+        other.append(lax.ppermute(own[t], "c", [(0, 1), (1, 0)]))
     acc = None
     for t in range(CHUNKS):
-        acc = chunk(core, xg, own[t], other[t], acc, t == CHUNKS - 1)
-    parts = lax.all_to_all(acc, WIDE, 0, 0, tiled=True)
-    part = jnp.sum(parts.reshape(NCHIP, 2 * HALF, OCC_DEV * NVIR).astype(F32), 0).astype(BF16)
-    every = lax.all_to_all(jnp.broadcast_to(part[None], (8, NVEC, OCC_DEV * NVIR)), NARROW, 0, 0, tiled=True)
-    total = jnp.sum(every.astype(F32), 0)
+        acc = chunk(where, xq, own[t], other[t], acc, t == CHUNKS - 1)
+    parts = lax.all_to_all(acc, NARROW, 0, 0, tiled=True)
+    part = jnp.sum(parts.astype(F32), 0).astype(BF16)
+    parts = lax.all_to_all(part, WIDE, 0, 0, tiled=True)
+    part = jnp.sum(parts.reshape(NCHIP, NVEC, PIECE).astype(F32), 0).astype(BF16)
+    every = lax.all_to_all(jnp.broadcast_to(part[None], (8, NVEC, PIECE)), NARROW, 0, 0, tiled=True)
+    total = every.reshape(2, OCC_DEV, NVEC, PIECE).transpose(2, 1, 0, 3).reshape(NVEC, OCC_DEV * NVIR)
     w = lax.axis_index(WIDE)
     occ = lax.dynamic_slice_in_dim(occ_energy, w * OCC_DEV, OCC_DEV)
     delta = (vir_energy[None, :] - occ[:, None]).reshape(OCC_DEV * NVIR)
-    return delta[None, :] * trials.astype(F32) - total
+    return delta[None, :] * trials.astype(F32) - total.astype(F32)
 
 
 def solution(mesh):
     fine = Mesh(mesh.devices.reshape(4, 2, 2, 2, 4), ("x", "yl", "c", "yh", "z"))
     in_specs = (P(NARROW, WIDE), P(None, WIDE), P(), P())
-    return jax.shard_map(local, mesh=fine, in_specs=in_specs, out_specs=P(None, WIDE), check_vma=False)
+    return jax.shard_map(body, mesh=fine, in_specs=in_specs, out_specs=P(None, WIDE), check_vma=False)

time: 158 us -> 157 us (level)
  blocking collectives: 71.6 us -> 58.9 us
  starting transfers between devices: 12.3 us -> 24.4 us
  waiting for transfers between devices: 41.3 us -> 38.5 us
    all_to_all x2 -> x4, waiting for transfers between devices: 39.4 us -> 25.8 us  [the longest x1 8.47 us: body(): lax.all_to_all(jnp.broadcast_to(part[None], (8, NVEC, PIECE)), NARROW, 0,...]
    all_to_all x4 -> x3, blocking collectives: 71.6 us -> 58.9 us  [the longest x2 30.3 us: body(): own.append(lax.all_to_all(blocks[t], CHIPS, 0, 0, tiled=True))]
    ppermute x3 -> x6, waiting for transfers between devices: 1.91 us -> 12.7 us  [the longest x3 12.7 us: body(): xq.append(lax.ppermute(xq[0], 'z', [(i, (i + s) % 4) for i in range(4)]))]
    all_to_all x2 -> x4, starting transfers between devices: 11.5 us -> 17.6 us  [the longest x1 5.53 us: body(): xq = [lax.all_to_all(send, WIDE, 0, 0, tiled=True)]]
    ppermute x3 -> x6, starting transfers between devices: 0.8 us -> 6.81 us  [the longest x3 6.58 us: body(): xq.append(lax.ppermute(xq[0], 'z', [(i, (i + s) % 4) for i in range(4)]))]
  transfers between devices with their start and end apart: 5 -> 10, of which waited for: 3 -> 6; matrix products, arithmetic and copies ran while one was open for 0% -> 2% of each run, Pallas kernels for 10% -> 11%
where the time goes in v2:
time: 157 us; the launch traced here: 156 us
  blocking collectives  58.9 us (38%)
  waiting for transfers between devices  38.5 us (25%)
  Pallas kernels  26.2 us (17%)
  starting transfers between devices  24.4 us (16%)
  local copies, waits for them, and re-layouts  5.7 us (4%)
  other arithmetic  1.92 us (1%)
    all_to_all x2, blocking collectives, body(): own.append(lax.all_to_all(blocks[t], CHIPS, 0, 0, tiled=True))  30.3 us
    all_to_all x1, blocking collectives, body(): parts = lax.all_to_all(acc, NARROW, 0, 0, tiled=True)  28.6 us
    pallas_call x3, Pallas kernels, chunk(): pl.pallas_call(lambda *refs: chunk_kernel(first, last, *refs), out_shape=...  26.2 us
    ppermute x3, waiting for transfers between devices, body(): xq.append(lax.ppermute(xq[0], 'z', [(i, (i + s) % 4) for i in range(4)]))  12.7 us
    all_to_all x1, waiting for transfers between devices, body(): lax.all_to_all(jnp.broadcast_to(part[None], (8, NVEC, PIECE)), NARROW, 0,...  8.47 us
    all_to_all x1, waiting for transfers between devices, body(): parts = lax.all_to_all(part, WIDE, 0, 0, tiled=True)  6.95 us
    ppermute x3, starting transfers between devices, body(): xq.append(lax.ppermute(xq[0], 'z', [(i, (i + s) % 4) for i in range(4)]))  6.58 us
    all_to_all x1, waiting for transfers between devices, body(): xq = [lax.all_to_all(send, WIDE, 0, 0, tiled=True)]  6.38 us
  transfers between devices with their start and end apart: 10, of which 6 were waited for; matrix products, arithmetic and copies ran while one was open for 2% of the time, Pallas kernels for 11%

profile of v2, /device:TPU:0, one launch (start us, length us, event | category | flops | bytes accessed | tf_op | source)
XLA Modules:
  0.0 155.9 jit_solution(8756095621990284622)
XLA Ops:
  0.0 0.8 constant_dynamic-slice_fusion
  0.8 0.8 broadcast_in_dim.7
  1.6 5.5 %all-to-all-start = ((bf16[16,16,768]{2,1,0:T(8,128)(2,1)}), bf16[16,16,768]{2,1,0:T(8,128)(2,1)S(1)}, u32[]{:S(2)}, u32[]{:S(2)}) async-start(bf16[16,16,768]{2,1,0:T(8,128)(2,1)} %bitcast.3), calls=%async_computation | async-start | bytes 786432 | tf_op jit(solution)/shard_map/all_to_all | solution.py:141
  7.1 2.7 %fusion = (bf16[128,3072]{1,0:T(8,128)(2,1)S(1)}, bf16[128,3072]{1,0:T(8,128)(2,1)}, bf16[128,3072]{1,0:T(8,128)(2,1)S(1)}) fusion(bf16[384,3072]{1,0:T(8,128)(2,1)} %param.4), kind=kLoop, calls=%fused_computation.6 | loop fusion | bytes 4718592 | tf_op jit(solution)/shard_map/slice | solution.py:147
  9.8 6.4 %all-to-all-done.refs_1_ = bf16[16,16,768]{2,1,0:T(8,128)(2,1)S(1)} async-done(((bf16[16,16,768]{2,1,0:T(8,128)(2,1)}), bf16[16,16,768]{2,1,0:T(8,128)(2,1)S(1)}, u32[]{:S(2)}, u32[]{:S(2)}) %all-to-all-start) | async-done | bytes 393248 | tf_op jit(solution)/shard_map/all_to_all | solution.py:141
  16.2 15.4 %all_to_all.35.refs_5_ = bf16[8,16,3072]{2,1,0:T(8,128)(2,1)S(1)} all-to-all(bf16[8,16,3072]{2,1,0:T(8,128)(2,1)S(1)} %bitcast.15), channel_id=1, replica_groups=mesh['x'=4,'yl'=2,'c'=2,'yh'=2,'z'=4] {'x','yl'}, dimensions={0} | all-to-all | bytes 1572864 | tf_op jit(solution)/shard_map/all_to_all | solution.py:147
  31.6 14.9 %all_to_all.36.refs_5_ = bf16[8,16,3072]{2,1,0:T(8,128)(2,1)S(1)} all-to-all(bf16[8,16,3072]{2,1,0:T(8,128)(2,1)S(1)} %bitcast.14), channel_id=1, replica_groups=mesh['x'=4,'yl'=2,'c'=2,'yh'=2,'z'=4] {'x','yl'}, dimensions={0} | all-to-all | bytes 1572864 | tf_op jit(solution)/shard_map/all_to_all | solution.py:147
  46.5 3.5 %all-to-all-start.1 = ((bf16[8,16,3072]{2,1,0:T(8,128)(2,1)}), bf16[8,16,3072]{2,1,0:T(8,128)(2,1)S(1)}, u32[]{:S(2)}, u32[]{:S(2)}) async-start(bf16[8,16,3072]{2,1,0:T(8,128)(2,1)} %bitcast.4), calls=%async_computation.1 | async-start | bytes 1572864 | tf_op jit(solution)/shard_map/all_to_all | solution.py:147
  50.1 0.1 collective-permute-start.5
  50.1 2.0 %collective-permute-start = (bf16[16,16,768]{2,1,0:T(8,128)(2,1)S(1)}, bf16[16,16,768]{2,1,0:T(8,128)(2,1)}, u32[]{:S(2)}, u32[]{:S(2)}) collective-permute-start(bf16[16,16,768]{2,1,0:T(8,128)(2,1)S(1)} %all-to-all-done.refs_1_), channel_id=1, source_target_pairs={{0,1},{1,2},{2,3},{3,0},{4,5},{5,6},{6,7},{7,4},{8,9},{9,10},{10,1... | collective-permute-start | bytes 1179656 | tf_op jit(solution)/shard_map/ppermute | solution.py:143
  52.1 0.1 collective-permute-start.4
  52.3 3.6 %collective-permute-start.1 = (bf16[16,16,768]{2,1,0:T(8,128)(2,1)S(1)}, bf16[16,16,768]{2,1,0:T(8,128)(2,1)}, u32[]{:S(2)}, u32[]{:S(2)}) collective-permute-start(bf16[16,16,768]{2,1,0:T(8,128)(2,1)S(1)} %all-to-all-done.refs_1_), channel_id=1, source_target_pairs={{0,2},{1,3},{2,0},{3,1},{4,6},{5,7},{6,4},{7,5},{8,10},{9,11},{10,... | collective-permute-start | bytes 1179656 | tf_op jit(solution)/shard_map/ppermute | solution.py:143
  55.9 1.0 collective-permute-start.2
  56.9 4.0 %all-to-all-done.1.refs_5_ = bf16[8,16,3072]{2,1,0:T(8,128)(2,1)S(1)} async-done(((bf16[8,16,3072]{2,1,0:T(8,128)(2,1)}), bf16[8,16,3072]{2,1,0:T(8,128)(2,1)S(1)}, u32[]{:S(2)}, u32[]{:S(2)}) %all-to-all-start.1) | async-done | bytes 786464 | tf_op jit(solution)/shard_map/all_to_all | solution.py:147
  60.9 3.2 %collective-permute-done.refs_2_ = bf16[16,16,768]{2,1,0:T(8,128)(2,1)} collective-permute-done((bf16[16,16,768]{2,1,0:T(8,128)(2,1)S(1)}, bf16[16,16,768]{2,1,0:T(8,128)(2,1)}, u32[]{:S(2)}, u32[]{:S(2)}) %collective-permute-start) | collective-permute-done | bytes 393248 | tf_op jit(solution)/shard_map/ppermute | solution.py:143
  64.1 0.0 collective-permute-start.3
  64.1 0.1 pad_add_fusion.refs_0_
  64.1 9.5 %collective-permute-done.1.refs_3_ = bf16[16,16,768]{2,1,0:T(8,128)(2,1)} collective-permute-done((bf16[16,16,768]{2,1,0:T(8,128)(2,1)S(1)}, bf16[16,16,768]{2,1,0:T(8,128)(2,1)}, u32[]{:S(2)}, u32[]{:S(2)}) %collective-permute-start.1) | collective-permute-done | bytes 393248 | tf_op jit(solution)/shard_map/ppermute | solution.py:143
  73.7 0.0 collective-permute-done.2.refs_4_
  73.7 0.0 collective-permute-done.5.refs_6_
  73.7 8.9 %terms_first.1.refs_7_ = f32[1024,768]{1,0:T(8,128)S(1)} custom-call(s32[2]{0:T(128)S(1)} %pad_add_fusion.refs_0_, bf16[16,16,768]{2,1,0:T(8,128)(2,1)S(1)} %all-to-all-done.refs_1_, bf16[16,16,768]{2,1,0:T(8,128)(2,1)} %collective-permute-done.refs_2_, bf16[16,16,768]{2,1,0:T(8,128)(2,1)} %collective-permute-done.1.refs_3_, ...), custom_call_target="tpu_custom_call" | custom-call | flops 3221225472 | bytes 6291456 | tf_op jit(solution)/shard_map/terms_first/pallas_call | solution.py:111
  82.5 0.0 collective-permute-done.4.refs_6_
  82.5 8.7 %terms_mid.1.refs_7_ = f32[1024,768]{1,0:T(8,128)S(1)} custom-call(s32[2]{0:T(128)S(1)} %pad_add_fusion.refs_0_, bf16[16,16,768]{2,1,0:T(8,128)(2,1)S(1)} %all-to-all-done.refs_1_, bf16[16,16,768]{2,1,0:T(8,128)(2,1)} %collective-permute-done.refs_2_, bf16[16,16,768]{2,1,0:T(8,128)(2,1)} %collective-permute-done.1.refs_3_, ...), custom_call_target="tpu_custom_call" | custom-call | flops 3221225472 | bytes 6291456 | tf_op jit(solution)/shard_map/terms_mid/pallas_call | solution.py:111
  91.2 0.0 collective-permute-done.3.refs_6_
  91.2 8.7 %terms_last.1 = bf16[8,16,16,384]{3,2,1,0:T(8,128)(2,1)S(1)} custom-call(s32[2]{0:T(128)S(1)} %pad_add_fusion.refs_0_, bf16[16,16,768]{2,1,0:T(8,128)(2,1)S(1)} %all-to-all-done.refs_1_, bf16[16,16,768]{2,1,0:T(8,128)(2,1)} %collective-permute-done.refs_2_, bf16[16,16,768]{2,1,0:T(8,128)(2,1)} %collective-permute-done.1.refs_3_, ...), custom_call_target="tpu_custom_call" | custom-call | flops 3221225472 | bytes 6291456 | tf_op jit(solution)/shard_map/terms_last/pallas_call | solution.py:111
  100.0 0.0 copy-start.2
  100.0 0.0 copy-start.1
  100.0 28.6 %all_to_all.37 = bf16[8,16,16,384]{3,2,1,0:T(8,128)(2,1)S(1)} all-to-all(bf16[8,16,16,384]{3,2,1,0:T(8,128)(2,1)S(1)} %terms_last.1), channel_id=1, replica_groups=mesh['x'=4,'yl'=2,'c'=2,'yh'=2,'z'=4] {'yh','z'}, dimensions={0} | all-to-all | bytes 3145728 | tf_op jit(solution)/shard_map/all_to_all | solution.py:152
  128.6 0.0 copy-start
  128.6 0.9 reduce_sum.24
  129.5 5.1 %all-to-all-start.5 = ((bf16[16,16,384]{2,1,0:T(8,128)(2,1)}), bf16[16,16,384]{2,1,0:T(8,128)(2,1)S(1)}, u32[]{:S(2)}, u32[]{:S(2)}) async-start(bf16[16,16,384]{2,1,0:T(8,128)(2,1)} %reduce_sum.24), calls=%async_computation.5 | async-start | bytes 393216 | tf_op jit(solution)/shard_map/all_to_all | solution.py:154
  134.7 0.0 copy-done.2
  134.7 0.1 dynamic_slice.6
  134.8 7.0 %all-to-all-done.5 = bf16[16,16,384]{2,1,0:T(8,128)(2,1)S(1)} async-done(((bf16[16,16,384]{2,1,0:T(8,128)(2,1)}), bf16[16,16,384]{2,1,0:T(8,128)(2,1)S(1)}, u32[]{:S(2)}, u32[]{:S(2)}) %all-to-all-start.5) | async-done | bytes 196640 | tf_op jit(solution)/shard_map/all_to_all | solution.py:154
  141.7 0.7 broadcast_in_dim.8
  142.4 3.4 %all-to-all-start.6 = ((bf16[8,32,384]{2,1,0:T(8,128)(2,1)}), bf16[8,32,384]{2,1,0:T(8,128)(2,1)S(1)}, u32[]{:S(2)}, u32[]{:S(2)}) async-start(bf16[8,32,384]{2,1,0:T(8,128)(2,1)} %broadcast_in_dim.8), calls=%async_computation.6 | async-start | bytes 393216 | tf_op jit(solution)/shard_map/all_to_all | solution.py:156
  145.8 0.0 copy-done.1
  145.8 0.1 broadcast_subtract_fusion
  145.9 8.5 %all-to-all-done.6 = bf16[8,32,384]{2,1,0:T(8,128)(2,1)S(1)} async-done(((bf16[8,32,384]{2,1,0:T(8,128)(2,1)}), bf16[8,32,384]{2,1,0:T(8,128)(2,1)S(1)}, u32[]{:S(2)}, u32[]{:S(2)}) %all-to-all-start.6) | async-done | bytes 196640 | tf_op jit(solution)/shard_map/all_to_all | solution.py:156
  154.4 0.3 copy.6
  154.7 0.3 reshape.40
  155.1 0.0 copy-done
  155.1 0.8 multiply_subtract_fusion
  (3 shorter events, 0.1 us)
Async XLA Ops:
  1.6 14.6 %all-to-all-start = ((bf16[16,16,768]{2,1,0:T(8,128)(2,1)}), bf16[16,16,768]{2,1,0:T(8,128)(2,1)S(1)}, u32[]{:S(2)}, u32[]{:S(2)}) async-start(bf16[16,16,768]{2,1,0:T(8,128)(2,1)} %bitcast.3), calls=%async_computation | async-start | bytes 786432 | tf_op jit(solution)/shard_map/all_to_all | solution.py:141
  46.5 14.4 %all-to-all-start.1 = ((bf16[8,16,3072]{2,1,0:T(8,128)(2,1)}), bf16[8,16,3072]{2,1,0:T(8,128)(2,1)S(1)}, u32[]{:S(2)}, u32[]{:S(2)}) async-start(bf16[8,16,3072]{2,1,0:T(8,128)(2,1)} %bitcast.4), calls=%async_computation.1 | async-start | bytes 1572864 | tf_op jit(solution)/shard_map/all_to_all | solution.py:147
  50.1 23.6 %collective-permute-start.5 = (bf16[8,16,3072]{2,1,0:T(8,128)(2,1)S(1)}, bf16[8,16,3072]{2,1,0:T(8,128)(2,1)S(1)}, u32[]{:S(2)}, u32[]{:S(2)}) collective-permute-start(bf16[8,16,3072]{2,1,0:T(8,128)(2,1)S(1)} %all_to_all.35.refs_5_), channel_id=1, source_target_pairs={{0,8},{8,0},{1,9},{9,1},{2,10},{10,2},{3,11},{11,3},{4,12},{12,4},... | collective-permute-start | bytes 2359304 | tf_op jit(solution)/shard_map/ppermute | solution.py:148
  50.1 13.9 %collective-permute-start = (bf16[16,16,768]{2,1,0:T(8,128)(2,1)S(1)}, bf16[16,16,768]{2,1,0:T(8,128)(2,1)}, u32[]{:S(2)}, u32[]{:S(2)}) collective-permute-start(bf16[16,16,768]{2,1,0:T(8,128)(2,1)S(1)} %all-to-all-done.refs_1_), channel_id=1, source_target_pairs={{0,1},{1,2},{2,3},{3,0},{4,5},{5,6},{6,7},{7,4},{8,9},{9,10},{10,1... | collective-permute-start | bytes 1179656 | tf_op jit(solution)/shard_map/ppermute | solution.py:143
  52.1 30.4 %collective-permute-start.4 = (bf16[8,16,3072]{2,1,0:T(8,128)(2,1)S(1)}, bf16[8,16,3072]{2,1,0:T(8,128)(2,1)}, u32[]{:S(2)}, u32[]{:S(2)}) collective-permute-start(bf16[8,16,3072]{2,1,0:T(8,128)(2,1)S(1)} %all_to_all.36.refs_5_), channel_id=1, source_target_pairs={{0,8},{8,0},{1,9},{9,1},{2,10},{10,2},{3,11},{11,3},{4,12},{12,4},... | collective-permute-start | bytes 2359304 | tf_op jit(solution)/shard_map/ppermute | solution.py:148
  52.3 21.4 %collective-permute-start.1 = (bf16[16,16,768]{2,1,0:T(8,128)(2,1)S(1)}, bf16[16,16,768]{2,1,0:T(8,128)(2,1)}, u32[]{:S(2)}, u32[]{:S(2)}) collective-permute-start(bf16[16,16,768]{2,1,0:T(8,128)(2,1)S(1)} %all-to-all-done.refs_1_), channel_id=1, source_target_pairs={{0,2},{1,3},{2,0},{3,1},{4,6},{5,7},{6,4},{7,5},{8,10},{9,11},{10,... | collective-permute-start | bytes 1179656 | tf_op jit(solution)/shard_map/ppermute | solution.py:143
  55.9 17.8 %collective-permute-start.2 = (bf16[16,16,768]{2,1,0:T(8,128)(2,1)S(1)}, bf16[16,16,768]{2,1,0:T(8,128)(2,1)}, u32[]{:S(2)}, u32[]{:S(2)}) collective-permute-start(bf16[16,16,768]{2,1,0:T(8,128)(2,1)S(1)} %all-to-all-done.refs_1_), channel_id=1, source_target_pairs={{0,3},{1,0},{2,1},{3,2},{4,7},{5,4},{6,5},{7,6},{8,11},{9,8},{10,9... | collective-permute-start | bytes 1179656 | tf_op jit(solution)/shard_map/ppermute | solution.py:143
  64.1 27.2 %collective-permute-start.3 = (bf16[8,16,3072]{2,1,0:T(8,128)(2,1)S(1)}, bf16[8,16,3072]{2,1,0:T(8,128)(2,1)}, u32[]{:S(2)}, u32[]{:S(2)}) collective-permute-start(bf16[8,16,3072]{2,1,0:T(8,128)(2,1)S(1)} %all-to-all-done.1.refs_5_), channel_id=1, source_target_pairs={{0,8},{8,0},{1,9},{9,1},{2,10},{10,2},{3,11},{11,3},{4,12},{12,4},... | collective-permute-start | bytes 2359304 | tf_op jit(solution)/shard_map/ppermute | solution.py:148
  100.0 34.7 %copy-start.2 = (f32[64]{0:T(128)S(1)}, f32[64]{0:T(128)}, u32[]{:S(2)}) copy-start(f32[64]{0:T(128)} %param.6) | copy-start | bytes 772
  100.0 45.9 %copy-start.1 = (f32[768]{0:T(1024)S(1)}, f32[768]{0:T(1024)}, u32[]{:S(2)}) copy-start(f32[768]{0:T(1024)} %param.7) | copy-start | bytes 9220
  128.6 26.5 %copy-start = (bf16[32,3072]{1,0:T(8,128)(2,1)S(1)}, bf16[32,3072]{1,0:T(8,128)(2,1)}, u32[]{:S(2)}) copy-start(bf16[32,3072]{1,0:T(8,128)(2,1)} %param.5) | copy-start | bytes 589828
  129.5 12.2 %all-to-all-start.5 = ((bf16[16,16,384]{2,1,0:T(8,128)(2,1)}), bf16[16,16,384]{2,1,0:T(8,128)(2,1)S(1)}, u32[]{:S(2)}, u32[]{:S(2)}) async-start(bf16[16,16,384]{2,1,0:T(8,128)(2,1)} %reduce_sum.24), calls=%async_computation.5 | async-start | bytes 393216 | tf_op jit(solution)/shard_map/all_to_all | solution.py:154
  142.4 12.0 %all-to-all-start.6 = ((bf16[8,32,384]{2,1,0:T(8,128)(2,1)}), bf16[8,32,384]{2,1,0:T(8,128)(2,1)S(1)}, u32[]{:S(2)}, u32[]{:S(2)}) async-start(bf16[8,32,384]{2,1,0:T(8,128)(2,1)} %broadcast_in_dim.8), calls=%async_computation.6 | async-start | bytes 393216 | tf_op jit(solution)/shard_map/all_to_all | solution.py:156

commit v3 on v2

v3 whole, which is shorter than its diff:
```python
import jax
import jax.numpy as jnp
from jax import lax
from jax.experimental import pallas as pl
from jax.experimental.pallas import tpu as pltpu
from jax.sharding import Mesh, PartitionSpec as P

NOCC = 64
NVIR = 768
NVEC = 32
NCHIP = 8
OCC_DEV = 4
PAIRS = OCC_DEV * NVIR
HALF = 16
CHUNKS = 3
ROWS = NOCC * HALF

F32 = jnp.float32
BF16 = jnp.bfloat16

CHIPS = ("x", "yl")
WIDE = ("x", "yl", "c")
NARROW = ("yh", "z")
MOST = ("x", "yl", "c", "z")


def swap_blocks(tile):
    v = [tile[j * 16 : (j + 1) * 16] for j in range(8)]
    lane = lax.broadcasted_iota(jnp.int32, (16, 128), 1)
    for s in (4, 2, 1):
        bit = (lane & (16 * s)) != 0
        new = list(v)
        for j in range(8):
            if j & s:
                continue
            lo, hi = v[j], v[j + s]
            new[j] = jnp.where(bit, pltpu.roll(hi, 16 * s, 1), lo)
            new[j + s] = jnp.where(bit, hi, pltpu.roll(lo, 128 - 16 * s, 1))
        v = new
    return jnp.concatenate(v, 0)


def gather_rows(b2, b_own, b_other):
    for rel, src in enumerate((b_own, b_other)):
        for chip in range(NCHIP):
            for q in range(OCC_DEV):
                row = ((rel * NCHIP + chip) * OCC_DEV + q) * 16
                b2[row : row + 16, :] = src[chip, :, q * NVIR : (q + 1) * NVIR]


def contract_first(x2, b2, d):
    row_i = lax.broadcasted_iota(jnp.int32, (128, 128), 0) // 16
    lane_i = lax.broadcasted_iota(jnp.int32, (128, 128), 1) // 16
    diag = row_i == lane_i
    fit = jnp.zeros((128, 128), F32)
    for g in range(4):
        rhs = b2[g * 256 : (g + 1) * 256, :]
        for rb in range(4):
            lhs = x2[rb * 256 : (rb + 1) * 256, :]
            inter = lax.dot_general(lhs, rhs, (((1,), (1,)), ((), ())), preferred_element_type=F32)
            for a in range(2):
                for h in range(2):
                    ig, jg = g * 2 + h, rb * 2 + a
                    tile = inter[a * 128 : (a + 1) * 128, h * 128 : (h + 1) * 128]
                    if ig == jg:
                        fit = fit + jnp.where(diag, tile, 0.0)
                    d[ig * 128 : (ig + 1) * 128, jg * 128 : (jg + 1) * 128] = swap_blocks(tile).astype(BF16)
    total = fit[0:16, :]
    for j in range(1, 8):
        total = total + fit[j * 16 : (j + 1) * 16, :]
    for s in (64, 32, 16):
        total = total + pltpu.roll(total, s, 1)
    fit_b = 2.0 * total.astype(BF16).astype(F32)
    sub = jnp.where(diag, jnp.concatenate([fit_b] * 8, 0), 0.0)
    for g in range(8):
        s = slice(g * 128, (g + 1) * 128)
        d[s, s] = (d[s, s].astype(F32) - sub).astype(BF16)


def early_kernel(where, x_a, x_b, x_c, x_d, own0, other0, own1, other1, out, x_out, x2, b2, d, acc, sems):
    z = where[1]
    for s, ref in enumerate((x_a, x_b, x_c, x_d)):
        q = (z - s) & 3
        for k in range(16):
            row = pl.multiple_of((k * OCC_DEV + q) * 16, 16)
            x2[pl.ds(row, 16), :] = ref[k // NCHIP, k % NCHIP]
    keep_x = pltpu.make_async_copy(x2, x_out, sems.at[0])
    keep_x.start()
    copies = []
    for t, (own, other) in enumerate(((own0, other0), (own1, other1))):
        gather_rows(b2, own, other)
        contract_first(x2, b2, d)
        for rb in range(4):
            rows = slice(rb * 256, (rb + 1) * 256)
            term = jnp.dot(d[rows, :], b2[...], preferred_element_type=F32)
            if t == 0:
                acc[rows, :] = term
            else:
                acc[rows, :] += term
                copies.append(pltpu.make_async_copy(acc.at[rows], out.at[rows], sems.at[1 + rb]))
                copies[-1].start()
    keep_x.wait()
    for cp in copies:
        cp.wait()


def late_kernel(where, x_in, own, other, acc_in, out, x2, b2, d, acc, sems):
    c = where[0]
    get_x = pltpu.make_async_copy(x_in, x2, sems.at[0])
    get_x.start()
    get_acc = pltpu.make_async_copy(acc_in, acc, sems.at[1])
    get_acc.start()
    gather_rows(b2, own, other)
    get_x.wait()
    contract_first(x2, b2, d)
    get_acc.wait()
    for rb in range(4):
        rows = slice(rb * 256, (rb + 1) * 256)
        term = acc[rows, :] + jnp.dot(d[rows, :], b2[...], preferred_element_type=F32)
        for k in range(16):
            i = rb * 16 + k
            rel, chip, q = i // 32, (i // 4) % 8, i % 4
            w = chip * 2 + (c ^ rel)
            out[w * OCC_DEV + q] = term[k * 16 : (k + 1) * 16, :].astype(BF16)


SMEM = pl.BlockSpec(memory_space=pltpu.SMEM)
VMEM = pl.BlockSpec(memory_space=pltpu.VMEM)
HBM = pl.BlockSpec(memory_space=pltpu.HBM)
SCRATCH = [
    pltpu.VMEM((ROWS, NVIR), BF16),
    pltpu.VMEM((ROWS, NVIR), BF16),
    pltpu.VMEM((ROWS, ROWS), BF16),
    pltpu.VMEM((ROWS, NVIR), F32),
    pltpu.SemaphoreType.DMA((5,)),
]


def cost(count):
    return pl.CostEstimate(flops=count * 4 * ROWS * ROWS * NVIR, bytes_accessed=4 * ROWS * NVIR * 2, transcendentals=0)


def early(where, x, own, other):
    return pl.pallas_call(
        early_kernel,
        out_shape=[jax.ShapeDtypeStruct((ROWS, NVIR), F32), jax.ShapeDtypeStruct((ROWS, NVIR), BF16)],
        in_specs=[SMEM] + [VMEM] * 8,
        out_specs=[HBM, HBM],
        scratch_shapes=SCRATCH,
        cost_estimate=cost(2),
        compiler_params=pltpu.CompilerParams(vmem_limit_bytes=32 << 20),
        name="terms_early",
    )(where, *x, own[0], other[0], own[1], other[1])


def late(where, x2, own, other, acc):
    return pl.pallas_call(
        late_kernel,
        out_shape=jax.ShapeDtypeStruct((16 * OCC_DEV, HALF, NVIR), BF16),
        in_specs=[SMEM, HBM, VMEM, VMEM, HBM],
        out_specs=VMEM,
        scratch_shapes=SCRATCH,
        cost_estimate=cost(1),
        compiler_params=pltpu.CompilerParams(vmem_limit_bytes=32 << 20),
        name="terms_late",
    )(where, x2, own[2], other[2], acc)


def ring(n, s):
    return [(i, (i + s) % n) for i in range(n)]


def body(fit_rows, trials, occ_energy, vir_energy):
    core = lax.axis_index("c").astype(jnp.int32)
    z = lax.axis_index("z").astype(jnp.int32)
    where = jnp.stack([core, z])
    blocks = fit_rows.reshape(CHUNKS, NCHIP, HALF, PAIRS)
    mine = lax.dynamic_slice_in_dim(trials, z * NVIR, NVIR, 1)
    mine = jnp.concatenate([mine[:HALF], mine[HALF:]], 1)
    mine = jnp.broadcast_to(mine[None], (NCHIP, HALF, 2 * NVIR))
    own, other = [], []
    for t in range(CHUNKS):
        send = blocks[t]
        if t == 0:
            send = jnp.concatenate([send, mine], 2)
        own.append(lax.all_to_all(send, CHIPS, 0, 0, tiled=True))
        other.append(lax.ppermute(own[t], "c", ring(2, 1)))
    x_own = lax.dynamic_slice_in_dim(own[0], PAIRS + core * NVIR, NVIR, 2)
    x_send = lax.dynamic_slice_in_dim(own[0], PAIRS + (1 - core) * NVIR, NVIR, 2)
    x_other = lax.ppermute(x_send, "c", ring(2, 1))
    x = [jnp.stack([x_own, x_other])]
    x = x + [lax.ppermute(x[0], "z", ring(4, s)) for s in (1, 2, 3)]
    acc, x2 = early(where, x, own, other)
    acc = late(where, x2, own, other, acc)
    parts = lax.all_to_all(acc, MOST, 0, 0, tiled=True)
    part = jnp.sum(parts.reshape(NCHIP, 2, 4, HALF, NVIR).astype(F32), (0, 2)).astype(BF16)
    part = jnp.broadcast_to(part.reshape(1, NVEC, NVIR), (8, NVEC, NVIR))
    every = lax.all_to_all(part, NARROW, 0, 0, tiled=True)
    total = jnp.sum(every.reshape(2, OCC_DEV, NVEC, NVIR).astype(F32), 0)
    total = total.transpose(1, 0, 2).reshape(NVEC, PAIRS)
    w = lax.axis_index(WIDE)
    occ = lax.dynamic_slice_in_dim(occ_energy, w * OCC_DEV, OCC_DEV)
    delta = (vir_energy[None, :] - occ[:, None]).reshape(PAIRS)
    return delta[None, :] * trials.astype(F32) - total


def solution(mesh):
    fine = Mesh(mesh.devices.reshape(4, 2, 2, 2, 4), ("x", "yl", "c", "yh", "z"))
    in_specs = (P(NARROW, WIDE), P(None, WIDE), P(), P())
    return jax.shard_map(body, mesh=fine, in_specs=in_specs, out_specs=P(None, WIDE), check_vma=False)
```

time: 157 us -> 137 us (0.87)
  Pallas kernels: 26.2 us -> 19.3 us
  blocking collectives: 58.9 us -> 53.4 us
  starting transfers between devices: 24.4 us -> 19.1 us
    pallas_call x3 -> x2, Pallas kernels: 26.2 us -> 19.3 us  [the longest x1 14.2 us: early(): pl.pallas_call(early_kernel, out_shape=[jax.ShapeDtypeStruct((ROWS, NVIR)...]
    all_to_all x4 -> x3, starting transfers between devices: 17.6 us -> 11.9 us  [the longest x2 7.09 us: body(): own.append(lax.all_to_all(send, CHIPS, 0, 0, tiled=True))]
    all_to_all x3 -> x2, blocking collectives: 58.9 us -> 53.4 us  [the longest x1 31.1 us: body(): parts = lax.all_to_all(acc, MOST, 0, 0, tiled=True)]
    slice x1 -> x2, local copies, waits for them, and re-layouts: 2.7 us -> 3.69 us  [the longest x1 2.93 us: body(): send = blocks[t]]
    ppermute x6 -> x7, waiting for transfers between devices: 12.7 us -> 12.1 us  [the longest x3 11 us: body(): x = x + [lax.ppermute(x[0], 'z', ring(4, s)) for s in (1, 2, 3)]]
    all_to_all x4 -> x3, waiting for transfers between devices: 25.8 us -> 26.3 us  [the longest x2 16.7 us: body(): own.append(lax.all_to_all(send, CHIPS, 0, 0, tiled=True))]
    ppermute x6 -> x7, starting transfers between devices: 6.81 us -> 7.25 us  [the longest x3 6.58 us: body(): x = x + [lax.ppermute(x[0], 'z', ring(4, s)) for s in (1, 2, 3)]]
  transfers between devices with their start and end apart: 10 -> 10, of which waited for: 6 -> 6; matrix products, arithmetic and copies ran while one was open for 2% -> 0% of each run, Pallas kernels for 11% -> 10%
where the time goes in v3:
time: 137 us; the launch traced here: 136 us
  blocking collectives  53.4 us (39%)
  waiting for transfers between devices  38.5 us (28%)
  Pallas kernels  19.3 us (14%)
  starting transfers between devices  19.1 us (14%)
  local copies, waits for them, and re-layouts  4.65 us (3%)
    all_to_all x1, blocking collectives, body(): parts = lax.all_to_all(acc, MOST, 0, 0, tiled=True)  31.1 us
    all_to_all x1, blocking collectives, body(): own.append(lax.all_to_all(send, CHIPS, 0, 0, tiled=True))  22.2 us
    all_to_all x2, waiting for transfers between devices, body(): own.append(lax.all_to_all(send, CHIPS, 0, 0, tiled=True))  16.7 us
    pallas_call x1, Pallas kernels, early(): pl.pallas_call(early_kernel, out_shape=[jax.ShapeDtypeStruct((ROWS, NVIR)...  14.2 us
    ppermute x3, waiting for transfers between devices, body(): x = x + [lax.ppermute(x[0], 'z', ring(4, s)) for s in (1, 2, 3)]  11 us
    all_to_all x1, waiting for transfers between devices, body(): every = lax.all_to_all(part, NARROW, 0, 0, tiled=True)  9.6 us
    all_to_all x2, starting transfers between devices, body(): own.append(lax.all_to_all(send, CHIPS, 0, 0, tiled=True))  7.09 us
    ppermute x3, starting transfers between devices, body(): x = x + [lax.ppermute(x[0], 'z', ring(4, s)) for s in (1, 2, 3)]  6.58 us
  transfers between devices with their start and end apart: 10, of which 6 were waited for; matrix products, arithmetic and copies ran while one was open for 0% of the time, Pallas kernels for 10%

profile of v3, /device:TPU:0, one launch (start us, length us, event | category | flops | bytes accessed | tf_op | source)
XLA Modules:
  0.0 136.4 jit_solution(2087591255161582484)
XLA Ops:
  0.0 2.9 %fusion = (bf16[128,3072]{1,0:T(8,128)(2,1)}, bf16[128,3072]{1,0:T(8,128)(2,1)S(1)}, bf16[128,3072]{1,0:T(8,128)(2,1)}) fusion(bf16[384,3072]{1,0:T(8,128)(2,1)} %param.4), kind=kLoop, calls=%fused_computation.10 | loop fusion | bytes 4718592 | tf_op jit(solution)/shard_map/slice | solution.py:183
  2.9 0.8 constant_dynamic-slice_fusion
  3.7 0.1 pad_maximum_fusion
  3.8 22.2 %all_to_all.25.own0 = bf16[8,16,4608]{2,1,0:T(8,128)(2,1)S(1)} all-to-all(bf16[8,16,4608]{2,1,0:T(8,128)(2,1)S(1)} %pad_maximum_fusion), channel_id=1, replica_groups=mesh['x'=4,'yl'=2,'c'=2,'yh'=2,'z'=4] {'x','yl'}, dimensions={0} | all-to-all | bytes 2359296 | tf_op jit(solution)/shard_map/all_to_all | solution.py:186
  26.1 3.5 %all-to-all-start.1 = ((bf16[8,16,3072]{2,1,0:T(8,128)(2,1)}), bf16[8,16,3072]{2,1,0:T(8,128)(2,1)S(1)}, u32[]{:S(2)}, u32[]{:S(2)}) async-start(bf16[8,16,3072]{2,1,0:T(8,128)(2,1)} %bitcast.5), calls=%async_computation.1 | async-start | bytes 1572864 | tf_op jit(solution)/shard_map/all_to_all | solution.py:186
  29.6 0.1 collective-permute-start.4
  29.7 11.0 %all-to-all-done.1.own1 = bf16[8,16,3072]{2,1,0:T(8,128)(2,1)S(1)} async-done(((bf16[8,16,3072]{2,1,0:T(8,128)(2,1)}), bf16[8,16,3072]{2,1,0:T(8,128)(2,1)S(1)}, u32[]{:S(2)}, u32[]{:S(2)}) %all-to-all-start.1) | async-done | bytes 786464 | tf_op jit(solution)/shard_map/all_to_all | solution.py:186
  40.7 0.0 collective-permute-start.5
  40.7 3.5 %all-to-all-start.2 = ((bf16[8,16,3072]{2,1,0:T(8,128)(2,1)}), bf16[8,16,3072]{2,1,0:T(8,128)(2,1)S(1)}, u32[]{:S(2)}, u32[]{:S(2)}) async-start(bf16[8,16,3072]{2,1,0:T(8,128)(2,1)} %bitcast.6), calls=%async_computation.2 | async-start | bytes 1572864 | tf_op jit(solution)/shard_map/all_to_all | solution.py:186
  44.3 0.6 collective-permute-start
  44.9 1.1 collective-permute-done
  46.0 2.0 %collective-permute-start.1 = (bf16[2,8,16,768]{3,2,1,0:T(8,128)(2,1)S(1)}, bf16[2,8,16,768]{3,2,1,0:T(8,128)(2,1)S(1)}, u32[]{:S(2)}, u32[]{:S(2)}) collective-permute-start(bf16[2,8,16,768]{3,2,1,0:T(8,128)(2,1)S(1)} %pad_maximum_fusion.1.x_a), channel_id=1, source_target_pairs={{0,1},{1,2},{2,3},{3,0},{4,5},{5,6},{6,7},{7,4},{8,9},{9,10},{10,1... | collective-permute-start | bytes 1179656 | tf_op jit(solution)/shard_map/ppermute | solution.py:192
  48.0 3.6 %collective-permute-start.2 = (bf16[2,8,16,768]{3,2,1,0:T(8,128)(2,1)S(1)}, bf16[2,8,16,768]{3,2,1,0:T(8,128)(2,1)}, u32[]{:S(2)}, u32[]{:S(2)}) collective-permute-start(bf16[2,8,16,768]{3,2,1,0:T(8,128)(2,1)S(1)} %pad_maximum_fusion.1.x_a), channel_id=1, source_target_pairs={{0,2},{1,3},{2,0},{3,1},{4,6},{5,7},{6,4},{7,5},{8,10},{9,11},{10,... | collective-permute-start | bytes 1179656 | tf_op jit(solution)/shard_map/ppermute | solution.py:192
  51.5 1.0 collective-permute-start.3
  52.6 5.8 %all-to-all-done.2.own = bf16[8,16,3072]{2,1,0:T(8,128)(2,1)S(1)} async-done(((bf16[8,16,3072]{2,1,0:T(8,128)(2,1)}), bf16[8,16,3072]{2,1,0:T(8,128)(2,1)S(1)}, u32[]{:S(2)}, u32[]{:S(2)}) %all-to-all-start.2) | async-done | bytes 786464 | tf_op jit(solution)/shard_map/all_to_all | solution.py:186
  58.3 0.0 collective-permute-done.5.other1
  58.3 0.0 collective-permute-start.6
  58.3 0.1 pad_add_fusion.where
  58.4 1.3 collective-permute-done.1.x_b
  59.7 9.7 %collective-permute-done.2.x_c = bf16[2,8,16,768]{3,2,1,0:T(8,128)(2,1)} collective-permute-done((bf16[2,8,16,768]{3,2,1,0:T(8,128)(2,1)S(1)}, bf16[2,8,16,768]{3,2,1,0:T(8,128)(2,1)}, u32[]{:S(2)}, u32[]{:S(2)}) %collective-permute-start.2) | collective-permute-done | bytes 393248 | tf_op jit(solution)/shard_map/ppermute | solution.py:192
  69.4 0.0 collective-permute-done.3.x_d
  69.4 0.0 collective-permute-done.4.other0
  69.4 14.2 %terms_early.1 = (f32[1024,768]{1,0:T(8,128)S(1)}, bf16[1024,768]{1,0:T(8,128)(2,1)S(1)}) custom-call(s32[2]{0:T(128)S(1)} %pad_add_fusion.where, bf16[2,8,16,768]{3,2,1,0:T(8,128)(2,1)S(1)} %pad_maximum_fusion.1.x_a, bf16[2,8,16,768]{3,2,1,0:T(8,128)(2,1)S(1)} %collective-permute-done.1.x_b, bf16[2,8,16,768]{3,2,1,0:T(8,128)(2,1)} %collective-permute-done.2.x_c, ...), custom_call_target="tpu_custom_call" | custom-call | flops 6442450944 | bytes 6291456 | tf_op jit(solution)/shard_map/terms_early/pallas_call | solution.py:144
  83.6 0.0 collective-permute-done.6.other
  83.7 5.1 %terms_late.1 = bf16[64,16,768]{2,1,0:T(8,128)(2,1)S(1)} custom-call(s32[2]{0:T(128)S(1)} %pad_add_fusion.where, bf16[1024,768]{1,0:T(8,128)(2,1)S(1)} %get-tuple-element.7.x_in, bf16[8,16,3072]{2,1,0:T(8,128)(2,1)S(1)} %all-to-all-done.2.own, bf16[8,16,3072]{2,1,0:T(8,128)(2,1)S(1)} %collective-permute-done.6.other, f32[1024,768]{1,0:T(8,128)S(1)} %get-tuple-element.8.acc_in), custom_call_target="tpu_custom_call" | custom-call | flops 3221225472 | bytes 6291456 | tf_op jit(solution)/shard_map/terms_late/pallas_call | solution.py:157
  88.8 31.1 %all_to_all.26 = bf16[64,16,768]{2,1,0:T(8,128)(2,1)S(1)} all-to-all(bf16[64,16,768]{2,1,0:T(8,128)(2,1)S(1)} %terms_late.1), channel_id=1, replica_groups=mesh['x'=4,'yl'=2,'c'=2,'yh'=2,'z'=4] {'x','yl','c','z'}, dimensions={0} | all-to-all | bytes 3145728 | tf_op jit(solution)/shard_map/all_to_all | solution.py:195
  119.9 0.0 copy-start.2
  119.9 0.0 copy-start.1
  119.9 0.2 reduce_sum.21
  120.1 0.0 copy-start
  120.2 0.8 broadcast_in_dim.8
  120.9 4.8 %all-to-all-start.4 = ((bf16[8,32,768]{2,1,0:T(8,128)(2,1)}), bf16[8,32,768]{2,1,0:T(8,128)(2,1)S(1)}, u32[]{:S(2)}, u32[]{:S(2)}) async-start(bf16[8,32,768]{2,1,0:T(8,128)(2,1)} %broadcast_in_dim.8), calls=%async_computation.4 | async-start | bytes 786432 | tf_op jit(solution)/shard_map/all_to_all | solution.py:198
  125.7 0.0 copy-done.2
  125.7 0.1 dynamic_slice.12
  125.8 0.0 copy-done.1
  125.8 0.1 broadcast_subtract_fusion
  125.9 9.6 %all-to-all-done.4 = bf16[8,32,768]{2,1,0:T(8,128)(2,1)S(1)} async-done(((bf16[8,32,768]{2,1,0:T(8,128)(2,1)}), bf16[8,32,768]{2,1,0:T(8,128)(2,1)S(1)}, u32[]{:S(2)}, u32[]{:S(2)}) %all-to-all-start.4) | async-done | bytes 393248 | tf_op jit(solution)/shard_map/all_to_all | solution.py:198
  135.5 0.1 convert_reduce_fusion
  135.6 0.0 copy-done
  135.6 0.8 multiply_subtract_fusion
  (6 shorter events, 0.1 us)
Async XLA Ops:
  26.1 14.6 %all-to-all-start.1 = ((bf16[8,16,3072]{2,1,0:T(8,128)(2,1)}), bf16[8,16,3072]{2,1,0:T(8,128)(2,1)S(1)}, u32[]{:S(2)}, u32[]{:S(2)}) async-start(bf16[8,16,3072]{2,1,0:T(8,128)(2,1)} %bitcast.5), calls=%async_computation.1 | async-start | bytes 1572864 | tf_op jit(solution)/shard_map/all_to_all | solution.py:186
  29.6 39.8 %collective-permute-start.4 = (bf16[8,16,4608]{2,1,0:T(8,128)(2,1)S(1)}, bf16[8,16,4608]{2,1,0:T(8,128)(2,1)}, u32[]{:S(2)}, u32[]{:S(2)}) collective-permute-start(bf16[8,16,4608]{2,1,0:T(8,128)(2,1)S(1)} %all_to_all.25.own0), channel_id=1, source_target_pairs={{0,8},{8,0},{1,9},{9,1},{2,10},{10,2},{3,11},{11,3},{4,12},{12,4},... | collective-permute-start | bytes 3538952 | tf_op jit(solution)/shard_map/ppermute | solution.py:187
  40.7 17.7 %collective-permute-start.5 = (bf16[8,16,3072]{2,1,0:T(8,128)(2,1)S(1)}, bf16[8,16,3072]{2,1,0:T(8,128)(2,1)}, u32[]{:S(2)}, u32[]{:S(2)}) collective-permute-start(bf16[8,16,3072]{2,1,0:T(8,128)(2,1)S(1)} %all-to-all-done.1.own1), channel_id=1, source_target_pairs={{0,8},{8,0},{1,9},{9,1},{2,10},{10,2},{3,11},{11,3},{4,12},{12,4},... | collective-permute-start | bytes 2359304 | tf_op jit(solution)/shard_map/ppermute | solution.py:187
  40.7 17.6 %all-to-all-start.2 = ((bf16[8,16,3072]{2,1,0:T(8,128)(2,1)}), bf16[8,16,3072]{2,1,0:T(8,128)(2,1)S(1)}, u32[]{:S(2)}, u32[]{:S(2)}) async-start(bf16[8,16,3072]{2,1,0:T(8,128)(2,1)} %bitcast.6), calls=%async_computation.2 | async-start | bytes 1572864 | tf_op jit(solution)/shard_map/all_to_all | solution.py:186
  44.3 1.7 %collective-permute-start = (bf16[8,16,768]{2,1,0:T(8,128)(2,1)S(1)}, bf16[8,16,768]{2,1,0:T(8,128)(2,1)S(1)}, u32[]{:S(2)}, u32[]{:S(2)}) collective-permute-start(bf16[8,16,768]{2,1,0:T(8,128)(2,1)S(1)} %get-tuple-element.13), channel_id=1, source_target_pairs={{0,8},{8,0},{1,9},{9,1},{2,10},{10,2},{3,11},{11,3},{4,12},{12,4},... | collective-permute-start | bytes 589832 | tf_op jit(solution)/shard_map/ppermute | solution.py:190
  46.0 13.8 %collective-permute-start.1 = (bf16[2,8,16,768]{3,2,1,0:T(8,128)(2,1)S(1)}, bf16[2,8,16,768]{3,2,1,0:T(8,128)(2,1)S(1)}, u32[]{:S(2)}, u32[]{:S(2)}) collective-permute-start(bf16[2,8,16,768]{3,2,1,0:T(8,128)(2,1)S(1)} %pad_maximum_fusion.1.x_a), channel_id=1, source_target_pairs={{0,1},{1,2},{2,3},{3,0},{4,5},{5,6},{6,7},{7,4},{8,9},{9,10},{10,1... | collective-permute-start | bytes 1179656 | tf_op jit(solution)/shard_map/ppermute | solution.py:192
  48.0 21.5 %collective-permute-start.2 = (bf16[2,8,16,768]{3,2,1,0:T(8,128)(2,1)S(1)}, bf16[2,8,16,768]{3,2,1,0:T(8,128)(2,1)}, u32[]{:S(2)}, u32[]{:S(2)}) collective-permute-start(bf16[2,8,16,768]{3,2,1,0:T(8,128)(2,1)S(1)} %pad_maximum_fusion.1.x_a), channel_id=1, source_target_pairs={{0,2},{1,3},{2,0},{3,1},{4,6},{5,7},{6,4},{7,5},{8,10},{9,11},{10,... | collective-permute-start | bytes 1179656 | tf_op jit(solution)/shard_map/ppermute | solution.py:192
  51.5 17.9 %collective-permute-start.3 = (bf16[2,8,16,768]{3,2,1,0:T(8,128)(2,1)S(1)}, bf16[2,8,16,768]{3,2,1,0:T(8,128)(2,1)}, u32[]{:S(2)}, u32[]{:S(2)}) collective-permute-start(bf16[2,8,16,768]{3,2,1,0:T(8,128)(2,1)S(1)} %pad_maximum_fusion.1.x_a), channel_id=1, source_target_pairs={{0,3},{1,0},{2,1},{3,2},{4,7},{5,4},{6,5},{7,6},{8,11},{9,8},{10,9... | collective-permute-start | bytes 1179656 | tf_op jit(solution)/shard_map/ppermute | solution.py:192
  58.3 25.3 %collective-permute-start.6 = (bf16[8,16,3072]{2,1,0:T(8,128)(2,1)S(1)}, bf16[8,16,3072]{2,1,0:T(8,128)(2,1)S(1)}, u32[]{:S(2)}, u32[]{:S(2)}) collective-permute-start(bf16[8,16,3072]{2,1,0:T(8,128)(2,1)S(1)} %all-to-all-done.2.own), channel_id=1, source_target_pairs={{0,8},{8,0},{1,9},{9,1},{2,10},{10,2},{3,11},{11,3},{4,12},{12,4},... | collective-permute-start | bytes 2359304 | tf_op jit(solution)/shard_map/ppermute | solution.py:187
  119.9 5.8 %copy-start.2 = (f32[64]{0:T(128)S(1)}, f32[64]{0:T(128)}, u32[]{:S(2)}) copy-start(f32[64]{0:T(128)} %param.6) | copy-start | bytes 772
  119.9 5.9 %copy-start.1 = (f32[768]{0:T(1024)S(1)}, f32[768]{0:T(1024)}, u32[]{:S(2)}) copy-start(f32[768]{0:T(1024)} %param.7) | copy-start | bytes 9220
  120.1 15.5 %copy-start = (bf16[32,3072]{1,0:T(8,128)(2,1)S(1)}, bf16[32,3072]{1,0:T(8,128)(2,1)}, u32[]{:S(2)}) copy-start(bf16[32,3072]{1,0:T(8,128)(2,1)} %param.5) | copy-start | bytes 589828
  120.9 14.6 %all-to-all-start.4 = ((bf16[8,32,768]{2,1,0:T(8,128)(2,1)}), bf16[8,32,768]{2,1,0:T(8,128)(2,1)S(1)}, u32[]{:S(2)}, u32[]{:S(2)}) async-start(bf16[8,32,768]{2,1,0:T(8,128)(2,1)} %broadcast_in_dim.8), calls=%async_computation.4 | async-start | bytes 786432 | tf_op jit(solution)/shard_map/all_to_all | solution.py:198

commit v4 on v3

v4 whole, which is shorter than its diff:
```python
import jax
import jax.numpy as jnp
from jax import lax
from jax.experimental import pallas as pl
from jax.experimental.pallas import tpu as pltpu
from jax.sharding import Mesh, PartitionSpec as P

NOCC = 64
NVIR = 768
NVEC = 32
NCHIP = 8
OCC_DEV = 4
PAIRS = OCC_DEV * NVIR
HALF = 16
CHUNKS = 3
ROWS = NOCC * HALF

F32 = jnp.float32
BF16 = jnp.bfloat16

CHIPS = ("x", "yl")
WIDE = ("x", "yl", "c")
NARROW = ("yh", "z")
MOST = ("x", "yl", "c", "z")


def swap_blocks(tile):
    v = [tile[j * 16 : (j + 1) * 16] for j in range(8)]
    lane = lax.broadcasted_iota(jnp.int32, (16, 128), 1)
    for s in (4, 2, 1):
        bit = (lane & (16 * s)) != 0
        new = list(v)
        for j in range(8):
            if j & s:
                continue
            lo, hi = v[j], v[j + s]
            new[j] = jnp.where(bit, pltpu.roll(hi, 16 * s, 1), lo)
            new[j + s] = jnp.where(bit, hi, pltpu.roll(lo, 128 - 16 * s, 1))
        v = new
    return jnp.concatenate(v, 0)


def fetch_rows(b2, own, other, sems):
    copies = []
    for rel, src in enumerate((own, other)):
        for q in range(OCC_DEV):
            there = b2.at[pl.ds(rel * NCHIP, NCHIP), q]
            cp = pltpu.make_async_copy(src.at[:, :, pl.ds(q * NVIR, NVIR)], there, sems.at[rel * OCC_DEV + q])
            cp.start()
            copies.append(cp)
    return copies


def rows_of(ref, start, count):
    return ref[start // 64 : (start + count) // 64].reshape(count, NVIR)


def contract_first(x2, b2, d, copies):
    row_i = lax.broadcasted_iota(jnp.int32, (128, 128), 0) // 16
    lane_i = lax.broadcasted_iota(jnp.int32, (128, 128), 1) // 16
    diag = row_i == lane_i
    fit = jnp.zeros((128, 128), F32)
    for g in range(4):
        if g % 2 == 0:
            for cp in copies[g * 2 : g * 2 + 4]:
                cp.wait()
        rhs = rows_of(b2, g * 256, 256)
        for rb in range(4):
            lhs = rows_of(x2, rb * 256, 256)
            inter = lax.dot_general(lhs, rhs, (((1,), (1,)), ((), ())), preferred_element_type=F32)
            for a in range(2):
                for h in range(2):
                    ig, jg = g * 2 + h, rb * 2 + a
                    tile = inter[a * 128 : (a + 1) * 128, h * 128 : (h + 1) * 128]
                    if ig == jg:
                        fit = fit + jnp.where(diag, tile, 0.0)
                    d[ig * 128 : (ig + 1) * 128, jg * 128 : (jg + 1) * 128] = swap_blocks(tile).astype(BF16)
    total = fit[0:16, :]
    for j in range(1, 8):
        total = total + fit[j * 16 : (j + 1) * 16, :]
    for s in (64, 32, 16):
        total = total + pltpu.roll(total, s, 1)
    fit_b = 2.0 * total.astype(BF16).astype(F32)
    sub = jnp.where(diag, jnp.concatenate([fit_b] * 8, 0), 0.0)
    for g in range(8):
        s = slice(g * 128, (g + 1) * 128)
        d[s, s] = (d[s, s].astype(F32) - sub).astype(BF16)


def early_kernel(where, x_a, x_b, x_c, x_d, own0, other0, own1, other1, out, x_out, x2, b_a, b_b, d, acc, xs, bs, os):
    z = where[1]
    gets = []
    for s, ref in enumerate((x_a, x_b, x_c, x_d)):
        gets.append(pltpu.make_async_copy(ref, x2.at[:, (z - s) & 3], xs.at[s]))
        gets[-1].start()
    rows0 = fetch_rows(b_a, own0, other0, bs.at[0])
    rows1 = fetch_rows(b_b, own1, other1, bs.at[1])
    for cp in gets:
        cp.wait()
    keep_x = pltpu.make_async_copy(x2, x_out, xs.at[4])
    keep_x.start()
    puts = []
    for t, (b2, copies) in enumerate(((b_a, rows0), (b_b, rows1))):
        contract_first(x2, b2, d, copies)
        for rb in range(4):
            rows = slice(rb * 256, (rb + 1) * 256)
            term = jnp.dot(d[rows, :], rows_of(b2, 0, ROWS), preferred_element_type=F32)
            if t == 0:
                acc[rows, :] = term
            else:
                acc[rows, :] += term
                puts.append(pltpu.make_async_copy(acc.at[rows], out.at[rows], os.at[rb]))
                puts[-1].start()
    keep_x.wait()
    for cp in puts:
        cp.wait()


def late_kernel(where, x_in, own, other, acc_in, out, x2, b2, d, acc, res, xs, bs, os):
    c = where[0]
    get_x = pltpu.make_async_copy(x_in, x2, xs.at[0])
    get_x.start()
    copies = fetch_rows(b2, own, other, bs)
    get_acc = pltpu.make_async_copy(acc_in, acc, xs.at[1])
    get_acc.start()
    get_x.wait()
    contract_first(x2, b2, d, copies)
    get_acc.wait()
    puts = []
    for rb in range(4):
        rows = slice(rb * 256, (rb + 1) * 256)
        term = acc[rows, :] + jnp.dot(d[rows, :], rows_of(b2, 0, ROWS), preferred_element_type=F32)
        res[rb * 4 : (rb + 1) * 4] = term.astype(BF16).reshape(4, OCC_DEV, HALF, NVIR)
        for k in range(4):
            rel, chip = rb // 2, (rb % 2) * 4 + k
            puts.append(pltpu.make_async_copy(res.at[rb * 4 + k], out.at[chip * 2 + (c ^ rel)], os.at[rb * 4 + k]))
            puts[-1].start()
    for cp in puts:
        cp.wait()


SMEM = pl.BlockSpec(memory_space=pltpu.SMEM)
ANY = pl.BlockSpec(memory_space=pl.ANY)
BLOCK = (16, OCC_DEV, HALF, NVIR)


def cost(count):
    return pl.CostEstimate(flops=count * 4 * ROWS * ROWS * NVIR, bytes_accessed=4 * ROWS * NVIR * 2, transcendentals=0)


def early(where, x, own, other):
    return pl.pallas_call(
        early_kernel,
        out_shape=[jax.ShapeDtypeStruct((ROWS, NVIR), F32), jax.ShapeDtypeStruct(BLOCK, BF16)],
        in_specs=[SMEM] + [ANY] * 8,
        out_specs=[ANY, ANY],
        scratch_shapes=[
            pltpu.VMEM(BLOCK, BF16),
            pltpu.VMEM(BLOCK, BF16),
            pltpu.VMEM(BLOCK, BF16),
            pltpu.VMEM((ROWS, ROWS), BF16),
            pltpu.VMEM((ROWS, NVIR), F32),
            pltpu.SemaphoreType.DMA((5,)),
            pltpu.SemaphoreType.DMA((2, 8)),
            pltpu.SemaphoreType.DMA((4,)),
        ],
        cost_estimate=cost(2),
        compiler_params=pltpu.CompilerParams(vmem_limit_bytes=60 << 20),
        name="terms_early",
    )(where, *x, own[0], other[0], own[1], other[1])


def late(where, x2, own, other, acc):
    return pl.pallas_call(
        late_kernel,
        out_shape=jax.ShapeDtypeStruct(BLOCK, BF16),
        in_specs=[SMEM] + [ANY] * 4,
        out_specs=ANY,
        scratch_shapes=[
            pltpu.VMEM(BLOCK, BF16),
            pltpu.VMEM(BLOCK, BF16),
            pltpu.VMEM((ROWS, ROWS), BF16),
            pltpu.VMEM((ROWS, NVIR), F32),
            pltpu.VMEM(BLOCK, BF16),
            pltpu.SemaphoreType.DMA((2,)),
            pltpu.SemaphoreType.DMA((8,)),
            pltpu.SemaphoreType.DMA((16,)),
        ],
        cost_estimate=cost(1),
        compiler_params=pltpu.CompilerParams(vmem_limit_bytes=60 << 20),
        name="terms_late",
    )(where, x2, own[2], other[2], acc).reshape(16 * OCC_DEV, HALF, NVIR)


def ring(n, s):
    return [(i, (i + s) % n) for i in range(n)]


def body(fit_rows, trials, occ_energy, vir_energy):
    core = lax.axis_index("c").astype(jnp.int32)
    z = lax.axis_index("z").astype(jnp.int32)
    where = jnp.stack([core, z])
    blocks = [fit_rows.reshape(CHUNKS, NCHIP, HALF, PAIRS)]
    for _ in range(1, CHUNKS):
        blocks.append(lax.optimization_barrier(blocks[-1]))
    mine = lax.dynamic_slice_in_dim(trials, z * NVIR, NVIR, 1)
    mine = jnp.concatenate([mine[:HALF], mine[HALF:]], 1)
    mine = jnp.broadcast_to(mine[None], (NCHIP, HALF, 2 * NVIR))
    own, other = [], []
    for t in range(CHUNKS):
        send = blocks[t][t]
        if t == 0:
            send = jnp.concatenate([send, mine], 2)
        own.append(lax.all_to_all(send, CHIPS, 0, 0, tiled=True))
        other.append(lax.ppermute(own[t], "c", ring(2, 1)))
    x_own = lax.dynamic_slice_in_dim(own[0], PAIRS + core * NVIR, NVIR, 2)
    x_send = lax.dynamic_slice_in_dim(own[0], PAIRS + (1 - core) * NVIR, NVIR, 2)
    x_other = lax.ppermute(x_send, "c", ring(2, 1))
    x = [jnp.concatenate([x_own, x_other])]
    x = x + [lax.ppermute(x[0], "z", ring(4, s)) for s in (1, 2, 3)]
    acc, x2 = early(where, x, own, other)
    acc = late(where, x2, own, other, acc)
    parts = lax.all_to_all(acc, MOST, 0, 0, tiled=True)
    part = jnp.sum(parts.reshape(NCHIP, 2, 4, HALF, NVIR).astype(F32), (0, 2)).astype(BF16)
    part = jnp.broadcast_to(part.reshape(1, NVEC, NVIR), (8, NVEC, NVIR))
    every = lax.all_to_all(part, NARROW, 0, 0, tiled=True)
    total = jnp.sum(every.reshape(2, OCC_DEV, NVEC, NVIR).astype(F32), 0)
    total = total.transpose(1, 0, 2).reshape(NVEC, PAIRS)
    w = lax.axis_index(WIDE)
    occ = lax.dynamic_slice_in_dim(occ_energy, w * OCC_DEV, OCC_DEV)
    delta = (vir_energy[None, :] - occ[:, None]).reshape(PAIRS)
    return delta[None, :] * trials.astype(F32) - total


def solution(mesh):
    fine = Mesh(mesh.devices.reshape(4, 2, 2, 2, 4), ("x", "yl", "c", "yh", "z"))
    in_specs = (P(NARROW, WIDE), P(None, WIDE), P(), P())
    return jax.shard_map(body, mesh=fine, in_specs=in_specs, out_specs=P(None, WIDE), check_vma=False)
```

time: 137 us -> 144 us (1.051)
  blocking collectives: 53.4 us -> 31.4 us
  waiting for transfers between devices: 38.5 us -> 53.7 us
  starting transfers between devices: 19.1 us -> 24.5 us
  Pallas kernels: 19.3 us -> 24.2 us
  local copies, waits for them, and re-layouts: 4.65 us -> 6.84 us
  other arithmetic: 1.35 us -> 2.96 us
    all_to_all x1 -> x0, blocking collectives: 22.2 us -> none  [body(): own.append(lax.all_to_all(send, CHIPS, 0, 0, tiled=True))]
    all_to_all x2 -> x3, waiting for transfers between devices: 16.7 us -> 32.5 us  [body(): own.append(lax.all_to_all(send, CHIPS, 0, 0, tiled=True))]
    all_to_all x2 -> x3, starting transfers between devices: 7.09 us -> 12.5 us  [body(): own.append(lax.all_to_all(send, CHIPS, 0, 0, tiled=True))]
    squeeze x0 -> x2, local copies, waits for them, and re-layouts: none -> 3.25 us  [body(): send = blocks[t][t]]
    slice x1, local copies, waits for them, and re-layouts: 2.93 us -> 0.05 us  [body(): send = blocks[t][t]]
    pallas_call x1, Pallas kernels: 5.11 us -> 7.79 us  [late(): pl.pallas_call(late_kernel, out_shape=jax.ShapeDtypeStruct(BLOCK, BF16),...]
    pallas_call x1, Pallas kernels: 14.2 us -> 16.4 us  [early(): pl.pallas_call(early_kernel, out_shape=[jax.ShapeDtypeStruct((ROWS, NVIR)...]
    unnamed x6 -> x20, local copies, waits for them, and re-layouts: 0.01 us -> 1.82 us
  transfers between devices with their start and end apart: 10 -> 11, of which waited for: 6 -> 7; matrix products, arithmetic and copies ran while one was open for 0% -> 3% of each run, Pallas kernels for 10% -> 11%
where the time goes in v4:
time: 144 us
  waiting for transfers between devices  53.7 us (37%)
  blocking collectives  31.4 us (22%)
  starting transfers between devices  24.5 us (17%)
  Pallas kernels  24.2 us (17%)
  local copies, waits for them, and re-layouts  6.84 us (5%)
  other arithmetic  2.96 us (2%)
    all_to_all x3, waiting for transfers between devices, body(): own.append(lax.all_to_all(send, CHIPS, 0, 0, tiled=True))  32.5 us
    all_to_all x1, blocking collectives, body(): parts = lax.all_to_all(acc, MOST, 0, 0, tiled=True)  31.4 us
    pallas_call x1, Pallas kernels, early(): pl.pallas_call(early_kernel, out_shape=[jax.ShapeDtypeStruct((ROWS, NVIR)...  16.4 us
    all_to_all x3, starting transfers between devices, body(): own.append(lax.all_to_all(send, CHIPS, 0, 0, tiled=True))  12.5 us
    ppermute x3, waiting for transfers between devices, body(): x = x + [lax.ppermute(x[0], 'z', ring(4, s)) for s in (1, 2, 3)]  10.6 us
    all_to_all x1, waiting for transfers between devices, body(): every = lax.all_to_all(part, NARROW, 0, 0, tiled=True)  9.6 us
    pallas_call x1, Pallas kernels, late(): pl.pallas_call(late_kernel, out_shape=jax.ShapeDtypeStruct(BLOCK, BF16),...  7.79 us
    ppermute x3, starting transfers between devices, body(): x = x + [lax.ppermute(x[0], 'z', ring(4, s)) for s in (1, 2, 3)]  6.58 us
  transfers between devices with their start and end apart: 11, of which 7 were waited for; matrix products, arithmetic and copies ran while one was open for 3% of the time, Pallas kernels for 11%

profile of v4, /device:TPU:0, one launch (start us, length us, event | category | flops | bytes accessed | tf_op | source)
XLA Modules:
  0.0 143.8 jit_solution(12470261234496781433)
XLA Ops:
  0.0 0.0 copy-start
  0.0 2.2 %slice_bitcast_fusion.1 = bf16[8,16,3072]{2,1,0:T(8,128)(2,1)} fusion(bf16[3,8,16,3072]{3,2,1,0:T(8,128)(2,1)} %bitcast.18), kind=kLoop, calls=%fused_computation.2 | loop fusion | bytes 1572864 | tf_op jit(solution)/shard_map/squeeze | solution.py:211
  2.2 5.4 %all-to-all-start.1 = ((bf16[8,16,3072]{2,1,0:T(8,128)(2,1)}), bf16[8,16,3072]{2,1,0:T(8,128)(2,1)S(1)}, u32[]{:S(2)}, u32[]{:S(2)}) async-start(bf16[8,16,3072]{2,1,0:T(8,128)(2,1)} %slice_bitcast_fusion.1), calls=%async_computation.1 | async-start | bytes 1572864 | tf_op jit(solution)/shard_map/all_to_all | solution.py:214
  7.6 0.8 constant_dynamic-slice_fusion
  8.4 0.0 copy-done
  8.4 0.1 slice.16
  8.5 1.1 pad_maximum_fusion
  9.6 10.4 %all-to-all-done.1.own1 = bf16[8,16,3072]{2,1,0:T(8,128)(2,1)S(1)} async-done(((bf16[8,16,3072]{2,1,0:T(8,128)(2,1)}), bf16[8,16,3072]{2,1,0:T(8,128)(2,1)S(1)}, u32[]{:S(2)}, u32[]{:S(2)}) %all-to-all-start.1) | async-done | bytes 786464 | tf_op jit(solution)/shard_map/all_to_all | solution.py:214
  20.0 0.0 copy-start.2
  20.0 0.9 copy-done.2
  20.9 3.6 %all-to-all-start = ((bf16[8,16,4608]{2,1,0:T(8,128)(2,1)}), bf16[8,16,4608]{2,1,0:T(8,128)(2,1)S(1)}, u32[]{:S(2)}, u32[]{:S(2)}) async-start(bf16[8,16,4608]{2,1,0:T(8,128)(2,1)} %pad_maximum_fusion), calls=%async_computation | async-start | bytes 2359296 | tf_op jit(solution)/shard_map/all_to_all | solution.py:214
  24.5 0.1 collective-permute-start.5
  24.6 16.4 %all-to-all-done.own0 = bf16[8,16,4608]{2,1,0:T(8,128)(2,1)S(1)} async-done(((bf16[8,16,4608]{2,1,0:T(8,128)(2,1)}), bf16[8,16,4608]{2,1,0:T(8,128)(2,1)S(1)}, u32[]{:S(2)}, u32[]{:S(2)}) %all-to-all-start) | async-done | bytes 1179680 | tf_op jit(solution)/shard_map/all_to_all | solution.py:214
  41.0 0.0 copy-start.1
  41.0 0.0 collective-permute-start.4
  41.0 1.0 slice_bitcast_fusion
  42.0 3.5 %all-to-all-start.2 = ((bf16[8,16,3072]{2,1,0:T(8,128)(2,1)}), bf16[8,16,3072]{2,1,0:T(8,128)(2,1)S(1)}, u32[]{:S(2)}, u32[]{:S(2)}) async-start(bf16[8,16,3072]{2,1,0:T(8,128)(2,1)} %slice_bitcast_fusion), calls=%async_computation.2 | async-start | bytes 1572864 | tf_op jit(solution)/shard_map/all_to_all | solution.py:214
  45.6 0.0 copy-done.1
  45.7 0.5 collective-permute-start
  46.2 1.1 collective-permute-done
  47.3 0.0 copy-start.4
  47.3 2.0 %collective-permute-start.1 = (bf16[16,16,768]{2,1,0:T(8,128)(2,1)S(1)}, bf16[16,16,768]{2,1,0:T(8,128)(2,1)S(1)}, u32[]{:S(2)}, u32[]{:S(2)}) collective-permute-start(bf16[16,16,768]{2,1,0:T(8,128)(2,1)S(1)} %pad_maximum_fusion.1.x_a), channel_id=1, source_target_pairs={{0,1},{1,2},{2,3},{3,0},{4,5},{5,6},{6,7},{7,4},{8,9},{9,10},{10,1... | collective-permute-start | bytes 1179656 | tf_op jit(solution)/shard_map/ppermute | solution.py:220
  49.3 3.6 %collective-permute-start.2 = (bf16[16,16,768]{2,1,0:T(8,128)(2,1)S(1)}, bf16[16,16,768]{2,1,0:T(8,128)(2,1)}, u32[]{:S(2)}, u32[]{:S(2)}) collective-permute-start(bf16[16,16,768]{2,1,0:T(8,128)(2,1)S(1)} %pad_maximum_fusion.1.x_a), channel_id=1, source_target_pairs={{0,2},{1,3},{2,0},{3,1},{4,6},{5,7},{6,4},{7,5},{8,10},{9,11},{10,... | collective-permute-start | bytes 1179656 | tf_op jit(solution)/shard_map/ppermute | solution.py:220
  52.9 1.0 collective-permute-start.3
  53.9 5.6 %all-to-all-done.2.own = bf16[8,16,3072]{2,1,0:T(8,128)(2,1)S(1)} async-done(((bf16[8,16,3072]{2,1,0:T(8,128)(2,1)}), bf16[8,16,3072]{2,1,0:T(8,128)(2,1)S(1)}, u32[]{:S(2)}, u32[]{:S(2)}) %all-to-all-start.2) | async-done | bytes 786464 | tf_op jit(solution)/shard_map/all_to_all | solution.py:214
  59.5 0.0 copy-start.3
  59.5 0.0 collective-permute-done.5.other1
  59.5 0.0 collective-permute-start.6
  59.5 0.6 pad_add_fusion.where
  60.2 0.9 collective-permute-done.1.x_b
  61.0 0.0 copy-start.8
  61.1 9.7 %collective-permute-done.2.x_c = bf16[16,16,768]{2,1,0:T(8,128)(2,1)} collective-permute-done((bf16[16,16,768]{2,1,0:T(8,128)(2,1)S(1)}, bf16[16,16,768]{2,1,0:T(8,128)(2,1)}, u32[]{:S(2)}, u32[]{:S(2)}) %collective-permute-start.2) | collective-permute-done | bytes 393248 | tf_op jit(solution)/shard_map/ppermute | solution.py:220
  70.8 0.0 collective-permute-done.3.x_d
  70.8 0.0 collective-permute-done.4.other0
  70.8 0.0 copy-done.4
  70.8 0.0 copy-done.8
  70.8 16.4 %terms_early.1 = (f32[1024,768]{1,0:T(8,128)}, bf16[16,4,16,768]{3,2,1,0:T(8,128)(2,1)}) custom-call(s32[2]{0:T(128)} %pad_add_fusion.where, bf16[16,16,768]{2,1,0:T(8,128)(2,1)} %copy-done.4, bf16[16,16,768]{2,1,0:T(8,128)(2,1)} %copy-done.8, bf16[16,16,768]{2,1,0:T(8,128)(2,1)} %collective-permute-done.2.x_c, ...), custom_call_target="tpu_custom_call" | custom-call | flops 6442450944 | bytes 6291456 | tf_op jit(solution)/shard_map/terms_early/pallas_call | solution.py:152
  87.2 0.0 copy-done.3
  87.2 0.0 collective-permute-done.6.other
  87.2 0.0 copy-start.7
  87.2 0.9 copy-done.7
  88.1 7.8 %terms_late.1 = bf16[16,4,16,768]{3,2,1,0:T(8,128)(2,1)} custom-call(s32[2]{0:T(128)} %pad_add_fusion.where, bf16[16,4,16,768]{3,2,1,0:T(8,128)(2,1)} %get-tuple-element.7.x_in, bf16[8,16,3072]{2,1,0:T(8,128)(2,1)} %copy-done.3, bf16[8,16,3072]{2,1,0:T(8,128)(2,1)} %copy-done.7, f32[1024,768]{1,0:T(8,128)} %get-tuple-element.8.acc_in), custom_call_target="tpu_custom_call" | custom-call | flops 3221225472 | bytes 6291456 | tf_op jit(solution)/shard_map/terms_late/pallas_call | solution.py:174
  95.9 31.4 %all_to_all.25 = bf16[64,16,768]{2,1,0:T(8,128)(2,1)S(1)} all-to-all(bf16[64,16,768]{2,1,0:T(8,128)(2,1)} %bitcast.20), channel_id=1, replica_groups=mesh['x'=4,'yl'=2,'c'=2,'yh'=2,'z'=4] {'x','yl','c','z'}, dimensions={0} | all-to-all | bytes 3145728 | tf_op jit(solution)/shard_map/all_to_all | solution.py:223
  127.3 0.0 copy-start.9
  127.3 0.0 copy-start.6
  127.3 0.2 reduce_sum.21
  127.5 0.0 copy-start.5
  127.5 0.8 broadcast_in_dim.8
  128.3 4.8 %all-to-all-start.4 = ((bf16[8,32,768]{2,1,0:T(8,128)(2,1)}), bf16[8,32,768]{2,1,0:T(8,128)(2,1)S(1)}, u32[]{:S(2)}, u32[]{:S(2)}) async-start(bf16[8,32,768]{2,1,0:T(8,128)(2,1)} %broadcast_in_dim.8), calls=%async_computation.4 | async-start | bytes 786432 | tf_op jit(solution)/shard_map/all_to_all | solution.py:226
  133.1 0.0 copy-done.9
  133.1 0.1 dynamic_slice.12
  133.2 0.0 copy-done.6
  133.2 0.1 broadcast_subtract_fusion
  133.3 9.6 %all-to-all-done.4 = bf16[8,32,768]{2,1,0:T(8,128)(2,1)S(1)} async-done(((bf16[8,32,768]{2,1,0:T(8,128)(2,1)}), bf16[8,32,768]{2,1,0:T(8,128)(2,1)S(1)}, u32[]{:S(2)}, u32[]{:S(2)}) %all-to-all-start.4) | async-done | bytes 393248 | tf_op jit(solution)/shard_map/all_to_all | solution.py:226
  142.9 0.1 convert_reduce_fusion
  143.0 0.0 copy-done.5
  143.0 0.8 multiply_subtract_fusion
  (6 shorter events, 0.1 us)
Async XLA Ops:
  0.0 8.4 %copy-start = (bf16[384,3072]{1,0:T(8,128)(2,1)S(1)}, bf16[384,3072]{1,0:T(8,128)(2,1)}, u32[]{:S(2)}) copy-start(bf16[384,3072]{1,0:T(8,128)(2,1)} %param.4) | copy-start | bytes 7077892
  2.2 17.8 %all-to-all-start.1 = ((bf16[8,16,3072]{2,1,0:T(8,128)(2,1)}), bf16[8,16,3072]{2,1,0:T(8,128)(2,1)S(1)}, u32[]{:S(2)}, u32[]{:S(2)}) async-start(bf16[8,16,3072]{2,1,0:T(8,128)(2,1)} %slice_bitcast_fusion.1), calls=%async_computation.1 | async-start | bytes 1572864 | tf_op jit(solution)/shard_map/all_to_all | solution.py:214
  20.0 0.9 copy-start.2
  20.9 20.1 %all-to-all-start = ((bf16[8,16,4608]{2,1,0:T(8,128)(2,1)}), bf16[8,16,4608]{2,1,0:T(8,128)(2,1)S(1)}, u32[]{:S(2)}, u32[]{:S(2)}) async-start(bf16[8,16,4608]{2,1,0:T(8,128)(2,1)} %pad_maximum_fusion), calls=%async_computation | async-start | bytes 2359296 | tf_op jit(solution)/shard_map/all_to_all | solution.py:214
  24.5 35.1 %collective-permute-start.5 = (bf16[8,16,3072]{2,1,0:T(8,128)(2,1)}, bf16[8,16,3072]{2,1,0:T(8,128)(2,1)}, u32[]{:S(2)}, u32[]{:S(2)}) collective-permute-start(bf16[8,16,3072]{2,1,0:T(8,128)(2,1)} %copy-done.2), channel_id=1, source_target_pairs={{0,8},{8,0},{1,9},{9,1},{2,10},{10,2},{3,11},{11,3},{4,12},{12,4},... | collective-permute-start | bytes 2359304 | tf_op jit(solution)/shard_map/ppermute | solution.py:215
  41.0 4.6 %copy-start.1 = (bf16[8,16,4608]{2,1,0:T(8,128)(2,1)}, bf16[8,16,4608]{2,1,0:T(8,128)(2,1)S(1)}, u32[]{:S(2)}) copy-start(bf16[8,16,4608]{2,1,0:T(8,128)(2,1)S(1)} %all-to-all-done.own0) | copy-start | bytes 3538948
  41.0 29.8 %collective-permute-start.4 = (bf16[8,16,4608]{2,1,0:T(8,128)(2,1)S(1)}, bf16[8,16,4608]{2,1,0:T(8,128)(2,1)}, u32[]{:S(2)}, u32[]{:S(2)}) collective-permute-start(bf16[8,16,4608]{2,1,0:T(8,128)(2,1)S(1)} %all-to-all-done.own0), channel_id=1, source_target_pairs={{0,8},{8,0},{1,9},{9,1},{2,10},{10,2},{3,11},{11,3},{4,12},{12,4},... | collective-permute-start | bytes 3538952 | tf_op jit(solution)/shard_map/ppermute | solution.py:215
  42.0 17.5 %all-to-all-start.2 = ((bf16[8,16,3072]{2,1,0:T(8,128)(2,1)}), bf16[8,16,3072]{2,1,0:T(8,128)(2,1)S(1)}, u32[]{:S(2)}, u32[]{:S(2)}) async-start(bf16[8,16,3072]{2,1,0:T(8,128)(2,1)} %slice_bitcast_fusion), calls=%async_computation.2 | async-start | bytes 1572864 | tf_op jit(solution)/shard_map/all_to_all | solution.py:214
  45.7 1.6 %collective-permute-start = (bf16[8,16,768]{2,1,0:T(8,128)(2,1)S(1)}, bf16[8,16,768]{2,1,0:T(8,128)(2,1)S(1)}, u32[]{:S(2)}, u32[]{:S(2)}) collective-permute-start(bf16[8,16,768]{2,1,0:T(8,128)(2,1)S(1)} %get-tuple-element.10), channel_id=1, source_target_pairs={{0,8},{8,0},{1,9},{9,1},{2,10},{10,2},{3,11},{11,3},{4,12},{12,4},... | collective-permute-start | bytes 589832 | tf_op jit(solution)/shard_map/ppermute | solution.py:218
  47.3 23.5 %copy-start.4 = (bf16[16,16,768]{2,1,0:T(8,128)(2,1)}, bf16[16,16,768]{2,1,0:T(8,128)(2,1)S(1)}, u32[]{:S(2)}) copy-start(bf16[16,16,768]{2,1,0:T(8,128)(2,1)S(1)} %pad_maximum_fusion.1.x_a) | copy-start | bytes 1179652
  47.3 13.8 %collective-permute-start.1 = (bf16[16,16,768]{2,1,0:T(8,128)(2,1)S(1)}, bf16[16,16,768]{2,1,0:T(8,128)(2,1)S(1)}, u32[]{:S(2)}, u32[]{:S(2)}) collective-permute-start(bf16[16,16,768]{2,1,0:T(8,128)(2,1)S(1)} %pad_maximum_fusion.1.x_a), channel_id=1, source_target_pairs={{0,1},{1,2},{2,3},{3,0},{4,5},{5,6},{6,7},{7,4},{8,9},{9,10},{10,1... | collective-permute-start | bytes 1179656 | tf_op jit(solution)/shard_map/ppermute | solution.py:220
  49.3 21.5 %collective-permute-start.2 = (bf16[16,16,768]{2,1,0:T(8,128)(2,1)S(1)}, bf16[16,16,768]{2,1,0:T(8,128)(2,1)}, u32[]{:S(2)}, u32[]{:S(2)}) collective-permute-start(bf16[16,16,768]{2,1,0:T(8,128)(2,1)S(1)} %pad_maximum_fusion.1.x_a), channel_id=1, source_target_pairs={{0,2},{1,3},{2,0},{3,1},{4,6},{5,7},{6,4},{7,5},{8,10},{9,11},{10,... | collective-permute-start | bytes 1179656 | tf_op jit(solution)/shard_map/ppermute | solution.py:220
  52.9 17.9 %collective-permute-start.3 = (bf16[16,16,768]{2,1,0:T(8,128)(2,1)S(1)}, bf16[16,16,768]{2,1,0:T(8,128)(2,1)}, u32[]{:S(2)}, u32[]{:S(2)}) collective-permute-start(bf16[16,16,768]{2,1,0:T(8,128)(2,1)S(1)} %pad_maximum_fusion.1.x_a), channel_id=1, source_target_pairs={{0,3},{1,0},{2,1},{3,2},{4,7},{5,4},{6,5},{7,6},{8,11},{9,8},{10,9... | collective-permute-start | bytes 1179656 | tf_op jit(solution)/shard_map/ppermute | solution.py:220
  59.5 27.7 %copy-start.3 = (bf16[8,16,3072]{2,1,0:T(8,128)(2,1)}, bf16[8,16,3072]{2,1,0:T(8,128)(2,1)S(1)}, u32[]{:S(2)}) copy-start(bf16[8,16,3072]{2,1,0:T(8,128)(2,1)S(1)} %all-to-all-done.2.own) | copy-start | bytes 2359300
  59.5 27.7 %collective-permute-start.6 = (bf16[8,16,3072]{2,1,0:T(8,128)(2,1)S(1)}, bf16[8,16,3072]{2,1,0:T(8,128)(2,1)S(1)}, u32[]{:S(2)}, u32[]{:S(2)}) collective-permute-start(bf16[8,16,3072]{2,1,0:T(8,128)(2,1)S(1)} %all-to-all-done.2.own), channel_id=1, source_target_pairs={{0,8},{8,0},{1,9},{9,1},{2,10},{10,2},{3,11},{11,3},{4,12},{12,4},... | collective-permute-start | bytes 2359304 | tf_op jit(solution)/shard_map/ppermute | solution.py:215
  61.0 9.7 %copy-start.8 = (bf16[16,16,768]{2,1,0:T(8,128)(2,1)}, bf16[16,16,768]{2,1,0:T(8,128)(2,1)S(1)}, u32[]{:S(2)}) copy-start(bf16[16,16,768]{2,1,0:T(8,128)(2,1)S(1)} %collective-permute-done.1.x_b) | copy-start | bytes 1179652
  87.2 0.9 copy-start.7
  127.3 5.8 %copy-start.9 = (f32[64]{0:T(128)S(1)}, f32[64]{0:T(128)}, u32[]{:S(2)}) copy-start(f32[64]{0:T(128)} %param.6) | copy-start | bytes 772
  127.3 5.9 %copy-start.6 = (f32[768]{0:T(1024)S(1)}, f32[768]{0:T(1024)}, u32[]{:S(2)}) copy-start(f32[768]{0:T(1024)} %param.7) | copy-start | bytes 9220
  127.5 15.5 %copy-start.5 = (bf16[32,3072]{1,0:T(8,128)(2,1)S(1)}, bf16[32,3072]{1,0:T(8,128)(2,1)}, u32[]{:S(2)}) copy-start(bf16[32,3072]{1,0:T(8,128)(2,1)} %param.5) | copy-start | bytes 589828
  128.3 14.6 %all-to-all-start.4 = ((bf16[8,32,768]{2,1,0:T(8,128)(2,1)}), bf16[8,32,768]{2,1,0:T(8,128)(2,1)S(1)}, u32[]{:S(2)}, u32[]{:S(2)}) async-start(bf16[8,32,768]{2,1,0:T(8,128)(2,1)} %broadcast_in_dim.8), calls=%async_computation.4 | async-start | bytes 786432 | tf_op jit(solution)/shard_map/all_to_all | solution.py:226

commit v5 on v4

--- a/solution.py
+++ b/solution.py
@@ -55,11 +55,7 @@
     return ref[start // 64 : (start + count) // 64].reshape(count, NVIR)
 
 
-def contract_first(x2, b2, d, copies):
-    row_i = lax.broadcasted_iota(jnp.int32, (128, 128), 0) // 16
-    lane_i = lax.broadcasted_iota(jnp.int32, (128, 128), 1) // 16
-    diag = row_i == lane_i
-    fit = jnp.zeros((128, 128), F32)
+def contract_first(x2, b2, d, diag, copies):
     for g in range(4):
         if g % 2 == 0:
             for cp in copies[g * 2 : g * 2 + 4]:
@@ -73,21 +69,30 @@
                     ig, jg = g * 2 + h, rb * 2 + a
                     tile = inter[a * 128 : (a + 1) * 128, h * 128 : (h + 1) * 128]
                     if ig == jg:
-                        fit = fit + jnp.where(diag, tile, 0.0)
+                        diag[ig] = tile
                     d[ig * 128 : (ig + 1) * 128, jg * 128 : (jg + 1) * 128] = swap_blocks(tile).astype(BF16)
+    same = lax.broadcasted_iota(jnp.int32, (128, 128), 0) // 16 == lax.broadcasted_iota(jnp.int32, (128, 128), 1) // 16
+    fit = diag[0]
+    for k in range(1, 8):
+        fit = fit + diag[k]
+    fit = jnp.where(same, fit, 0.0)
     total = fit[0:16, :]
     for j in range(1, 8):
         total = total + fit[j * 16 : (j + 1) * 16, :]
     for s in (64, 32, 16):
         total = total + pltpu.roll(total, s, 1)
-    fit_b = 2.0 * total.astype(BF16).astype(F32)
-    sub = jnp.where(diag, jnp.concatenate([fit_b] * 8, 0), 0.0)
-    for g in range(8):
-        s = slice(g * 128, (g + 1) * 128)
-        d[s, s] = (d[s, s].astype(F32) - sub).astype(BF16)
-
-
-def early_kernel(where, x_a, x_b, x_c, x_d, own0, other0, own1, other1, out, x_out, x2, b_a, b_b, d, acc, xs, bs, os):
+    double = 2.0 * total.astype(BF16).astype(F32)
+    return jnp.where(same, jnp.concatenate([double] * 8, 0), 0.0).astype(BF16)
+
+
+def contract_second(b2, d, acc, clear):
+    for rb in range(4):
+        rows = slice(rb * 256, (rb + 1) * 256)
+        term = jnp.dot(d[rows, :], rows_of(b2, 0, ROWS), preferred_element_type=F32)
+        acc[rows, :] = term if clear else acc[rows, :] + term
+
+
+def early_kernel(where, x_a, x_b, x_c, x_d, own0, other0, own1, other1, out, x_out, x2, b_a, b_b, d, acc, diag, xs, bs, os):
     z = where[1]
     gets = []
     for s, ref in enumerate((x_a, x_b, x_c, x_d)):
@@ -101,22 +106,20 @@
     keep_x.start()
     puts = []
     for t, (b2, copies) in enumerate(((b_a, rows0), (b_b, rows1))):
-        contract_first(x2, b2, d, copies)
-        for rb in range(4):
-            rows = slice(rb * 256, (rb + 1) * 256)
-            term = jnp.dot(d[rows, :], rows_of(b2, 0, ROWS), preferred_element_type=F32)
-            if t == 0:
-                acc[rows, :] = term
-            else:
-                acc[rows, :] += term
-                puts.append(pltpu.make_async_copy(acc.at[rows], out.at[rows], os.at[rb]))
+        fit = contract_first(x2, b2, d, diag, copies)
+        contract_second(b2, d, acc, t == 0)
+        for g in range(8):
+            rows = slice(g * 128, (g + 1) * 128)
+            acc[rows, :] -= jnp.dot(fit, rows_of(b2, g * 128, 128), preferred_element_type=F32)
+            if t == 1:
+                puts.append(pltpu.make_async_copy(acc.at[rows], out.at[rows], os.at[g]))
                 puts[-1].start()
     keep_x.wait()
     for cp in puts:
         cp.wait()
 
 
-def late_kernel(where, x_in, own, other, acc_in, out, x2, b2, d, acc, res, xs, bs, os):
+def late_kernel(where, x_in, own, other, acc_in, out, x2, b2, d, acc, diag, res, xs, bs, os):
     c = where[0]
     get_x = pltpu.make_async_copy(x_in, x2, xs.at[0])
     get_x.start()
@@ -124,16 +127,16 @@
     get_acc = pltpu.make_async_copy(acc_in, acc, xs.at[1])
     get_acc.start()
     get_x.wait()
-    contract_first(x2, b2, d, copies)
+    fit = contract_first(x2, b2, d, diag, copies)
     get_acc.wait()
+    contract_second(b2, d, acc, False)
     puts = []
-    for rb in range(4):
-        rows = slice(rb * 256, (rb + 1) * 256)
-        term = acc[rows, :] + jnp.dot(d[rows, :], rows_of(b2, 0, ROWS), preferred_element_type=F32)
-        res[rb * 4 : (rb + 1) * 4] = term.astype(BF16).reshape(4, OCC_DEV, HALF, NVIR)
-        for k in range(4):
-            rel, chip = rb // 2, (rb % 2) * 4 + k
-            puts.append(pltpu.make_async_copy(res.at[rb * 4 + k], out.at[chip * 2 + (c ^ rel)], os.at[rb * 4 + k]))
+    for g in range(8):
+        term = acc[g * 128 : (g + 1) * 128, :] - jnp.dot(fit, rows_of(b2, g * 128, 128), preferred_element_type=F32)
+        res[g * 2 : (g + 1) * 2] = term.astype(BF16).reshape(2, OCC_DEV, HALF, NVIR)
+        for k in range(2):
+            rel, chip = g // 4, (g % 4) * 2 + k
+            puts.append(pltpu.make_async_copy(res.at[g * 2 + k], out.at[chip * 2 + (c ^ rel)], os.at[g * 2 + k]))
             puts[-1].start()
     for cp in puts:
         cp.wait()
@@ -160,9 +163,10 @@
             pltpu.VMEM(BLOCK, BF16),
             pltpu.VMEM((ROWS, ROWS), BF16),
             pltpu.VMEM((ROWS, NVIR), F32),
+            pltpu.VMEM((8, 128, 128), F32),
             pltpu.SemaphoreType.DMA((5,)),
             pltpu.SemaphoreType.DMA((2, 8)),
-            pltpu.SemaphoreType.DMA((4,)),
+            pltpu.SemaphoreType.DMA((8,)),
         ],
         cost_estimate=cost(2),
         compiler_params=pltpu.CompilerParams(vmem_limit_bytes=60 << 20),
@@ -181,6 +185,7 @@
             pltpu.VMEM(BLOCK, BF16),
             pltpu.VMEM((ROWS, ROWS), BF16),
             pltpu.VMEM((ROWS, NVIR), F32),
+            pltpu.VMEM((8, 128, 128), F32),
             pltpu.VMEM(BLOCK, BF16),
             pltpu.SemaphoreType.DMA((2,)),
             pltpu.SemaphoreType.DMA((8,)),

time: 144 us -> 141 us (0.979)
  Pallas kernels: 24.2 us -> 20.8 us
    pallas_call x1, Pallas kernels: 16.4 us -> 12.7 us  [early(): pl.pallas_call(early_kernel, out_shape=[jax.ShapeDtypeStruct((ROWS, NVIR)...]
  transfers between devices with their start and end apart: 11 -> 11, of which waited for: 7 -> 7; matrix products, arithmetic and copies ran while one was open for 3% -> 3% of each run, Pallas kernels for 11% -> 9%
where the time goes in v5:
time: 141 us; the launch traced here: 140 us
  waiting for transfers between devices  53.7 us (38%)
  blocking collectives  31.4 us (22%)
  starting transfers between devices  24.5 us (17%)
  Pallas kernels  20.8 us (15%)
  local copies, waits for them, and re-layouts  6.84 us (5%)
  other arithmetic  2.96 us (2%)
    all_to_all x3, waiting for transfers between devices, body(): own.append(lax.all_to_all(send, CHIPS, 0, 0, tiled=True))  32.5 us
    all_to_all x1, blocking collectives, body(): parts = lax.all_to_all(acc, MOST, 0, 0, tiled=True)  31.4 us
    pallas_call x1, Pallas kernels, early(): pl.pallas_call(early_kernel, out_shape=[jax.ShapeDtypeStruct((ROWS, NVIR)...  12.7 us
    all_to_all x3, starting transfers between devices, body(): own.append(lax.all_to_all(send, CHIPS, 0, 0, tiled=True))  12.5 us
    ppermute x3, waiting for transfers between devices, body(): x = x + [lax.ppermute(x[0], 'z', ring(4, s)) for s in (1, 2, 3)]  10.6 us
    all_to_all x1, waiting for transfers between devices, body(): every = lax.all_to_all(part, NARROW, 0, 0, tiled=True)  9.6 us
    pallas_call x1, Pallas kernels, late(): pl.pallas_call(late_kernel, out_shape=jax.ShapeDtypeStruct(BLOCK, BF16),...  8.17 us
    ppermute x3, starting transfers between devices, body(): x = x + [lax.ppermute(x[0], 'z', ring(4, s)) for s in (1, 2, 3)]  6.58 us
  transfers between devices with their start and end apart: 11, of which 7 were waited for; matrix products, arithmetic and copies ran while one was open for 3% of the time, Pallas kernels for 9%

profile of v5, /device:TPU:0, one launch (start us, length us, event | category | flops | bytes accessed | tf_op | source)
XLA Modules:
  0.0 140.4 jit_solution(12198362027886798305)
XLA Ops:
  0.0 0.0 copy-start
  0.0 2.2 %slice_bitcast_fusion.1 = bf16[8,16,3072]{2,1,0:T(8,128)(2,1)} fusion(bf16[3,8,16,3072]{3,2,1,0:T(8,128)(2,1)} %bitcast.18), kind=kLoop, calls=%fused_computation.2 | loop fusion | bytes 1572864 | tf_op jit(solution)/shard_map/squeeze | solution.py:216
  2.2 5.4 %all-to-all-start.1 = ((bf16[8,16,3072]{2,1,0:T(8,128)(2,1)}), bf16[8,16,3072]{2,1,0:T(8,128)(2,1)S(1)}, u32[]{:S(2)}, u32[]{:S(2)}) async-start(bf16[8,16,3072]{2,1,0:T(8,128)(2,1)} %slice_bitcast_fusion.1), calls=%async_computation.1 | async-start | bytes 1572864 | tf_op jit(solution)/shard_map/all_to_all | solution.py:219
  7.6 0.8 constant_dynamic-slice_fusion
  8.4 0.0 copy-done
  8.4 0.1 slice.16
  8.5 1.1 pad_maximum_fusion
  9.6 10.4 %all-to-all-done.1.own1 = bf16[8,16,3072]{2,1,0:T(8,128)(2,1)S(1)} async-done(((bf16[8,16,3072]{2,1,0:T(8,128)(2,1)}), bf16[8,16,3072]{2,1,0:T(8,128)(2,1)S(1)}, u32[]{:S(2)}, u32[]{:S(2)}) %all-to-all-start.1) | async-done | bytes 786464 | tf_op jit(solution)/shard_map/all_to_all | solution.py:219
  20.0 0.0 copy-start.2
  20.0 0.9 copy-done.2
  20.9 3.6 %all-to-all-start = ((bf16[8,16,4608]{2,1,0:T(8,128)(2,1)}), bf16[8,16,4608]{2,1,0:T(8,128)(2,1)S(1)}, u32[]{:S(2)}, u32[]{:S(2)}) async-start(bf16[8,16,4608]{2,1,0:T(8,128)(2,1)} %pad_maximum_fusion), calls=%async_computation | async-start | bytes 2359296 | tf_op jit(solution)/shard_map/all_to_all | solution.py:219
  24.5 0.1 collective-permute-start.5
  24.6 16.4 %all-to-all-done.own0 = bf16[8,16,4608]{2,1,0:T(8,128)(2,1)S(1)} async-done(((bf16[8,16,4608]{2,1,0:T(8,128)(2,1)}), bf16[8,16,4608]{2,1,0:T(8,128)(2,1)S(1)}, u32[]{:S(2)}, u32[]{:S(2)}) %all-to-all-start) | async-done | bytes 1179680 | tf_op jit(solution)/shard_map/all_to_all | solution.py:219
  41.0 0.0 copy-start.1
  41.0 0.0 collective-permute-start.4
  41.0 1.0 slice_bitcast_fusion
  42.0 3.5 %all-to-all-start.2 = ((bf16[8,16,3072]{2,1,0:T(8,128)(2,1)}), bf16[8,16,3072]{2,1,0:T(8,128)(2,1)S(1)}, u32[]{:S(2)}, u32[]{:S(2)}) async-start(bf16[8,16,3072]{2,1,0:T(8,128)(2,1)} %slice_bitcast_fusion), calls=%async_computation.2 | async-start | bytes 1572864 | tf_op jit(solution)/shard_map/all_to_all | solution.py:219
  45.6 0.0 copy-done.1
  45.7 0.5 collective-permute-start
  46.2 1.1 collective-permute-done
  47.3 0.0 copy-start.4
  47.3 2.0 %collective-permute-start.1 = (bf16[16,16,768]{2,1,0:T(8,128)(2,1)S(1)}, bf16[16,16,768]{2,1,0:T(8,128)(2,1)S(1)}, u32[]{:S(2)}, u32[]{:S(2)}) collective-permute-start(bf16[16,16,768]{2,1,0:T(8,128)(2,1)S(1)} %pad_maximum_fusion.1.x_a), channel_id=1, source_target_pairs={{0,1},{1,2},{2,3},{3,0},{4,5},{5,6},{6,7},{7,4},{8,9},{9,10},{10,1... | collective-permute-start | bytes 1179656 | tf_op jit(solution)/shard_map/ppermute | solution.py:225
  49.3 3.6 %collective-permute-start.2 = (bf16[16,16,768]{2,1,0:T(8,128)(2,1)S(1)}, bf16[16,16,768]{2,1,0:T(8,128)(2,1)}, u32[]{:S(2)}, u32[]{:S(2)}) collective-permute-start(bf16[16,16,768]{2,1,0:T(8,128)(2,1)S(1)} %pad_maximum_fusion.1.x_a), channel_id=1, source_target_pairs={{0,2},{1,3},{2,0},{3,1},{4,6},{5,7},{6,4},{7,5},{8,10},{9,11},{10,... | collective-permute-start | bytes 1179656 | tf_op jit(solution)/shard_map/ppermute | solution.py:225
  52.9 1.0 collective-permute-start.3
  53.9 5.6 %all-to-all-done.2.own = bf16[8,16,3072]{2,1,0:T(8,128)(2,1)S(1)} async-done(((bf16[8,16,3072]{2,1,0:T(8,128)(2,1)}), bf16[8,16,3072]{2,1,0:T(8,128)(2,1)S(1)}, u32[]{:S(2)}, u32[]{:S(2)}) %all-to-all-start.2) | async-done | bytes 786464 | tf_op jit(solution)/shard_map/all_to_all | solution.py:219
  59.5 0.0 copy-start.3
  59.5 0.0 collective-permute-done.5.other1
  59.5 0.0 collective-permute-start.6
  59.5 0.6 pad_add_fusion.where
  60.2 0.9 collective-permute-done.1.x_b
  61.0 0.0 copy-start.8
  61.1 9.7 %collective-permute-done.2.x_c = bf16[16,16,768]{2,1,0:T(8,128)(2,1)} collective-permute-done((bf16[16,16,768]{2,1,0:T(8,128)(2,1)S(1)}, bf16[16,16,768]{2,1,0:T(8,128)(2,1)}, u32[]{:S(2)}, u32[]{:S(2)}) %collective-permute-start.2) | collective-permute-done | bytes 393248 | tf_op jit(solution)/shard_map/ppermute | solution.py:225
  70.8 0.0 collective-permute-done.3.x_d
  70.8 0.0 collective-permute-done.4.other0
  70.8 0.0 copy-done.4
  70.8 0.0 copy-done.8
  70.8 12.7 %terms_early.1 = (f32[1024,768]{1,0:T(8,128)}, bf16[16,4,16,768]{3,2,1,0:T(8,128)(2,1)}) custom-call(s32[2]{0:T(128)} %pad_add_fusion.where, bf16[16,16,768]{2,1,0:T(8,128)(2,1)} %copy-done.4, bf16[16,16,768]{2,1,0:T(8,128)(2,1)} %copy-done.8, bf16[16,16,768]{2,1,0:T(8,128)(2,1)} %collective-permute-done.2.x_c, ...), custom_call_target="tpu_custom_call" | custom-call | flops 6442450944 | bytes 6291456 | tf_op jit(solution)/shard_map/terms_early/pallas_call | solution.py:155
  83.4 0.0 copy-done.3
  83.5 0.0 collective-permute-done.6.other
  83.5 0.0 copy-start.7
  83.5 0.9 copy-done.7
  84.4 8.2 %terms_late.1 = bf16[16,4,16,768]{3,2,1,0:T(8,128)(2,1)} custom-call(s32[2]{0:T(128)} %pad_add_fusion.where, bf16[16,4,16,768]{3,2,1,0:T(8,128)(2,1)} %get-tuple-element.7.x_in, bf16[8,16,3072]{2,1,0:T(8,128)(2,1)} %copy-done.3, bf16[8,16,3072]{2,1,0:T(8,128)(2,1)} %copy-done.7, f32[1024,768]{1,0:T(8,128)} %get-tuple-element.8.acc_in), custom_call_target="tpu_custom_call" | custom-call | flops 3221225472 | bytes 6291456 | tf_op jit(solution)/shard_map/terms_late/pallas_call | solution.py:178
  92.5 31.4 %all_to_all.25 = bf16[64,16,768]{2,1,0:T(8,128)(2,1)S(1)} all-to-all(bf16[64,16,768]{2,1,0:T(8,128)(2,1)} %bitcast.20), channel_id=1, replica_groups=mesh['x'=4,'yl'=2,'c'=2,'yh'=2,'z'=4] {'x','yl','c','z'}, dimensions={0} | all-to-all | bytes 3145728 | tf_op jit(solution)/shard_map/all_to_all | solution.py:228
  123.9 0.0 copy-start.9
  123.9 0.0 copy-start.6
  123.9 0.2 reduce_sum.21
  124.1 0.0 copy-start.5
  124.2 0.8 broadcast_in_dim.8
  124.9 4.8 %all-to-all-start.4 = ((bf16[8,32,768]{2,1,0:T(8,128)(2,1)}), bf16[8,32,768]{2,1,0:T(8,128)(2,1)S(1)}, u32[]{:S(2)}, u32[]{:S(2)}) async-start(bf16[8,32,768]{2,1,0:T(8,128)(2,1)} %broadcast_in_dim.8), calls=%async_computation.4 | async-start | bytes 786432 | tf_op jit(solution)/shard_map/all_to_all | solution.py:231
  129.7 0.0 copy-done.9
  129.7 0.1 dynamic_slice.12
  129.8 0.0 copy-done.6
  129.8 0.1 broadcast_subtract_fusion
  129.9 9.6 %all-to-all-done.4 = bf16[8,32,768]{2,1,0:T(8,128)(2,1)S(1)} async-done(((bf16[8,32,768]{2,1,0:T(8,128)(2,1)}), bf16[8,32,768]{2,1,0:T(8,128)(2,1)S(1)}, u32[]{:S(2)}, u32[]{:S(2)}) %all-to-all-start.4) | async-done | bytes 393248 | tf_op jit(solution)/shard_map/all_to_all | solution.py:231
  139.5 0.1 convert_reduce_fusion
  139.6 0.0 copy-done.5
  139.6 0.8 multiply_subtract_fusion
  (6 shorter events, 0.1 us)
Async XLA Ops:
  0.0 8.4 %copy-start = (bf16[384,3072]{1,0:T(8,128)(2,1)S(1)}, bf16[384,3072]{1,0:T(8,128)(2,1)}, u32[]{:S(2)}) copy-start(bf16[384,3072]{1,0:T(8,128)(2,1)} %param.4) | copy-start | bytes 7077892
  2.2 17.8 %all-to-all-start.1 = ((bf16[8,16,3072]{2,1,0:T(8,128)(2,1)}), bf16[8,16,3072]{2,1,0:T(8,128)(2,1)S(1)}, u32[]{:S(2)}, u32[]{:S(2)}) async-start(bf16[8,16,3072]{2,1,0:T(8,128)(2,1)} %slice_bitcast_fusion.1), calls=%async_computation.1 | async-start | bytes 1572864 | tf_op jit(solution)/shard_map/all_to_all | solution.py:219
  20.0 0.9 copy-start.2
  20.9 20.1 %all-to-all-start = ((bf16[8,16,4608]{2,1,0:T(8,128)(2,1)}), bf16[8,16,4608]{2,1,0:T(8,128)(2,1)S(1)}, u32[]{:S(2)}, u32[]{:S(2)}) async-start(bf16[8,16,4608]{2,1,0:T(8,128)(2,1)} %pad_maximum_fusion), calls=%async_computation | async-start | bytes 2359296 | tf_op jit(solution)/shard_map/all_to_all | solution.py:219
  24.5 35.1 %collective-permute-start.5 = (bf16[8,16,3072]{2,1,0:T(8,128)(2,1)}, bf16[8,16,3072]{2,1,0:T(8,128)(2,1)}, u32[]{:S(2)}, u32[]{:S(2)}) collective-permute-start(bf16[8,16,3072]{2,1,0:T(8,128)(2,1)} %copy-done.2), channel_id=1, source_target_pairs={{0,8},{8,0},{1,9},{9,1},{2,10},{10,2},{3,11},{11,3},{4,12},{12,4},... | collective-permute-start | bytes 2359304 | tf_op jit(solution)/shard_map/ppermute | solution.py:220
  41.0 4.6 %copy-start.1 = (bf16[8,16,4608]{2,1,0:T(8,128)(2,1)}, bf16[8,16,4608]{2,1,0:T(8,128)(2,1)S(1)}, u32[]{:S(2)}) copy-start(bf16[8,16,4608]{2,1,0:T(8,128)(2,1)S(1)} %all-to-all-done.own0) | copy-start | bytes 3538948
  41.0 29.8 %collective-permute-start.4 = (bf16[8,16,4608]{2,1,0:T(8,128)(2,1)S(1)}, bf16[8,16,4608]{2,1,0:T(8,128)(2,1)}, u32[]{:S(2)}, u32[]{:S(2)}) collective-permute-start(bf16[8,16,4608]{2,1,0:T(8,128)(2,1)S(1)} %all-to-all-done.own0), channel_id=1, source_target_pairs={{0,8},{8,0},{1,9},{9,1},{2,10},{10,2},{3,11},{11,3},{4,12},{12,4},... | collective-permute-start | bytes 3538952 | tf_op jit(solution)/shard_map/ppermute | solution.py:220
  42.0 17.5 %all-to-all-start.2 = ((bf16[8,16,3072]{2,1,0:T(8,128)(2,1)}), bf16[8,16,3072]{2,1,0:T(8,128)(2,1)S(1)}, u32[]{:S(2)}, u32[]{:S(2)}) async-start(bf16[8,16,3072]{2,1,0:T(8,128)(2,1)} %slice_bitcast_fusion), calls=%async_computation.2 | async-start | bytes 1572864 | tf_op jit(solution)/shard_map/all_to_all | solution.py:219
  45.7 1.6 %collective-permute-start = (bf16[8,16,768]{2,1,0:T(8,128)(2,1)S(1)}, bf16[8,16,768]{2,1,0:T(8,128)(2,1)S(1)}, u32[]{:S(2)}, u32[]{:S(2)}) collective-permute-start(bf16[8,16,768]{2,1,0:T(8,128)(2,1)S(1)} %get-tuple-element.10), channel_id=1, source_target_pairs={{0,8},{8,0},{1,9},{9,1},{2,10},{10,2},{3,11},{11,3},{4,12},{12,4},... | collective-permute-start | bytes 589832 | tf_op jit(solution)/shard_map/ppermute | solution.py:223
  47.3 23.5 %copy-start.4 = (bf16[16,16,768]{2,1,0:T(8,128)(2,1)}, bf16[16,16,768]{2,1,0:T(8,128)(2,1)S(1)}, u32[]{:S(2)}) copy-start(bf16[16,16,768]{2,1,0:T(8,128)(2,1)S(1)} %pad_maximum_fusion.1.x_a) | copy-start | bytes 1179652
  47.3 13.8 %collective-permute-start.1 = (bf16[16,16,768]{2,1,0:T(8,128)(2,1)S(1)}, bf16[16,16,768]{2,1,0:T(8,128)(2,1)S(1)}, u32[]{:S(2)}, u32[]{:S(2)}) collective-permute-start(bf16[16,16,768]{2,1,0:T(8,128)(2,1)S(1)} %pad_maximum_fusion.1.x_a), channel_id=1, source_target_pairs={{0,1},{1,2},{2,3},{3,0},{4,5},{5,6},{6,7},{7,4},{8,9},{9,10},{10,1... | collective-permute-start | bytes 1179656 | tf_op jit(solution)/shard_map/ppermute | solution.py:225
  49.3 21.5 %collective-permute-start.2 = (bf16[16,16,768]{2,1,0:T(8,128)(2,1)S(1)}, bf16[16,16,768]{2,1,0:T(8,128)(2,1)}, u32[]{:S(2)}, u32[]{:S(2)}) collective-permute-start(bf16[16,16,768]{2,1,0:T(8,128)(2,1)S(1)} %pad_maximum_fusion.1.x_a), channel_id=1, source_target_pairs={{0,2},{1,3},{2,0},{3,1},{4,6},{5,7},{6,4},{7,5},{8,10},{9,11},{10,... | collective-permute-start | bytes 1179656 | tf_op jit(solution)/shard_map/ppermute | solution.py:225
  52.9 17.9 %collective-permute-start.3 = (bf16[16,16,768]{2,1,0:T(8,128)(2,1)S(1)}, bf16[16,16,768]{2,1,0:T(8,128)(2,1)}, u32[]{:S(2)}, u32[]{:S(2)}) collective-permute-start(bf16[16,16,768]{2,1,0:T(8,128)(2,1)S(1)} %pad_maximum_fusion.1.x_a), channel_id=1, source_target_pairs={{0,3},{1,0},{2,1},{3,2},{4,7},{5,4},{6,5},{7,6},{8,11},{9,8},{10,9... | collective-permute-start | bytes 1179656 | tf_op jit(solution)/shard_map/ppermute | solution.py:225
  59.5 23.9 %copy-start.3 = (bf16[8,16,3072]{2,1,0:T(8,128)(2,1)}, bf16[8,16,3072]{2,1,0:T(8,128)(2,1)S(1)}, u32[]{:S(2)}) copy-start(bf16[8,16,3072]{2,1,0:T(8,128)(2,1)S(1)} %all-to-all-done.2.own) | copy-start | bytes 2359300
  59.5 23.9 %collective-permute-start.6 = (bf16[8,16,3072]{2,1,0:T(8,128)(2,1)S(1)}, bf16[8,16,3072]{2,1,0:T(8,128)(2,1)S(1)}, u32[]{:S(2)}, u32[]{:S(2)}) collective-permute-start(bf16[8,16,3072]{2,1,0:T(8,128)(2,1)S(1)} %all-to-all-done.2.own), channel_id=1, source_target_pairs={{0,8},{8,0},{1,9},{9,1},{2,10},{10,2},{3,11},{11,3},{4,12},{12,4},... | collective-permute-start | bytes 2359304 | tf_op jit(solution)/shard_map/ppermute | solution.py:220
  61.0 9.7 %copy-start.8 = (bf16[16,16,768]{2,1,0:T(8,128)(2,1)}, bf16[16,16,768]{2,1,0:T(8,128)(2,1)S(1)}, u32[]{:S(2)}) copy-start(bf16[16,16,768]{2,1,0:T(8,128)(2,1)S(1)} %collective-permute-done.1.x_b) | copy-start | bytes 1179652
  83.5 0.9 copy-start.7
  123.9 5.8 %copy-start.9 = (f32[64]{0:T(128)S(1)}, f32[64]{0:T(128)}, u32[]{:S(2)}) copy-start(f32[64]{0:T(128)} %param.6) | copy-start | bytes 772
  123.9 5.9 %copy-start.6 = (f32[768]{0:T(1024)S(1)}, f32[768]{0:T(1024)}, u32[]{:S(2)}) copy-start(f32[768]{0:T(1024)} %param.7) | copy-start | bytes 9220
  124.1 15.4 %copy-start.5 = (bf16[32,3072]{1,0:T(8,128)(2,1)S(1)}, bf16[32,3072]{1,0:T(8,128)(2,1)}, u32[]{:S(2)}) copy-start(bf16[32,3072]{1,0:T(8,128)(2,1)} %param.5) | copy-start | bytes 589828
  124.9 14.6 %all-to-all-start.4 = ((bf16[8,32,768]{2,1,0:T(8,128)(2,1)}), bf16[8,32,768]{2,1,0:T(8,128)(2,1)S(1)}, u32[]{:S(2)}, u32[]{:S(2)}) async-start(bf16[8,32,768]{2,1,0:T(8,128)(2,1)} %broadcast_in_dim.8), calls=%async_computation.4 | async-start | bytes 786432 | tf_op jit(solution)/shard_map/all_to_all | solution.py:231

commit v6 on v5

--- a/solution.py
+++ b/solution.py
@@ -55,13 +55,15 @@
     return ref[start // 64 : (start + count) // 64].reshape(count, NVIR)
 
 
-def contract_first(x2, b2, d, diag, copies):
+def contract_first(x2, b2, d, diag, gets, copies):
     for g in range(4):
         if g % 2 == 0:
             for cp in copies[g * 2 : g * 2 + 4]:
                 cp.wait()
         rhs = rows_of(b2, g * 256, 256)
         for rb in range(4):
+            if g == 0 and gets:
+                gets[rb].wait()
             lhs = rows_of(x2, rb * 256, 256)
             inter = lax.dot_general(lhs, rhs, (((1,), (1,)), ((), ())), preferred_element_type=F32)
             for a in range(2):
@@ -106,7 +108,7 @@
     keep_x.start()
     puts = []
     for t, (b2, copies) in enumerate(((b_a, rows0), (b_b, rows1))):
-        fit = contract_first(x2, b2, d, diag, copies)
+        fit = contract_first(x2, b2, d, diag, [], copies)
         contract_second(b2, d, acc, t == 0)
         for g in range(8):
             rows = slice(g * 128, (g + 1) * 128)
@@ -119,29 +121,31 @@
         cp.wait()
 
 
-def late_kernel(where, x_in, own, other, acc_in, out, x2, b2, d, acc, diag, res, xs, bs, os):
+def late_kernel(where, x_in, own, other, acc_in, out, x2, b2, d, acc, diag, xs, os):
     c = where[0]
-    get_x = pltpu.make_async_copy(x_in, x2, xs.at[0])
-    get_x.start()
-    copies = fetch_rows(b2, own, other, bs)
-    get_acc = pltpu.make_async_copy(acc_in, acc, xs.at[1])
+    gets = []
+    for k in range(4):
+        gets.append(pltpu.make_async_copy(x_in.at[pl.ds(k * 4, 4)], x2.at[pl.ds(k * 4, 4)], xs.at[k]))
+        gets[-1].start()
+    get_acc = pltpu.make_async_copy(acc_in, acc, os.at[0])
     get_acc.start()
-    get_x.wait()
-    fit = contract_first(x2, b2, d, diag, copies)
+    for rel, src in enumerate((own, other)):
+        for chip in range(NCHIP):
+            for q in range(OCC_DEV):
+                b2[rel * NCHIP + chip, q] = src[chip, :, q * NVIR : (q + 1) * NVIR]
+    fit = contract_first(x2, b2, d, diag, gets, [])
     get_acc.wait()
     contract_second(b2, d, acc, False)
-    puts = []
     for g in range(8):
         term = acc[g * 128 : (g + 1) * 128, :] - jnp.dot(fit, rows_of(b2, g * 128, 128), preferred_element_type=F32)
-        res[g * 2 : (g + 1) * 2] = term.astype(BF16).reshape(2, OCC_DEV, HALF, NVIR)
+        term = term.astype(BF16).reshape(2, OCC_DEV, HALF, NVIR)
         for k in range(2):
             rel, chip = g // 4, (g % 4) * 2 + k
-            puts.append(pltpu.make_async_copy(res.at[g * 2 + k], out.at[chip * 2 + (c ^ rel)], os.at[g * 2 + k]))
-            puts[-1].start()
-    for cp in puts:
-        cp.wait()
-
-
+            out[chip * 2 + (c ^ rel)] = term[k]
+
+
+VMEM = pl.BlockSpec(memory_space=pltpu.VMEM)
+LATE_MIB = 50
 SMEM = pl.BlockSpec(memory_space=pltpu.SMEM)
 ANY = pl.BlockSpec(memory_space=pl.ANY)
 BLOCK = (16, OCC_DEV, HALF, NVIR)
@@ -178,21 +182,19 @@
     return pl.pallas_call(
         late_kernel,
         out_shape=jax.ShapeDtypeStruct(BLOCK, BF16),
-        in_specs=[SMEM] + [ANY] * 4,
-        out_specs=ANY,
+        in_specs=[SMEM, ANY, VMEM, VMEM, ANY],
+        out_specs=VMEM,
         scratch_shapes=[
             pltpu.VMEM(BLOCK, BF16),
             pltpu.VMEM(BLOCK, BF16),
             pltpu.VMEM((ROWS, ROWS), BF16),
             pltpu.VMEM((ROWS, NVIR), F32),
             pltpu.VMEM((8, 128, 128), F32),
-            pltpu.VMEM(BLOCK, BF16),
-            pltpu.SemaphoreType.DMA((2,)),
-            pltpu.SemaphoreType.DMA((8,)),
-            pltpu.SemaphoreType.DMA((16,)),
+            pltpu.SemaphoreType.DMA((4,)),
+            pltpu.SemaphoreType.DMA((1,)),
         ],
         cost_estimate=cost(1),
-        compiler_params=pltpu.CompilerParams(vmem_limit_bytes=60 << 20),
+        compiler_params=pltpu.CompilerParams(vmem_limit_bytes=LATE_MIB << 20),
         name="terms_late",
     )(where, x2, own[2], other[2], acc).reshape(16 * OCC_DEV, HALF, NVIR)
 
@@ -203,7 +205,7 @@
 
 def body(fit_rows, trials, occ_energy, vir_energy):
     core = lax.axis_index("c").astype(jnp.int32)
-    z = lax.axis_index("z").astype(jnp.int32)
+    z = (lax.axis_index("z") + 2 * lax.axis_index("yh")).astype(jnp.int32) & 3
     where = jnp.stack([core, z])
     blocks = [fit_rows.reshape(CHUNKS, NCHIP, HALF, PAIRS)]
     for _ in range(1, CHUNKS):
@@ -222,7 +224,8 @@
     x_send = lax.dynamic_slice_in_dim(own[0], PAIRS + (1 - core) * NVIR, NVIR, 2)
     x_other = lax.ppermute(x_send, "c", ring(2, 1))
     x = [jnp.concatenate([x_own, x_other])]
-    x = x + [lax.ppermute(x[0], "z", ring(4, s)) for s in (1, 2, 3)]
+    steps = (("z", ring(4, 1)), ("yh", ring(2, 1)), ("z", ring(4, 3)))
+    x = x + [lax.ppermute(x[0], axis, perm) for axis, perm in steps]
     acc, x2 = early(where, x, own, other)
     acc = late(where, x2, own, other, acc)
     parts = lax.all_to_all(acc, MOST, 0, 0, tiled=True)

time: 141 us -> 136 us (0.965)
  waiting for transfers between devices: 53.7 us -> 49.3 us
    ppermute x3, waiting for transfers between devices: 10.6 us -> 6.75 us  [body(): x = x + [lax.ppermute(x[0], axis, perm) for axis, perm in steps]]
where the time goes in v6:
time: 136 us; the launch traced here: 135 us
  waiting for transfers between devices  49.3 us (36%)
  blocking collectives  32.4 us (24%)
  starting transfers between devices  24 us (18%)
  Pallas kernels  20.5 us (15%)
  local copies, waits for them, and re-layouts  5.94 us (4%)
  other arithmetic  2.99 us (2%)
    all_to_all x1, blocking collectives, body(): parts = lax.all_to_all(acc, MOST, 0, 0, tiled=True)  32.4 us
    all_to_all x3, waiting for transfers between devices, body(): own.append(lax.all_to_all(send, CHIPS, 0, 0, tiled=True))  31.9 us
    pallas_call x1, Pallas kernels, early(): pl.pallas_call(early_kernel, out_shape=[jax.ShapeDtypeStruct((ROWS, NVIR)...  12.7 us
    all_to_all x3, starting transfers between devices, body(): own.append(lax.all_to_all(send, CHIPS, 0, 0, tiled=True))  12.5 us
    all_to_all x1, waiting for transfers between devices, body(): every = lax.all_to_all(part, NARROW, 0, 0, tiled=True)  9.6 us
    pallas_call x1, Pallas kernels, late(): pl.pallas_call(late_kernel, out_shape=jax.ShapeDtypeStruct(BLOCK, BF16),...  7.86 us
    ppermute x3, starting transfers between devices, body(): x = x + [lax.ppermute(x[0], axis, perm) for axis, perm in steps]  7.1 us
    ppermute x3, waiting for transfers between devices, body(): x = x + [lax.ppermute(x[0], axis, perm) for axis, perm in steps]  6.75 us
  transfers between devices with their start and end apart: 11, of which 7 were waited for; matrix products, arithmetic and copies ran while one was open for 3% of the time, Pallas kernels for 9%

profile of v6, /device:TPU:0, one launch (start us, length us, event | category | flops | bytes accessed | tf_op | source)
XLA Modules:
  0.0 135.3 jit_solution(9458124849497328346)
XLA Ops:
  0.0 0.0 copy-start.1
  0.0 2.2 %slice_bitcast_fusion.1 = bf16[8,16,3072]{2,1,0:T(8,128)(2,1)} fusion(bf16[3,8,16,3072]{3,2,1,0:T(8,128)(2,1)} %bitcast.19), kind=kLoop, calls=%fused_computation.2 | loop fusion | bytes 1572864 | tf_op jit(solution)/shard_map/squeeze | solution.py:218
  2.2 5.4 %all-to-all-start.1 = ((bf16[8,16,3072]{2,1,0:T(8,128)(2,1)}), bf16[8,16,3072]{2,1,0:T(8,128)(2,1)S(1)}, u32[]{:S(2)}, u32[]{:S(2)}) async-start(bf16[8,16,3072]{2,1,0:T(8,128)(2,1)} %slice_bitcast_fusion.1), calls=%async_computation.1 | async-start | bytes 1572864 | tf_op jit(solution)/shard_map/all_to_all | solution.py:221
  7.6 0.8 constant_dynamic-slice_fusion
  8.4 0.0 copy-done.1
  8.4 0.1 slice.16
  8.5 1.1 pad_maximum_fusion
  9.6 10.4 %all-to-all-done.1.own1 = bf16[8,16,3072]{2,1,0:T(8,128)(2,1)S(1)} async-done(((bf16[8,16,3072]{2,1,0:T(8,128)(2,1)}), bf16[8,16,3072]{2,1,0:T(8,128)(2,1)S(1)}, u32[]{:S(2)}, u32[]{:S(2)}) %all-to-all-start.1) | async-done | bytes 786464 | tf_op jit(solution)/shard_map/all_to_all | solution.py:221
  20.0 0.0 copy-start.3
  20.0 0.9 copy-done.3
  20.9 3.6 %all-to-all-start = ((bf16[8,16,4608]{2,1,0:T(8,128)(2,1)}), bf16[8,16,4608]{2,1,0:T(8,128)(2,1)S(1)}, u32[]{:S(2)}, u32[]{:S(2)}) async-start(bf16[8,16,4608]{2,1,0:T(8,128)(2,1)} %pad_maximum_fusion), calls=%async_computation | async-start | bytes 2359296 | tf_op jit(solution)/shard_map/all_to_all | solution.py:221
  24.5 0.1 collective-permute-start.5
  24.6 16.4 %all-to-all-done.own0 = bf16[8,16,4608]{2,1,0:T(8,128)(2,1)S(1)} async-done(((bf16[8,16,4608]{2,1,0:T(8,128)(2,1)}), bf16[8,16,4608]{2,1,0:T(8,128)(2,1)S(1)}, u32[]{:S(2)}, u32[]{:S(2)}) %all-to-all-start) | async-done | bytes 1179680 | tf_op jit(solution)/shard_map/all_to_all | solution.py:221
  41.0 0.0 copy-start.2
  41.0 0.0 collective-permute-start.4
  41.0 1.0 slice_bitcast_fusion
  42.0 3.5 %all-to-all-start.2 = ((bf16[8,16,3072]{2,1,0:T(8,128)(2,1)}), bf16[8,16,3072]{2,1,0:T(8,128)(2,1)S(1)}, u32[]{:S(2)}, u32[]{:S(2)}) async-start(bf16[8,16,3072]{2,1,0:T(8,128)(2,1)} %slice_bitcast_fusion), calls=%async_computation.2 | async-start | bytes 1572864 | tf_op jit(solution)/shard_map/all_to_all | solution.py:221
  45.6 0.0 copy-done.2
  45.7 0.5 collective-permute-start
  46.2 1.1 collective-permute-done
  47.3 0.0 copy-start.4
  47.3 2.0 %collective-permute-start.1 = (bf16[16,16,768]{2,1,0:T(8,128)(2,1)S(1)}, bf16[16,16,768]{2,1,0:T(8,128)(2,1)S(1)}, u32[]{:S(2)}, u32[]{:S(2)}) collective-permute-start(bf16[16,16,768]{2,1,0:T(8,128)(2,1)S(1)} %pad_maximum_fusion.1.x_a), channel_id=1, source_target_pairs={{0,1},{1,2},{2,3},{3,0},{4,5},{5,6},{6,7},{7,4},{8,9},{9,10},{10,1... | collective-permute-start | bytes 1179656 | tf_op jit(solution)/shard_map/ppermute | solution.py:228
  49.3 2.9 %collective-permute-start.2 = (bf16[16,16,768]{2,1,0:T(8,128)(2,1)S(1)}, bf16[16,16,768]{2,1,0:T(8,128)(2,1)}, u32[]{:S(2)}, u32[]{:S(2)}) collective-permute-start(bf16[16,16,768]{2,1,0:T(8,128)(2,1)S(1)} %pad_maximum_fusion.1.x_a), channel_id=1, source_target_pairs={{0,4},{4,0},{1,5},{5,1},{2,6},{6,2},{3,7},{7,3},{8,12},{12,8},{9,1... | collective-permute-start | bytes 1179656 | tf_op jit(solution)/shard_map/ppermute | solution.py:228
  52.2 2.2 %collective-permute-start.3 = (bf16[16,16,768]{2,1,0:T(8,128)(2,1)S(1)}, bf16[16,16,768]{2,1,0:T(8,128)(2,1)}, u32[]{:S(2)}, u32[]{:S(2)}) collective-permute-start(bf16[16,16,768]{2,1,0:T(8,128)(2,1)S(1)} %pad_maximum_fusion.1.x_a), channel_id=1, source_target_pairs={{0,3},{1,0},{2,1},{3,2},{4,7},{5,4},{6,5},{7,6},{8,11},{9,8},{10,9... | collective-permute-start | bytes 1179656 | tf_op jit(solution)/shard_map/ppermute | solution.py:228
  54.4 5.1 %all-to-all-done.2.own = bf16[8,16,3072]{2,1,0:T(8,128)(2,1)S(1)} async-done(((bf16[8,16,3072]{2,1,0:T(8,128)(2,1)}), bf16[8,16,3072]{2,1,0:T(8,128)(2,1)S(1)}, u32[]{:S(2)}, u32[]{:S(2)}) %all-to-all-start.2) | async-done | bytes 786464 | tf_op jit(solution)/shard_map/all_to_all | solution.py:221
  59.5 0.0 collective-permute-done.5.other1
  59.5 0.0 collective-permute-start.6
  59.5 0.7 pad_add_fusion.where
  60.2 0.0 copy-start
  60.2 0.9 collective-permute-done.1.x_b
  61.0 0.0 copy-start.7
  61.0 5.9 %collective-permute-done.2.x_c = bf16[16,16,768]{2,1,0:T(8,128)(2,1)} collective-permute-done((bf16[16,16,768]{2,1,0:T(8,128)(2,1)S(1)}, bf16[16,16,768]{2,1,0:T(8,128)(2,1)}, u32[]{:S(2)}, u32[]{:S(2)}) %collective-permute-start.2) | collective-permute-done | bytes 393248 | tf_op jit(solution)/shard_map/ppermute | solution.py:228
  66.9 0.0 collective-permute-done.3.x_d
  66.9 0.0 collective-permute-done.4.other0
  66.9 0.0 copy-done.4
  66.9 0.0 copy-done.7
  67.0 12.7 %terms_early.1 = (f32[1024,768]{1,0:T(8,128)}, bf16[16,4,16,768]{3,2,1,0:T(8,128)(2,1)}) custom-call(s32[2]{0:T(128)} %pad_add_fusion.where, bf16[16,16,768]{2,1,0:T(8,128)(2,1)} %copy-done.4, bf16[16,16,768]{2,1,0:T(8,128)(2,1)} %copy-done.7, bf16[16,16,768]{2,1,0:T(8,128)(2,1)} %collective-permute-done.2.x_c, ...), custom_call_target="tpu_custom_call" | custom-call | flops 6442450944 | bytes 6291456 | tf_op jit(solution)/shard_map/terms_early/pallas_call | solution.py:159
  79.6 0.0 collective-permute-done.6.other
  79.6 0.0 copy-done
  79.6 7.9 %terms_late.1 = bf16[16,4,16,768]{3,2,1,0:T(8,128)(2,1)S(1)} custom-call(s32[2]{0:T(128)S(1)} %copy-done, bf16[16,4,16,768]{3,2,1,0:T(8,128)(2,1)} %get-tuple-element.7.x_in, bf16[8,16,3072]{2,1,0:T(8,128)(2,1)S(1)} %all-to-all-done.2.own, bf16[8,16,3072]{2,1,0:T(8,128)(2,1)S(1)} %collective-permute-done.6.other, f32[1024,768]{1,0:T(8,128)} %get-tuple-element.8.acc_in), custom_call_target="tpu_custom_call" | custom-call | flops 3221225472 | bytes 6291456 | tf_op jit(solution)/shard_map/terms_late/pallas_call | solution.py:182
  87.5 32.4 %all_to_all.25 = bf16[64,16,768]{2,1,0:T(8,128)(2,1)S(1)} all-to-all(bf16[64,16,768]{2,1,0:T(8,128)(2,1)S(1)} %bitcast.16), channel_id=1, replica_groups=mesh['x'=4,'yl'=2,'c'=2,'yh'=2,'z'=4] {'x','yl','c','z'}, dimensions={0} | all-to-all | bytes 3145728 | tf_op jit(solution)/shard_map/all_to_all | solution.py:231
  119.9 0.0 copy-start.8
  119.9 0.0 copy-start.6
  119.9 0.2 reduce_sum.21
  120.1 0.0 copy-start.5
  120.1 0.8 broadcast_in_dim.8
  120.9 3.7 %all-to-all-start.4 = ((bf16[8,32,768]{2,1,0:T(8,128)(2,1)}), bf16[8,32,768]{2,1,0:T(8,128)(2,1)S(1)}, u32[]{:S(2)}, u32[]{:S(2)}) async-start(bf16[8,32,768]{2,1,0:T(8,128)(2,1)} %broadcast_in_dim.8), calls=%async_computation.4 | async-start | bytes 786432 | tf_op jit(solution)/shard_map/all_to_all | solution.py:234
  124.6 0.0 copy-done.8
  124.6 0.1 dynamic_slice.12
  124.7 0.0 copy-done.6
  124.7 0.1 broadcast_subtract_fusion
  124.8 9.6 %all-to-all-done.4 = bf16[8,32,768]{2,1,0:T(8,128)(2,1)S(1)} async-done(((bf16[8,32,768]{2,1,0:T(8,128)(2,1)}), bf16[8,32,768]{2,1,0:T(8,128)(2,1)S(1)}, u32[]{:S(2)}, u32[]{:S(2)}) %all-to-all-start.4) | async-done | bytes 393248 | tf_op jit(solution)/shard_map/all_to_all | solution.py:234
  134.4 0.1 convert_reduce_fusion
  134.5 0.0 copy-done.5
  134.5 0.8 multiply_subtract_fusion
  (6 shorter events, 0.1 us)
Async XLA Ops:
  0.0 8.4 %copy-start.1 = (bf16[384,3072]{1,0:T(8,128)(2,1)S(1)}, bf16[384,3072]{1,0:T(8,128)(2,1)}, u32[]{:S(2)}) copy-start(bf16[384,3072]{1,0:T(8,128)(2,1)} %param.4) | copy-start | bytes 7077892
  2.2 17.8 %all-to-all-start.1 = ((bf16[8,16,3072]{2,1,0:T(8,128)(2,1)}), bf16[8,16,3072]{2,1,0:T(8,128)(2,1)S(1)}, u32[]{:S(2)}, u32[]{:S(2)}) async-start(bf16[8,16,3072]{2,1,0:T(8,128)(2,1)} %slice_bitcast_fusion.1), calls=%async_computation.1 | async-start | bytes 1572864 | tf_op jit(solution)/shard_map/all_to_all | solution.py:221
  20.0 0.9 copy-start.3
  20.9 20.1 %all-to-all-start = ((bf16[8,16,4608]{2,1,0:T(8,128)(2,1)}), bf16[8,16,4608]{2,1,0:T(8,128)(2,1)S(1)}, u32[]{:S(2)}, u32[]{:S(2)}) async-start(bf16[8,16,4608]{2,1,0:T(8,128)(2,1)} %pad_maximum_fusion), calls=%async_computation | async-start | bytes 2359296 | tf_op jit(solution)/shard_map/all_to_all | solution.py:221
  24.5 35.0 %collective-permute-start.5 = (bf16[8,16,3072]{2,1,0:T(8,128)(2,1)}, bf16[8,16,3072]{2,1,0:T(8,128)(2,1)}, u32[]{:S(2)}, u32[]{:S(2)}) collective-permute-start(bf16[8,16,3072]{2,1,0:T(8,128)(2,1)} %copy-done.3), channel_id=1, source_target_pairs={{0,8},{8,0},{1,9},{9,1},{2,10},{10,2},{3,11},{11,3},{4,12},{12,4},... | collective-permute-start | bytes 2359304 | tf_op jit(solution)/shard_map/ppermute | solution.py:222
  41.0 4.6 %copy-start.2 = (bf16[8,16,4608]{2,1,0:T(8,128)(2,1)}, bf16[8,16,4608]{2,1,0:T(8,128)(2,1)S(1)}, u32[]{:S(2)}) copy-start(bf16[8,16,4608]{2,1,0:T(8,128)(2,1)S(1)} %all-to-all-done.own0) | copy-start | bytes 3538948
  41.0 25.9 %collective-permute-start.4 = (bf16[8,16,4608]{2,1,0:T(8,128)(2,1)S(1)}, bf16[8,16,4608]{2,1,0:T(8,128)(2,1)}, u32[]{:S(2)}, u32[]{:S(2)}) collective-permute-start(bf16[8,16,4608]{2,1,0:T(8,128)(2,1)S(1)} %all-to-all-done.own0), channel_id=1, source_target_pairs={{0,8},{8,0},{1,9},{9,1},{2,10},{10,2},{3,11},{11,3},{4,12},{12,4},... | collective-permute-start | bytes 3538952 | tf_op jit(solution)/shard_map/ppermute | solution.py:222
  42.0 17.5 %all-to-all-start.2 = ((bf16[8,16,3072]{2,1,0:T(8,128)(2,1)}), bf16[8,16,3072]{2,1,0:T(8,128)(2,1)S(1)}, u32[]{:S(2)}, u32[]{:S(2)}) async-start(bf16[8,16,3072]{2,1,0:T(8,128)(2,1)} %slice_bitcast_fusion), calls=%async_computation.2 | async-start | bytes 1572864 | tf_op jit(solution)/shard_map/all_to_all | solution.py:221
  45.7 1.6 %collective-permute-start = (bf16[8,16,768]{2,1,0:T(8,128)(2,1)S(1)}, bf16[8,16,768]{2,1,0:T(8,128)(2,1)S(1)}, u32[]{:S(2)}, u32[]{:S(2)}) collective-permute-start(bf16[8,16,768]{2,1,0:T(8,128)(2,1)S(1)} %get-tuple-element.10), channel_id=1, source_target_pairs={{0,8},{8,0},{1,9},{9,1},{2,10},{10,2},{3,11},{11,3},{4,12},{12,4},... | collective-permute-start | bytes 589832 | tf_op jit(solution)/shard_map/ppermute | solution.py:225
  47.3 19.7 %copy-start.4 = (bf16[16,16,768]{2,1,0:T(8,128)(2,1)}, bf16[16,16,768]{2,1,0:T(8,128)(2,1)S(1)}, u32[]{:S(2)}) copy-start(bf16[16,16,768]{2,1,0:T(8,128)(2,1)S(1)} %pad_maximum_fusion.1.x_a) | copy-start | bytes 1179652
  47.3 13.8 %collective-permute-start.1 = (bf16[16,16,768]{2,1,0:T(8,128)(2,1)S(1)}, bf16[16,16,768]{2,1,0:T(8,128)(2,1)S(1)}, u32[]{:S(2)}, u32[]{:S(2)}) collective-permute-start(bf16[16,16,768]{2,1,0:T(8,128)(2,1)S(1)} %pad_maximum_fusion.1.x_a), channel_id=1, source_target_pairs={{0,1},{1,2},{2,3},{3,0},{4,5},{5,6},{6,7},{7,4},{8,9},{9,10},{10,1... | collective-permute-start | bytes 1179656 | tf_op jit(solution)/shard_map/ppermute | solution.py:228
  49.3 17.7 %collective-permute-start.2 = (bf16[16,16,768]{2,1,0:T(8,128)(2,1)S(1)}, bf16[16,16,768]{2,1,0:T(8,128)(2,1)}, u32[]{:S(2)}, u32[]{:S(2)}) collective-permute-start(bf16[16,16,768]{2,1,0:T(8,128)(2,1)S(1)} %pad_maximum_fusion.1.x_a), channel_id=1, source_target_pairs={{0,4},{4,0},{1,5},{5,1},{2,6},{6,2},{3,7},{7,3},{8,12},{12,8},{9,1... | collective-permute-start | bytes 1179656 | tf_op jit(solution)/shard_map/ppermute | solution.py:228
  52.2 14.8 %collective-permute-start.3 = (bf16[16,16,768]{2,1,0:T(8,128)(2,1)S(1)}, bf16[16,16,768]{2,1,0:T(8,128)(2,1)}, u32[]{:S(2)}, u32[]{:S(2)}) collective-permute-start(bf16[16,16,768]{2,1,0:T(8,128)(2,1)S(1)} %pad_maximum_fusion.1.x_a), channel_id=1, source_target_pairs={{0,3},{1,0},{2,1},{3,2},{4,7},{5,4},{6,5},{7,6},{8,11},{9,8},{10,9... | collective-permute-start | bytes 1179656 | tf_op jit(solution)/shard_map/ppermute | solution.py:228
  59.5 20.1 %collective-permute-start.6 = (bf16[8,16,3072]{2,1,0:T(8,128)(2,1)S(1)}, bf16[8,16,3072]{2,1,0:T(8,128)(2,1)S(1)}, u32[]{:S(2)}, u32[]{:S(2)}) collective-permute-start(bf16[8,16,3072]{2,1,0:T(8,128)(2,1)S(1)} %all-to-all-done.2.own), channel_id=1, source_target_pairs={{0,8},{8,0},{1,9},{9,1},{2,10},{10,2},{3,11},{11,3},{4,12},{12,4},... | collective-permute-start | bytes 2359304 | tf_op jit(solution)/shard_map/ppermute | solution.py:222
  60.2 19.5 %copy-start = (s32[2]{0:T(128)S(1)}, s32[2]{0:T(128)}, u32[]{:S(2)}) copy-start(s32[2]{0:T(128)} %pad_add_fusion.where) | copy-start | bytes 28
  61.0 5.9 %copy-start.7 = (bf16[16,16,768]{2,1,0:T(8,128)(2,1)}, bf16[16,16,768]{2,1,0:T(8,128)(2,1)S(1)}, u32[]{:S(2)}) copy-start(bf16[16,16,768]{2,1,0:T(8,128)(2,1)S(1)} %collective-permute-done.1.x_b) | copy-start | bytes 1179652
  119.9 4.8 %copy-start.8 = (f32[64]{0:T(128)S(1)}, f32[64]{0:T(128)}, u32[]{:S(2)}) copy-start(f32[64]{0:T(128)} %param.6) | copy-start | bytes 772
  119.9 4.8 %copy-start.6 = (f32[768]{0:T(1024)S(1)}, f32[768]{0:T(1024)}, u32[]{:S(2)}) copy-start(f32[768]{0:T(1024)} %param.7) | copy-start | bytes 9220
  120.1 14.4 %copy-start.5 = (bf16[32,3072]{1,0:T(8,128)(2,1)S(1)}, bf16[32,3072]{1,0:T(8,128)(2,1)}, u32[]{:S(2)}) copy-start(bf16[32,3072]{1,0:T(8,128)(2,1)} %param.5) | copy-start | bytes 589828
  120.9 13.5 %all-to-all-start.4 = ((bf16[8,32,768]{2,1,0:T(8,128)(2,1)}), bf16[8,32,768]{2,1,0:T(8,128)(2,1)S(1)}, u32[]{:S(2)}, u32[]{:S(2)}) async-start(bf16[8,32,768]{2,1,0:T(8,128)(2,1)} %broadcast_in_dim.8), calls=%async_computation.4 | async-start | bytes 786432 | tf_op jit(solution)/shard_map/all_to_all | solution.py:234

commit v7 on v6

v7 whole, which is shorter than its diff:
```python
import jax
import jax.numpy as jnp
from jax import lax
from jax.experimental import pallas as pl
from jax.experimental.pallas import tpu as pltpu
from jax.sharding import Mesh, PartitionSpec as P

NOCC = 64
NVIR = 768
NVEC = 32
NCHIP = 8
OCC_DEV = 4
PAIRS = OCC_DEV * NVIR
HALF = 16
CHUNKS = 3
ROWS = NOCC * HALF

F32 = jnp.float32
BF16 = jnp.bfloat16

CHIPS = ("x", "yl")
WIDE = ("x", "yl", "c")
NARROW = ("yh", "z")
MOST = ("x", "yl", "c", "z")


def swap_blocks(tile):
    v = [tile[j * 16 : (j + 1) * 16] for j in range(8)]
    lane = lax.broadcasted_iota(jnp.int32, (16, 128), 1)
    for s in (4, 2, 1):
        bit = (lane & (16 * s)) != 0
        new = list(v)
        for j in range(8):
            if j & s:
                continue
            lo, hi = v[j], v[j + s]
            new[j] = jnp.where(bit, pltpu.roll(hi, 16 * s, 1), lo)
            new[j + s] = jnp.where(bit, hi, pltpu.roll(lo, 128 - 16 * s, 1))
        v = new
    return jnp.concatenate(v, 0)


def rows_of(ref, start, count):
    return ref[start // 64 : (start + count) // 64].reshape(count, NVIR)


def get_rows(b2, own, other, g, sems):
    src, chips = (own, other)[g // 2], pl.ds((g % 2) * 4, 4)
    copies = []
    for q in range(OCC_DEV):
        lanes = pl.ds(q * NVIR, NVIR)
        copies.append(pltpu.make_async_copy(src.at[chips, :, lanes], b2.at[pl.ds(g * 4, 4), q], sems.at[g, q]))
    return copies


def contract_first(x2, b2, d, diag, order, before):
    for g, rb in order:
        before(g, rb)
        lhs, rhs = rows_of(x2, rb * 256, 256), rows_of(b2, g * 256, 256)
        inter = lax.dot_general(lhs, rhs, (((1,), (1,)), ((), ())), preferred_element_type=F32)
        for a in range(2):
            for h in range(2):
                ig, jg = g * 2 + h, rb * 2 + a
                tile = inter[a * 128 : (a + 1) * 128, h * 128 : (h + 1) * 128]
                if ig == jg:
                    diag[ig] = tile
                d[ig * 128 : (ig + 1) * 128, jg * 128 : (jg + 1) * 128] = swap_blocks(tile).astype(BF16)
    same = lax.broadcasted_iota(jnp.int32, (128, 128), 0) // 16 == lax.broadcasted_iota(jnp.int32, (128, 128), 1) // 16
    fit = diag[0]
    for k in range(1, 8):
        fit = fit + diag[k]
    fit = jnp.where(same, fit, 0.0)
    total = fit[0:16, :]
    for j in range(1, 8):
        total = total + fit[j * 16 : (j + 1) * 16, :]
    for s in (64, 32, 16):
        total = total + pltpu.roll(total, s, 1)
    double = 2.0 * total.astype(BF16).astype(F32)
    return jnp.where(same, jnp.concatenate([double] * 8, 0), 0.0).astype(BF16)


def contract_second(b2, d, acc, fit, before, emit):
    def close(rb):
        for g in (rb * 2, rb * 2 + 1):
            rows = slice(g * 128, (g + 1) * 128)
            emit(g, acc[rows, :] - jnp.dot(fit, rows_of(b2, g * 128, 128), preferred_element_type=F32))

    for rb in range(4):
        rows = slice(rb * 256, (rb + 1) * 256)
        clear = before(rb)
        term = jnp.dot(d[rows, :], rows_of(b2, 0, ROWS), preferred_element_type=F32)
        acc[rows, :] = term if clear else acc[rows, :] + term
        if rb:
            close(rb - 1)
    close(3)


WAVE = sorted(((g, rb) for g in range(4) for rb in range(4)), key=lambda pair: (max(pair), pair))


def early_kernel(where, x_a, x_b, x_c, x_d, own0, other0, own1, other1, out, x_out, x2, b_a, b_b, d, acc, diag, xs, bs, os):
    z = where[1]
    gets, rows0, rows1 = [], [], []
    for k in range(4):
        part = pl.ds(k * 4, 4)
        gets.append([pltpu.make_async_copy(ref.at[part], x2.at[part, (z - s) & 3], xs.at[k, s]) for s, ref in enumerate((x_a, x_b, x_c, x_d))])
        rows0.append(get_rows(b_a, own0, other0, k, bs.at[0]))
        rows1.append(get_rows(b_b, own1, other1, k, bs.at[1]))
        for cp in gets[k] + rows0[k]:
            cp.start()
    keep_x = pltpu.make_async_copy(x2, x_out, xs.at[4, 0])
    puts = []

    def before0(g, rb):
        if max(g, rb) == g and rb == 0:
            for cp in rows0[g]:
                cp.wait()
        if g == 0:
            for cp in gets[rb]:
                cp.wait()
        if (g, rb) == WAVE[-1]:
            for row in rows1:
                for cp in row:
                    cp.start()

    def before1(g, rb):
        if rb == 0:
            for cp in rows1[g]:
                cp.wait()
        if (g, rb) == (1, 0):
            keep_x.start()

    def store(g, value):
        acc[g * 128 : (g + 1) * 128, :] = value

    def send(g, value):
        store(g, value)
        rows = pl.ds(g * 128, 128)
        puts.append(pltpu.make_async_copy(acc.at[rows], out.at[rows], os.at[g]))
        puts[-1].start()

    fit = contract_first(x2, b_a, d, diag, WAVE, before0)
    contract_second(b_a, d, acc, fit, lambda rb: True, store)
    fit = contract_first(x2, b_b, d, diag, [(g, rb) for g in range(4) for rb in range(4)], before1)
    contract_second(b_b, d, acc, fit, lambda rb: False, send)
    keep_x.wait()
    for cp in puts:
        cp.wait()


def late_kernel(where, x_in, own, other, acc_in, out, x2, b2, d, acc, diag, xs, os):
    c = where[0]
    gets, sums = [], []
    for k in range(4):
        part = pl.ds(k * 4, 4)
        gets.append(pltpu.make_async_copy(x_in.at[part], x2.at[part], xs.at[k]))
        gets[k].start()
        part = pl.ds(k * 256, 256)
        sums.append(pltpu.make_async_copy(acc_in.at[part], acc.at[part], os.at[k]))

    def before(g, rb):
        if g == 0:
            gets[rb].wait()
            if rb == 1:
                for cp in sums:
                    cp.start()
        if rb == 0:
            src = (own, other)[g // 2]
            for k in range(4):
                for q in range(OCC_DEV):
                    b2[g * 4 + k, q] = src[(g % 2) * 4 + k, :, q * NVIR : (q + 1) * NVIR]

    def before_sum(rb):
        sums[rb].wait()
        return False

    def emit(g, value):
        value = value.astype(BF16).reshape(2, OCC_DEV, HALF, NVIR)
        for k in range(2):
            rel, chip = g // 4, (g % 4) * 2 + k
            out[chip * 2 + (c ^ rel)] = value[k]

    fit = contract_first(x2, b2, d, diag, [(g, rb) for rb in range(4) for g in range(4)], before)
    contract_second(b2, d, acc, fit, before_sum, emit)


def final_kernel(where, occ, vir, trials, p_a, p_b, p_c, p_d, out):
    for s, ref in enumerate((p_a, p_b, p_c, p_d)):
        q = (where[0] - s) & 3
        lanes = pl.ds(pl.multiple_of(q * NVIR, NVIR), NVIR)
        delta = vir[...] - occ[where[1] * OCC_DEV + q]
        out[:, lanes] = delta * trials[:, lanes].astype(F32) - ref[...]


VMEM = pl.BlockSpec(memory_space=pltpu.VMEM)
LATE_MIB = 50
SMEM = pl.BlockSpec(memory_space=pltpu.SMEM)
ANY = pl.BlockSpec(memory_space=pl.ANY)
BLOCK = (16, OCC_DEV, HALF, NVIR)


def cost(count):
    return pl.CostEstimate(flops=count * 4 * ROWS * ROWS * NVIR, bytes_accessed=4 * ROWS * NVIR * 2, transcendentals=0)


def early(where, x, own, other):
    return pl.pallas_call(
        early_kernel,
        out_shape=[jax.ShapeDtypeStruct((ROWS, NVIR), F32), jax.ShapeDtypeStruct(BLOCK, BF16)],
        in_specs=[SMEM] + [ANY] * 8,
        out_specs=[ANY, ANY],
        scratch_shapes=[
            pltpu.VMEM(BLOCK, BF16),
            pltpu.VMEM(BLOCK, BF16),
            pltpu.VMEM(BLOCK, BF16),
            pltpu.VMEM((ROWS, ROWS), BF16),
            pltpu.VMEM((ROWS, NVIR), F32),
            pltpu.VMEM((8, 128, 128), F32),
            pltpu.SemaphoreType.DMA((5, 4)),
            pltpu.SemaphoreType.DMA((2, 4, 4)),
            pltpu.SemaphoreType.DMA((8,)),
        ],
        cost_estimate=cost(2),
        compiler_params=pltpu.CompilerParams(vmem_limit_bytes=60 << 20),
        name="terms_early",
    )(where, *x, own[0], other[0], own[1], other[1])


def late(where, x2, own, other, acc):
    return pl.pallas_call(
        late_kernel,
        out_shape=jax.ShapeDtypeStruct(BLOCK, BF16),
        in_specs=[SMEM, ANY, VMEM, VMEM, ANY],
        out_specs=VMEM,
        scratch_shapes=[
            pltpu.VMEM(BLOCK, BF16),
            pltpu.VMEM(BLOCK, BF16),
            pltpu.VMEM((ROWS, ROWS), BF16),
            pltpu.VMEM((ROWS, NVIR), F32),
            pltpu.VMEM((8, 128, 128), F32),
            pltpu.SemaphoreType.DMA((4,)),
            pltpu.SemaphoreType.DMA((4,)),
        ],
        cost_estimate=cost(1),
        compiler_params=pltpu.CompilerParams(vmem_limit_bytes=LATE_MIB << 20),
        name="terms_late",
    )(where, x2, own[2], other[2], acc).reshape(16 * OCC_DEV, HALF, NVIR)


def final(where, occ, vir, trials, pieces):
    return pl.pallas_call(
        final_kernel,
        out_shape=jax.ShapeDtypeStruct((NVEC, PAIRS), F32),
        in_specs=[SMEM, SMEM] + [VMEM] * 6,
        out_specs=VMEM,
        compiler_params=pltpu.CompilerParams(vmem_limit_bytes=16 << 20),
        name="final",
    )(where, occ, vir.reshape(1, NVIR), trials, *pieces)


def ring(n, s):
    return [(i, (i + s) % n) for i in range(n)]


def body(fit_rows, trials, occ_energy, vir_energy):
    core = lax.axis_index("c").astype(jnp.int32)
    z = (lax.axis_index("z") + 2 * lax.axis_index("yh")).astype(jnp.int32) & 3
    where = jnp.stack([core, z])
    blocks = [fit_rows.reshape(CHUNKS, NCHIP, HALF, PAIRS)]
    for _ in range(1, CHUNKS):
        blocks.append(lax.optimization_barrier(blocks[-1]))
    mine = lax.dynamic_slice_in_dim(trials, z * NVIR, NVIR, 1)
    mine = jnp.concatenate([mine[:HALF], mine[HALF:]], 1)
    mine = jnp.broadcast_to(mine[None], (NCHIP, HALF, 2 * NVIR))
    own, other = [], []
    for t in range(CHUNKS):
        send = blocks[t][t]
        if t == 0:
            send = jnp.concatenate([send, mine], 2)
        own.append(lax.all_to_all(send, CHIPS, 0, 0, tiled=True))
        other.append(lax.ppermute(own[t], "c", ring(2, 1)))
    x_own = lax.dynamic_slice_in_dim(own[0], PAIRS + core * NVIR, NVIR, 2)
    x_send = lax.dynamic_slice_in_dim(own[0], PAIRS + (1 - core) * NVIR, NVIR, 2)
    x_other = lax.ppermute(x_send, "c", ring(2, 1))
    x = [jnp.concatenate([x_own, x_other])]
    steps = (("z", ring(4, 1)), ("yh", ring(2, 1)), ("z", ring(4, 3)))
    x = x + [lax.ppermute(x[0], axis, perm) for axis, perm in steps]
    acc, x2 = early(where, x, own, other)
    acc = late(where, x2, own, other, acc)
    parts = lax.all_to_all(acc, MOST, 0, 0, tiled=True)
    part = jnp.sum(parts.reshape(NCHIP, 2, 4, HALF, NVIR).astype(F32), (0, 2)).reshape(NVEC, NVIR)
    part = part + lax.ppermute(part, "yh", ring(2, 1))
    pieces = [part] + [lax.ppermute(part, "z", ring(4, s)) for s in (1, 2, 3)]
    place = jnp.stack([lax.axis_index("z"), lax.axis_index(WIDE)]).astype(jnp.int32)
    return final(place, occ_energy, vir_energy, trials, pieces)


def solution(mesh):
    fine = Mesh(mesh.devices.reshape(4, 2, 2, 2, 4), ("x", "yl", "c", "yh", "z"))
    in_specs = (P(NARROW, WIDE), P(None, WIDE), P(), P())
    return jax.shard_map(body, mesh=fine, in_specs=in_specs, out_specs=P(None, WIDE), check_vma=False)
```

time: 136 us -> 141 us (1.037)
  Pallas kernels: 20.5 us -> 26.1 us
  starting transfers between devices: 24 us -> 26.2 us
    all_to_all x1 -> x0, waiting for transfers between devices: 9.6 us -> none  [body(): every = lax.all_to_all(part, NARROW, 0, 0, tiled=True)]
    ppermute x0 -> x4, waiting for transfers between devices: none -> 9.12 us  [the longest x3 4.85 us: body(): pieces = [part] + [lax.ppermute(part, 'z', ring(4, s)) for s in (1, 2, 3)]]
    ppermute x0 -> x4, starting transfers between devices: none -> 5.22 us  [the longest x3 3.29 us: body(): pieces = [part] + [lax.ppermute(part, 'z', ring(4, s)) for s in (1, 2, 3)]]
    all_to_all x1 -> x0, starting transfers between devices: 3.74 us -> none  [body(): every = lax.all_to_all(part, NARROW, 0, 0, tiled=True)]
    pallas_call x1, Pallas kernels: 12.7 us -> 16.4 us  [early(): pl.pallas_call(early_kernel, out_shape=[jax.ShapeDtypeStruct((ROWS, NVIR)...]
  transfers between devices with their start and end apart: 11 -> 14, of which waited for: 7 -> 10; matrix products, arithmetic and copies ran while one was open for 3% -> 3% of each run, Pallas kernels for 9% -> 12%
where the time goes in v7:
time: 141 us
  waiting for transfers between devices  48.6 us (34%)
  blocking collectives  32.4 us (23%)
  starting transfers between devices  26.2 us (19%)
  Pallas kernels  26.1 us (19%)
  local copies, waits for them, and re-layouts  5.22 us (4%)
  other arithmetic  2.08 us (1%)
    all_to_all x1, blocking collectives, body(): parts = lax.all_to_all(acc, MOST, 0, 0, tiled=True)  32.4 us
    all_to_all x3, waiting for transfers between devices, body(): own.append(lax.all_to_all(send, CHIPS, 0, 0, tiled=True))  31.8 us
    pallas_call x1, Pallas kernels, early(): pl.pallas_call(early_kernel, out_shape=[jax.ShapeDtypeStruct((ROWS, NVIR)...  16.4 us
    all_to_all x3, starting transfers between devices, body(): own.append(lax.all_to_all(send, CHIPS, 0, 0, tiled=True))  13.2 us
    pallas_call x1, Pallas kernels, late(): pl.pallas_call(late_kernel, out_shape=jax.ShapeDtypeStruct(BLOCK, BF16),...  8.43 us
    ppermute x3, starting transfers between devices, body(): x = x + [lax.ppermute(x[0], axis, perm) for axis, perm in steps]  7.1 us
    ppermute x3, waiting for transfers between devices, body(): x = x + [lax.ppermute(x[0], axis, perm) for axis, perm in steps]  6.6 us
    ppermute x3, waiting for transfers between devices, body(): pieces = [part] + [lax.ppermute(part, 'z', ring(4, s)) for s in (1, 2, 3)]  4.85 us
  transfers between devices with their start and end apart: 14, of which 10 were waited for; matrix products, arithmetic and copies ran while one was open for 3% of the time, Pallas kernels for 12%

profile of v7, /device:TPU:0, one launch (start us, length us, event | category | flops | bytes accessed | tf_op | source)
XLA Modules:
  0.0 140.8 jit_solution(9102058538528754834)
XLA Ops:
  0.0 0.0 copy-start
  0.0 0.0 copy-start.3
  0.0 2.2 %slice_bitcast_fusion.1 = bf16[8,16,3072]{2,1,0:T(8,128)(2,1)} fusion(bf16[3,8,16,3072]{3,2,1,0:T(8,128)(2,1)} %bitcast.18), kind=kLoop, calls=%fused_computation.3 | loop fusion | bytes 1572864 | tf_op jit(solution)/shard_map/squeeze | solution.py:277
  2.2 5.4 %all-to-all-start.1 = ((bf16[8,16,3072]{2,1,0:T(8,128)(2,1)}), bf16[8,16,3072]{2,1,0:T(8,128)(2,1)}, u32[]{:S(2)}, u32[]{:S(2)}) async-start(bf16[8,16,3072]{2,1,0:T(8,128)(2,1)} %slice_bitcast_fusion.1), calls=%async_computation.1 | async-start | bytes 1572864 | tf_op jit(solution)/shard_map/all_to_all | solution.py:280
  7.7 0.0 copy-done
  7.7 0.0 copy-done.3
  7.7 0.1 slice.16
  7.8 1.1 pad_maximum_fusion
  8.9 11.2 %all-to-all-done.1.own1 = bf16[8,16,3072]{2,1,0:T(8,128)(2,1)} async-done(((bf16[8,16,3072]{2,1,0:T(8,128)(2,1)}), bf16[8,16,3072]{2,1,0:T(8,128)(2,1)}, u32[]{:S(2)}, u32[]{:S(2)}) %all-to-all-start.1) | async-done | bytes 786464 | tf_op jit(solution)/shard_map/all_to_all | solution.py:280
  20.1 4.3 %all-to-all-start = ((bf16[8,16,4608]{2,1,0:T(8,128)(2,1)}), bf16[8,16,4608]{2,1,0:T(8,128)(2,1)}, u32[]{:S(2)}, u32[]{:S(2)}) async-start(bf16[8,16,4608]{2,1,0:T(8,128)(2,1)} %pad_maximum_fusion), calls=%async_computation | async-start | bytes 2359296 | tf_op jit(solution)/shard_map/all_to_all | solution.py:280
  24.4 0.1 collective-permute-start.5
  24.5 16.4 %all-to-all-done.own0 = bf16[8,16,4608]{2,1,0:T(8,128)(2,1)} async-done(((bf16[8,16,4608]{2,1,0:T(8,128)(2,1)}), bf16[8,16,4608]{2,1,0:T(8,128)(2,1)}, u32[]{:S(2)}, u32[]{:S(2)}) %all-to-all-start) | async-done | bytes 1179680 | tf_op jit(solution)/shard_map/all_to_all | solution.py:280
  40.9 0.0 collective-permute-start.4
  40.9 1.0 slice_bitcast_fusion
  41.9 3.5 %all-to-all-start.2 = ((bf16[8,16,3072]{2,1,0:T(8,128)(2,1)}), bf16[8,16,3072]{2,1,0:T(8,128)(2,1)S(1)}, u32[]{:S(2)}, u32[]{:S(2)}) async-start(bf16[8,16,3072]{2,1,0:T(8,128)(2,1)} %slice_bitcast_fusion), calls=%async_computation.2 | async-start | bytes 1572864 | tf_op jit(solution)/shard_map/all_to_all | solution.py:280
  45.4 1.1 constant_dynamic-slice_fusion.2
  46.5 0.6 collective-permute-start
  47.1 1.1 collective-permute-done
  48.2 0.0 copy-start.4
  48.2 2.0 %collective-permute-start.1 = (bf16[16,16,768]{2,1,0:T(8,128)(2,1)S(1)}, bf16[16,16,768]{2,1,0:T(8,128)(2,1)S(1)}, u32[]{:S(2)}, u32[]{:S(2)}) collective-permute-start(bf16[16,16,768]{2,1,0:T(8,128)(2,1)S(1)} %pad_maximum_fusion.1.x_a), channel_id=1, source_target_pairs={{0,1},{1,2},{2,3},{3,0},{4,5},{5,6},{6,7},{7,4},{8,9},{9,10},{10,1... | collective-permute-start | bytes 1179656 | tf_op jit(solution)/shard_map/ppermute | solution.py:287
  50.2 2.9 %collective-permute-start.2 = (bf16[16,16,768]{2,1,0:T(8,128)(2,1)S(1)}, bf16[16,16,768]{2,1,0:T(8,128)(2,1)S(1)}, u32[]{:S(2)}, u32[]{:S(2)}) collective-permute-start(bf16[16,16,768]{2,1,0:T(8,128)(2,1)S(1)} %pad_maximum_fusion.1.x_a), channel_id=1, source_target_pairs={{0,4},{4,0},{1,5},{5,1},{2,6},{6,2},{3,7},{7,3},{8,12},{12,8},{9,1... | collective-permute-start | bytes 1179656 | tf_op jit(solution)/shard_map/ppermute | solution.py:287
  53.1 2.2 %collective-permute-start.3 = (bf16[16,16,768]{2,1,0:T(8,128)(2,1)S(1)}, bf16[16,16,768]{2,1,0:T(8,128)(2,1)S(1)}, u32[]{:S(2)}, u32[]{:S(2)}) collective-permute-start(bf16[16,16,768]{2,1,0:T(8,128)(2,1)S(1)} %pad_maximum_fusion.1.x_a), channel_id=1, source_target_pairs={{0,3},{1,0},{2,1},{3,2},{4,7},{5,4},{6,5},{7,6},{8,11},{9,8},{10,9... | collective-permute-start | bytes 1179656 | tf_op jit(solution)/shard_map/ppermute | solution.py:287
  55.3 4.2 %all-to-all-done.2.own = bf16[8,16,3072]{2,1,0:T(8,128)(2,1)S(1)} async-done(((bf16[8,16,3072]{2,1,0:T(8,128)(2,1)}), bf16[8,16,3072]{2,1,0:T(8,128)(2,1)S(1)}, u32[]{:S(2)}, u32[]{:S(2)}) %all-to-all-start.2) | async-done | bytes 786464 | tf_op jit(solution)/shard_map/all_to_all | solution.py:280
  59.5 0.0 collective-permute-done.5.other1
  59.5 0.0 collective-permute-start.6
  59.5 0.6 pad_add_fusion.1.where
  60.1 0.0 copy-start.2
  60.1 1.8 %collective-permute-done.1.x_b = bf16[16,16,768]{2,1,0:T(8,128)(2,1)S(1)} collective-permute-done((bf16[16,16,768]{2,1,0:T(8,128)(2,1)S(1)}, bf16[16,16,768]{2,1,0:T(8,128)(2,1)S(1)}, u32[]{:S(2)}, u32[]{:S(2)}) %collective-permute-start.1) | collective-permute-done | bytes 393248 | tf_op jit(solution)/shard_map/ppermute | solution.py:287
  61.9 0.0 copy-start.6
  61.9 4.8 %collective-permute-done.2.x_c = bf16[16,16,768]{2,1,0:T(8,128)(2,1)S(1)} collective-permute-done((bf16[16,16,768]{2,1,0:T(8,128)(2,1)S(1)}, bf16[16,16,768]{2,1,0:T(8,128)(2,1)S(1)}, u32[]{:S(2)}, u32[]{:S(2)}) %collective-permute-start.2) | collective-permute-done | bytes 393248 | tf_op jit(solution)/shard_map/ppermute | solution.py:287
  66.7 0.0 copy-start.7
  66.7 0.0 collective-permute-done.3.x_d
  66.7 0.0 copy-start.8
  66.7 0.0 collective-permute-done.4.other0
  66.7 0.0 copy-done.4
  66.7 0.0 copy-done.6
  66.7 0.7 copy-done.7
  67.5 0.1 copy-done.8
  67.6 16.4 %terms_early.1 = (f32[1024,768]{1,0:T(8,128)}, bf16[16,4,16,768]{3,2,1,0:T(8,128)(2,1)}) custom-call(s32[2]{0:T(128)} %pad_add_fusion.1.where, bf16[16,16,768]{2,1,0:T(8,128)(2,1)} %copy-done.4, bf16[16,16,768]{2,1,0:T(8,128)(2,1)} %copy-done.6, bf16[16,16,768]{2,1,0:T(8,128)(2,1)} %copy-done.7, bf16[16,16,768]{2,1,0:T(8,128)(2,1)} %copy-done.8, ...), custom_call_target="tpu_custom_call" | custom-call | flops 6442450944 | bytes 6291456 | tf_op jit(solution)/shard_map/terms_early/pallas_call | solution.py:207
  84.0 0.0 collective-permute-done.6.other
  84.0 0.0 copy-done.2
  84.0 8.4 %terms_late.1 = bf16[16,4,16,768]{3,2,1,0:T(8,128)(2,1)S(1)} custom-call(s32[2]{0:T(128)S(1)} %copy-done.2, bf16[16,4,16,768]{3,2,1,0:T(8,128)(2,1)} %get-tuple-element.7.x_in, bf16[8,16,3072]{2,1,0:T(8,128)(2,1)S(1)} %all-to-all-done.2.own, bf16[8,16,3072]{2,1,0:T(8,128)(2,1)S(1)} %collective-permute-done.6.other, f32[1024,768]{1,0:T(8,128)} %get-tuple-element.8.acc_in), custom_call_target="tpu_custom_call" | custom-call | flops 3221225472 | bytes 6291456 | tf_op jit(solution)/shard_map/terms_late/pallas_call | solution.py:230
  92.4 32.4 %all_to_all.20 = bf16[64,16,768]{2,1,0:T(8,128)(2,1)S(1)} all-to-all(bf16[64,16,768]{2,1,0:T(8,128)(2,1)S(1)} %bitcast.15), channel_id=1, replica_groups=mesh['x'=4,'yl'=2,'c'=2,'yh'=2,'z'=4] {'x','yl','c','z'}, dimensions={0} | all-to-all | bytes 3145728 | tf_op jit(solution)/shard_map/all_to_all | solution.py:290
  124.8 0.0 copy-start.5
  124.8 0.0 copy-start.1
  124.8 0.2 convert_reduce_fusion
  125.0 1.9 %collective-permute-start.7 = (f32[32,768]{1,0:T(8,128)S(1)}, f32[32,768]{1,0:T(8,128)S(1)}, u32[]{:S(2)}, u32[]{:S(2)}) collective-permute-start(f32[32,768]{1,0:T(8,128)S(1)} %bitcast.20), channel_id=1, source_target_pairs={{0,4},{4,0},{1,5},{5,1},{2,6},{6,2},{3,7},{7,3},{8,12},{12,8},{9,1... | collective-permute-start | bytes 294920 | tf_op jit(solution)/shard_map/ppermute | solution.py:292
  126.9 0.0 copy-done.5
  126.9 4.3 %collective-permute-done.7 = f32[32,768]{1,0:T(8,128)S(1)} collective-permute-done((f32[32,768]{1,0:T(8,128)S(1)}, f32[32,768]{1,0:T(8,128)S(1)}, u32[]{:S(2)}, u32[]{:S(2)}) %collective-permute-start.7) | collective-permute-done | bytes 98336 | tf_op jit(solution)/shard_map/ppermute | solution.py:292
  131.2 0.8 collective-permute-start.10
  132.0 1.3 collective-permute-start.8
  133.3 1.2 collective-permute-start.9
  134.5 0.1 pad_add_fusion.where
  134.6 1.8 %collective-permute-done.10.p_d = f32[32,768]{1,0:T(8,128)S(1)} collective-permute-done((f32[32,768]{1,0:T(8,128)S(1)}, f32[32,768]{1,0:T(8,128)S(1)}, u32[]{:S(2)}, u32[]{:S(2)}) %collective-permute-start.10) | collective-permute-done | bytes 98336 | tf_op jit(solution)/shard_map/ppermute | solution.py:293
  136.4 1.5 %collective-permute-done.8.p_b = f32[32,768]{1,0:T(8,128)S(1)} collective-permute-done((f32[32,768]{1,0:T(8,128)S(1)}, f32[32,768]{1,0:T(8,128)S(1)}, u32[]{:S(2)}, u32[]{:S(2)}) %collective-permute-start.8) | collective-permute-done | bytes 98336 | tf_op jit(solution)/shard_map/ppermute | solution.py:293
  138.0 1.5 %collective-permute-done.9.p_c = f32[32,768]{1,0:T(8,128)S(1)} collective-permute-done((f32[32,768]{1,0:T(8,128)S(1)}, f32[32,768]{1,0:T(8,128)S(1)}, u32[]{:S(2)}, u32[]{:S(2)}) %collective-permute-start.9) | collective-permute-done | bytes 98336 | tf_op jit(solution)/shard_map/ppermute | solution.py:293
  139.4 0.0 copy-done.1
  139.4 1.3 final.1
  (6 shorter events, 0.1 us)
Async XLA Ops:
  0.0 7.7 %copy-start = (bf16[32,3072]{1,0:T(8,128)(2,1)S(1)}, bf16[32,3072]{1,0:T(8,128)(2,1)}, u32[]{:S(2)}) copy-start(bf16[32,3072]{1,0:T(8,128)(2,1)} %trials.1) | copy-start | bytes 589828
  0.0 7.7 %copy-start.3 = (bf16[384,3072]{1,0:T(8,128)(2,1)S(1)}, bf16[384,3072]{1,0:T(8,128)(2,1)}, u32[]{:S(2)}) copy-start(bf16[384,3072]{1,0:T(8,128)(2,1)} %param.4) | copy-start | bytes 7077892
  2.2 17.9 %all-to-all-start.1 = ((bf16[8,16,3072]{2,1,0:T(8,128)(2,1)}), bf16[8,16,3072]{2,1,0:T(8,128)(2,1)}, u32[]{:S(2)}, u32[]{:S(2)}) async-start(bf16[8,16,3072]{2,1,0:T(8,128)(2,1)} %slice_bitcast_fusion.1), calls=%async_computation.1 | async-start | bytes 1572864 | tf_op jit(solution)/shard_map/all_to_all | solution.py:280
  20.1 20.8 %all-to-all-start = ((bf16[8,16,4608]{2,1,0:T(8,128)(2,1)}), bf16[8,16,4608]{2,1,0:T(8,128)(2,1)}, u32[]{:S(2)}, u32[]{:S(2)}) async-start(bf16[8,16,4608]{2,1,0:T(8,128)(2,1)} %pad_maximum_fusion), calls=%async_computation | async-start | bytes 2359296 | tf_op jit(solution)/shard_map/all_to_all | solution.py:280
  24.4 35.1 %collective-permute-start.5 = (bf16[8,16,3072]{2,1,0:T(8,128)(2,1)}, bf16[8,16,3072]{2,1,0:T(8,128)(2,1)}, u32[]{:S(2)}, u32[]{:S(2)}) collective-permute-start(bf16[8,16,3072]{2,1,0:T(8,128)(2,1)} %all-to-all-done.1.own1), channel_id=1, source_target_pairs={{0,8},{8,0},{1,9},{9,1},{2,10},{10,2},{3,11},{11,3},{4,12},{12,4},... | collective-permute-start | bytes 2359304 | tf_op jit(solution)/shard_map/ppermute | solution.py:281
  40.9 25.8 %collective-permute-start.4 = (bf16[8,16,4608]{2,1,0:T(8,128)(2,1)}, bf16[8,16,4608]{2,1,0:T(8,128)(2,1)}, u32[]{:S(2)}, u32[]{:S(2)}) collective-permute-start(bf16[8,16,4608]{2,1,0:T(8,128)(2,1)} %all-to-all-done.own0), channel_id=1, source_target_pairs={{0,8},{8,0},{1,9},{9,1},{2,10},{10,2},{3,11},{11,3},{4,12},{12,4},... | collective-permute-start | bytes 3538952 | tf_op jit(solution)/shard_map/ppermute | solution.py:281
  41.9 17.6 %all-to-all-start.2 = ((bf16[8,16,3072]{2,1,0:T(8,128)(2,1)}), bf16[8,16,3072]{2,1,0:T(8,128)(2,1)S(1)}, u32[]{:S(2)}, u32[]{:S(2)}) async-start(bf16[8,16,3072]{2,1,0:T(8,128)(2,1)} %slice_bitcast_fusion), calls=%async_computation.2 | async-start | bytes 1572864 | tf_op jit(solution)/shard_map/all_to_all | solution.py:280
  46.5 1.7 %collective-permute-start = (bf16[8,16,768]{2,1,0:T(8,128)(2,1)S(1)}, bf16[8,16,768]{2,1,0:T(8,128)(2,1)S(1)}, u32[]{:S(2)}, u32[]{:S(2)}) collective-permute-start(bf16[8,16,768]{2,1,0:T(8,128)(2,1)S(1)} %get-tuple-element.10), channel_id=1, source_target_pairs={{0,8},{8,0},{1,9},{9,1},{2,10},{10,2},{3,11},{11,3},{4,12},{12,4},... | collective-permute-start | bytes 589832 | tf_op jit(solution)/shard_map/ppermute | solution.py:284
  48.2 18.6 %copy-start.4 = (bf16[16,16,768]{2,1,0:T(8,128)(2,1)}, bf16[16,16,768]{2,1,0:T(8,128)(2,1)S(1)}, u32[]{:S(2)}) copy-start(bf16[16,16,768]{2,1,0:T(8,128)(2,1)S(1)} %pad_maximum_fusion.1.x_a) | copy-start | bytes 1179652
  48.2 13.8 %collective-permute-start.1 = (bf16[16,16,768]{2,1,0:T(8,128)(2,1)S(1)}, bf16[16,16,768]{2,1,0:T(8,128)(2,1)S(1)}, u32[]{:S(2)}, u32[]{:S(2)}) collective-permute-start(bf16[16,16,768]{2,1,0:T(8,128)(2,1)S(1)} %pad_maximum_fusion.1.x_a), channel_id=1, source_target_pairs={{0,1},{1,2},{2,3},{3,0},{4,5},{5,6},{6,7},{7,4},{8,9},{9,10},{10,1... | collective-permute-start | bytes 1179656 | tf_op jit(solution)/shard_map/ppermute | solution.py:287
  50.2 16.5 %collective-permute-start.2 = (bf16[16,16,768]{2,1,0:T(8,128)(2,1)S(1)}, bf16[16,16,768]{2,1,0:T(8,128)(2,1)S(1)}, u32[]{:S(2)}, u32[]{:S(2)}) collective-permute-start(bf16[16,16,768]{2,1,0:T(8,128)(2,1)S(1)} %pad_maximum_fusion.1.x_a), channel_id=1, source_target_pairs={{0,4},{4,0},{1,5},{5,1},{2,6},{6,2},{3,7},{7,3},{8,12},{12,8},{9,1... | collective-permute-start | bytes 1179656 | tf_op jit(solution)/shard_map/ppermute | solution.py:287
  53.1 13.6 %collective-permute-start.3 = (bf16[16,16,768]{2,1,0:T(8,128)(2,1)S(1)}, bf16[16,16,768]{2,1,0:T(8,128)(2,1)S(1)}, u32[]{:S(2)}, u32[]{:S(2)}) collective-permute-start(bf16[16,16,768]{2,1,0:T(8,128)(2,1)S(1)} %pad_maximum_fusion.1.x_a), channel_id=1, source_target_pairs={{0,3},{1,0},{2,1},{3,2},{4,7},{5,4},{6,5},{7,6},{8,11},{9,8},{10,9... | collective-permute-start | bytes 1179656 | tf_op jit(solution)/shard_map/ppermute | solution.py:287
  59.5 24.5 %collective-permute-start.6 = (bf16[8,16,3072]{2,1,0:T(8,128)(2,1)S(1)}, bf16[8,16,3072]{2,1,0:T(8,128)(2,1)S(1)}, u32[]{:S(2)}, u32[]{:S(2)}) collective-permute-start(bf16[8,16,3072]{2,1,0:T(8,128)(2,1)S(1)} %all-to-all-done.2.own), channel_id=1, source_target_pairs={{0,8},{8,0},{1,9},{9,1},{2,10},{10,2},{3,11},{11,3},{4,12},{12,4},... | collective-permute-start | bytes 2359304 | tf_op jit(solution)/shard_map/ppermute | solution.py:281
  60.1 23.9 %copy-start.2 = (s32[2]{0:T(128)S(1)}, s32[2]{0:T(128)}, u32[]{:S(2)}) copy-start(s32[2]{0:T(128)} %pad_add_fusion.1.where) | copy-start | bytes 28
  61.9 4.8 %copy-start.6 = (bf16[16,16,768]{2,1,0:T(8,128)(2,1)}, bf16[16,16,768]{2,1,0:T(8,128)(2,1)S(1)}, u32[]{:S(2)}) copy-start(bf16[16,16,768]{2,1,0:T(8,128)(2,1)S(1)} %collective-permute-done.1.x_b) | copy-start | bytes 1179652
  66.7 0.7 copy-start.7
  66.7 0.9 copy-start.8
  124.8 2.2 %copy-start.5 = (f32[768]{0:T(1024)S(1)}, f32[768]{0:T(1024)}, u32[]{:S(2)}) copy-start(f32[768]{0:T(1024)} %param.7) | copy-start | bytes 9220
  124.8 14.7 %copy-start.1 = (f32[64]{0:T(128)S(1)}, f32[64]{0:T(128)}, u32[]{:S(2)}) copy-start(f32[64]{0:T(128)} %occ.1) | copy-start | bytes 772
  125.0 6.2 %collective-permute-start.7 = (f32[32,768]{1,0:T(8,128)S(1)}, f32[32,768]{1,0:T(8,128)S(1)}, u32[]{:S(2)}, u32[]{:S(2)}) collective-permute-start(f32[32,768]{1,0:T(8,128)S(1)} %bitcast.20), channel_id=1, source_target_pairs={{0,4},{4,0},{1,5},{5,1},{2,6},{6,2},{3,7},{7,3},{8,12},{12,8},{9,1... | collective-permute-start | bytes 294920 | tf_op jit(solution)/shard_map/ppermute | solution.py:292
  131.2 5.2 %collective-permute-start.10 = (f32[32,768]{1,0:T(8,128)S(1)}, f32[32,768]{1,0:T(8,128)S(1)}, u32[]{:S(2)}, u32[]{:S(2)}) collective-permute-start(f32[32,768]{1,0:T(8,128)S(1)} %bitcast_add_fusion.p_a), channel_id=1, source_target_pairs={{0,3},{1,0},{2,1},{3,2},{4,7},{5,4},{6,5},{7,6},{8,11},{9,8},{10,9... | collective-permute-start | bytes 294920 | tf_op jit(solution)/shard_map/ppermute | solution.py:293
  132.0 6.0 %collective-permute-start.8 = (f32[32,768]{1,0:T(8,128)S(1)}, f32[32,768]{1,0:T(8,128)S(1)}, u32[]{:S(2)}, u32[]{:S(2)}) collective-permute-start(f32[32,768]{1,0:T(8,128)S(1)} %bitcast_add_fusion.p_a), channel_id=1, source_target_pairs={{0,1},{1,2},{2,3},{3,0},{4,5},{5,6},{6,7},{7,4},{8,9},{9,10},{10,1... | collective-permute-start | bytes 294920 | tf_op jit(solution)/shard_map/ppermute | solution.py:293
  133.3 6.1 %collective-permute-start.9 = (f32[32,768]{1,0:T(8,128)S(1)}, f32[32,768]{1,0:T(8,128)S(1)}, u32[]{:S(2)}, u32[]{:S(2)}) collective-permute-start(f32[32,768]{1,0:T(8,128)S(1)} %bitcast_add_fusion.p_a), channel_id=1, source_target_pairs={{0,2},{1,3},{2,0},{3,1},{4,6},{5,7},{6,4},{7,5},{8,10},{9,11},{10,... | collective-permute-start | bytes 294920 | tf_op jit(solution)/shard_map/ppermute | solution.py:293

commit v8 on v7

v8 whole, which is shorter than its diff:
```python
import jax
import jax.numpy as jnp
from jax import lax
from jax.experimental import pallas as pl
from jax.experimental.pallas import tpu as pltpu
from jax.sharding import Mesh, PartitionSpec as P

NOCC = 64
NVIR = 768
NVEC = 32
NCHIP = 8
OCC_DEV = 4
PAIRS = OCC_DEV * NVIR
HALF = 16
STEPS = (1, 2)
ROWS = NOCC * HALF

F32 = jnp.float32
BF16 = jnp.bfloat16

CHIPS = ("x", "yl")
WIDE = ("x", "yl", "c")
NARROW = ("yh", "z")
MOST = ("x", "yl", "c", "z")


def swap_blocks(tile):
    v = [tile[j * 16 : (j + 1) * 16] for j in range(8)]
    lane = lax.broadcasted_iota(jnp.int32, (16, 128), 1)
    for s in (4, 2, 1):
        bit = (lane & (16 * s)) != 0
        new = list(v)
        for j in range(8):
            if j & s:
                continue
            lo, hi = v[j], v[j + s]
            new[j] = jnp.where(bit, pltpu.roll(hi, 16 * s, 1), lo)
            new[j + s] = jnp.where(bit, hi, pltpu.roll(lo, 128 - 16 * s, 1))
        v = new
    return jnp.concatenate(v, 0)


def rows_of(ref, start, count):
    return ref[start // 64 : (start + count) // 64].reshape(count, NVIR)


def take_rows(b2, own, other, step):
    for rel, src in enumerate((own, other)):
        for chip in range(NCHIP):
            for q in range(OCC_DEV):
                b2[rel * NCHIP + chip, q] = src[chip, step * HALF : (step + 1) * HALF, q * NVIR : (q + 1) * NVIR]


def contract_first(x2, b2, d, diag):
    for g, rb in ((g, rb) for g in range(4) for rb in range(4)):
        lhs, rhs = rows_of(x2, rb * 256, 256), rows_of(b2, g * 256, 256)
        inter = lax.dot_general(lhs, rhs, (((1,), (1,)), ((), ())), preferred_element_type=F32)
        for a in range(2):
            for h in range(2):
                ig, jg = g * 2 + h, rb * 2 + a
                tile = inter[a * 128 : (a + 1) * 128, h * 128 : (h + 1) * 128]
                if ig == jg:
                    diag[ig] = tile
                d[ig * 128 : (ig + 1) * 128, jg * 128 : (jg + 1) * 128] = swap_blocks(tile).astype(BF16)
    same = lax.broadcasted_iota(jnp.int32, (128, 128), 0) // 16 == lax.broadcasted_iota(jnp.int32, (128, 128), 1) // 16
    fit = diag[0]
    for k in range(1, 8):
        fit = fit + diag[k]
    fit = jnp.where(same, fit, 0.0)
    total = fit[0:16, :]
    for j in range(1, 8):
        total = total + fit[j * 16 : (j + 1) * 16, :]
    for s in (64, 32, 16):
        total = total + pltpu.roll(total, s, 1)
    double = 2.0 * total.astype(BF16).astype(F32)
    return jnp.where(same, jnp.concatenate([double] * 8, 0), 0.0).astype(BF16)


def contract_second(b2, d, acc, clear):
    for rb in range(4):
        rows = slice(rb * 256, (rb + 1) * 256)
        term = jnp.dot(d[rows, :], rows_of(b2, 0, ROWS), preferred_element_type=F32)
        acc[rows, :] = term if clear else acc[rows, :] + term


def less_coulomb(b2, acc, fit, g):
    return acc[g * 128 : (g + 1) * 128, :] - jnp.dot(fit, rows_of(b2, g * 128, 128), preferred_element_type=F32)


def early_kernel(where, x_a, x_b, x_c, x_e, x_d, own, other, out, x_out, x2, b2, d, acc, diag, xs, os):
    for s, low, high in ((0, x_a, x_a), (1, x_b, x_b), (2, x_c, x_e), (3, x_d, x_d)):
        q = (where[1] - s) & 3
        for k in range(NCHIP):
            x2[k, q] = low[k]
            x2[NCHIP + k, q] = high[high.shape[0] - NCHIP + k]
    keep_x = pltpu.make_async_copy(x2, x_out, xs.at[0])
    keep_x.start()
    take_rows(b2, own, other, 0)
    fit = contract_first(x2, b2, d, diag)
    contract_second(b2, d, acc, True)
    puts = []
    for half in range(2):
        for g in range(half * 4, half * 4 + 4):
            acc[g * 128 : (g + 1) * 128, :] = less_coulomb(b2, acc, fit, g)
        rows = pl.ds(half * 512, 512)
        puts.append(pltpu.make_async_copy(acc.at[rows], out.at[rows], os.at[half]))
        puts[-1].start()
    keep_x.wait()
    for cp in puts:
        cp.wait()


def late_kernel(where, x_in, own, other, acc_in, out, x2, b_a, b_b, d, acc, diag, xs, os):
    c = where[0]
    get_x = pltpu.make_async_copy(x_in, x2, xs.at[0])
    get_x.start()
    take_rows(b_a, own, other, 0)
    take_rows(b_b, own, other, 1)
    get_x.wait()
    get_acc = pltpu.make_async_copy(acc_in, acc, os.at[0])
    get_acc.start()
    fit_a = contract_first(x2, b_a, d, diag)
    get_acc.wait()
    contract_second(b_a, d, acc, False)
    for g in range(8):
        acc[g * 128 : (g + 1) * 128, :] = less_coulomb(b_a, acc, fit_a, g)
    fit_b = contract_first(x2, b_b, d, diag)
    contract_second(b_b, d, acc, False)
    for g in range(8):
        value = less_coulomb(b_b, acc, fit_b, g).astype(BF16).reshape(2, OCC_DEV, HALF, NVIR)
        for k in range(2):
            rel, chip = g // 4, (g % 4) * 2 + k
            out[chip * 2 + (c ^ rel)] = value[k]


def final_kernel(where, occ, vir, trials, p_a, p_b, p_c, p_d, out):
    for s, ref in enumerate((p_a, p_b, p_c, p_d)):
        q = (where[0] - s) & 3
        lanes = pl.ds(pl.multiple_of(q * NVIR, NVIR), NVIR)
        delta = vir[...] - occ[where[1] * OCC_DEV + q]
        out[:, lanes] = delta * trials[:, lanes].astype(F32) - ref[...]


VMEM = pl.BlockSpec(memory_space=pltpu.VMEM)
LATE_MIB = 46
EARLY_MIB = 46
SMEM = pl.BlockSpec(memory_space=pltpu.SMEM)
ANY = pl.BlockSpec(memory_space=pl.ANY)
BLOCK = (16, OCC_DEV, HALF, NVIR)


def cost(count):
    return pl.CostEstimate(flops=count * 4 * ROWS * ROWS * NVIR, bytes_accessed=4 * ROWS * NVIR * 2, transcendentals=0)


def early(where, x, own, other):
    return pl.pallas_call(
        early_kernel,
        out_shape=[jax.ShapeDtypeStruct((ROWS, NVIR), F32), jax.ShapeDtypeStruct(BLOCK, BF16)],
        in_specs=[SMEM] + [VMEM] * 7,
        out_specs=[ANY, ANY],
        scratch_shapes=[
            pltpu.VMEM(BLOCK, BF16),
            pltpu.VMEM(BLOCK, BF16),
            pltpu.VMEM((ROWS, ROWS), BF16),
            pltpu.VMEM((ROWS, NVIR), F32),
            pltpu.VMEM((8, 128, 128), F32),
            pltpu.SemaphoreType.DMA((1,)),
            pltpu.SemaphoreType.DMA((2,)),
        ],
        cost_estimate=cost(1),
        compiler_params=pltpu.CompilerParams(vmem_limit_bytes=EARLY_MIB << 20),
        name="terms_early",
    )(where, *x, own[0], other[0])


def late(where, x2, own, other, acc):
    return pl.pallas_call(
        late_kernel,
        out_shape=jax.ShapeDtypeStruct(BLOCK, BF16),
        in_specs=[SMEM, ANY, VMEM, VMEM, ANY],
        out_specs=VMEM,
        scratch_shapes=[
            pltpu.VMEM(BLOCK, BF16),
            pltpu.VMEM(BLOCK, BF16),
            pltpu.VMEM(BLOCK, BF16),
            pltpu.VMEM((ROWS, ROWS), BF16),
            pltpu.VMEM((ROWS, NVIR), F32),
            pltpu.VMEM((8, 128, 128), F32),
            pltpu.SemaphoreType.DMA((1,)),
            pltpu.SemaphoreType.DMA((1,)),
        ],
        cost_estimate=cost(2),
        compiler_params=pltpu.CompilerParams(vmem_limit_bytes=LATE_MIB << 20),
        name="terms_late",
    )(where, x2, own[1], other[1], acc).reshape(16 * OCC_DEV, HALF, NVIR)


def final(where, occ, vir, trials, pieces):
    return pl.pallas_call(
        final_kernel,
        out_shape=jax.ShapeDtypeStruct((NVEC, PAIRS), F32),
        in_specs=[SMEM, SMEM] + [VMEM] * 6,
        out_specs=VMEM,
        compiler_params=pltpu.CompilerParams(vmem_limit_bytes=16 << 20),
        name="final",
    )(where, occ, vir.reshape(1, NVIR), trials, *pieces)


def ring(n, s):
    return [(i, (i + s) % n) for i in range(n)]


def body(fit_rows, trials, occ_energy, vir_energy):
    core = lax.axis_index("c").astype(jnp.int32)
    z = (lax.axis_index("z") + 2 * lax.axis_index("yh")).astype(jnp.int32) & 3
    where = jnp.stack([core, z])
    mine = [lax.dynamic_slice(trials, (half * HALF, z * NVIR), (HALF, NVIR)) for half in (core, 1 - core)]
    mine = jnp.broadcast_to(jnp.concatenate(mine, 1)[None], (NCHIP, HALF, 2 * NVIR))
    own, other, rows = [], [], fit_rows
    first = 0
    for t, steps in enumerate(STEPS):
        count = steps * HALF
        send = rows[first : first + NCHIP * count].reshape(NCHIP, count, PAIRS)
        if t == 0:
            send = jnp.concatenate([send, mine], 2)
        own.append(lax.all_to_all(send, CHIPS, 0, 0, tiled=True))
        first += NCHIP * count
        rows = lax.optimization_barrier(rows)
        other.append(lax.ppermute(own[t], "c", ring(2, 1)))
    x_own, x_send = own[0][:, :, PAIRS : PAIRS + NVIR], own[0][:, :, PAIRS + NVIR :]
    x_other = lax.ppermute(x_send, "c", ring(2, 1))
    x = jnp.concatenate([x_own, x_other])
    x_far = [lax.ppermute(x_own, "yh", ring(2, 1))]
    x_far.append(lax.ppermute(x_other, "z", ring(4, 2)))
    x = [x, lax.ppermute(x, "z", ring(4, 1)), *x_far, lax.ppermute(x, "z", ring(4, 3))]
    acc, x2 = early(where, x, own, other)
    acc = late(where, x2, own, other, acc)
    parts = lax.all_to_all(acc, MOST, 0, 0, tiled=True)
    part = jnp.sum(parts.reshape(NCHIP, 2, 4, HALF, NVIR).astype(F32), (0, 2)).reshape(NVEC, NVIR)
    part = part + lax.ppermute(part, "yh", ring(2, 1))
    pieces = [part] + [lax.ppermute(part, "z", ring(4, s)) for s in (1, 2, 3)]
    place = jnp.stack([lax.axis_index("z"), lax.axis_index(WIDE)]).astype(jnp.int32)
    return final(place, occ_energy, vir_energy, trials, pieces)


def solution(mesh):
    fine = Mesh(mesh.devices.reshape(4, 2, 2, 2, 4), ("x", "yl", "c", "yh", "z"))
    in_specs = (P(NARROW, WIDE), P(None, WIDE), P(), P())
    return jax.shard_map(body, mesh=fine, in_specs=in_specs, out_specs=P(None, WIDE), check_vma=False)
```

time: 141 us -> 135 us (0.957)
  Pallas kernels: 26.1 us -> 17.6 us
  waiting for transfers between devices: 48.6 us -> 56.5 us
  blocking collectives: 32.4 us -> 27.9 us
    pallas_call x1, Pallas kernels: 16.4 us -> 6.2 us  [early(): pl.pallas_call(early_kernel, out_shape=[jax.ShapeDtypeStruct((ROWS, NVIR)...]
    all_to_all x3 -> x2, waiting for transfers between devices: 31.8 us -> 37.9 us  [body(): own.append(lax.all_to_all(send, CHIPS, 0, 0, tiled=True))]
    all_to_all x1, blocking collectives: 32.4 us -> 27.9 us  [body(): parts = lax.all_to_all(acc, MOST, 0, 0, tiled=True)]
    all_to_all x3 -> x2, starting transfers between devices: 13.2 us -> 8.99 us  [body(): own.append(lax.all_to_all(send, CHIPS, 0, 0, tiled=True))]
    ppermute x3 -> x4, starting transfers between devices: 7.1 us -> 11 us  [the longest x1 3.88 us: body(): x_far.append(lax.ppermute(x_other, 'z', ring(4, 2)))]
    ppermute x3 -> x4, waiting for transfers between devices: 6.6 us -> 10.5 us  [the longest x1 9.17 us: body(): x_far.append(lax.ppermute(x_other, 'z', ring(4, 2)))]
    squeeze x2 -> x0, local copies, waits for them, and re-layouts: 3.19 us -> none  [body(): send = blocks[t][t]]
    slice x2 -> x4, local copies, waits for them, and re-layouts: 0.06 us -> 2.98 us  [the longest x3 2.96 us: body(): send = rows[first:first + NCHIP * count].reshape(NCHIP, count, PAIRS)]
  transfers between devices with their start and end apart: 14 -> 13, of which waited for: 10 -> 8; matrix products, arithmetic and copies ran while one was open for 3% -> 1% of each run, Pallas kernels for 12% -> 5%
where the time goes in v8:
time: 135 us; the launch traced here: 134 us
  waiting for transfers between devices  56.5 us (42%)
  blocking collectives  27.9 us (21%)
  starting transfers between devices  26.9 us (20%)
  Pallas kernels  17.6 us (13%)
  local copies, waits for them, and re-layouts  3.92 us (3%)
  other arithmetic  1.53 us (1%)
    all_to_all x2, waiting for transfers between devices, body(): own.append(lax.all_to_all(send, CHIPS, 0, 0, tiled=True))  37.9 us
    all_to_all x1, blocking collectives, body(): parts = lax.all_to_all(acc, MOST, 0, 0, tiled=True)  27.9 us
    pallas_call x1, Pallas kernels, late(): pl.pallas_call(late_kernel, out_shape=jax.ShapeDtypeStruct(BLOCK, BF16),...  10 us
    ppermute x1, waiting for transfers between devices, body(): x_far.append(lax.ppermute(x_other, 'z', ring(4, 2)))  9.17 us
    all_to_all x2, starting transfers between devices, body(): own.append(lax.all_to_all(send, CHIPS, 0, 0, tiled=True))  8.99 us
    pallas_call x1, Pallas kernels, early(): pl.pallas_call(early_kernel, out_shape=[jax.ShapeDtypeStruct((ROWS, NVIR)...  6.2 us
    ppermute x3, waiting for transfers between devices, body(): pieces = [part] + [lax.ppermute(part, 'z', ring(4, s)) for s in (1, 2, 3)]  4.85 us
    ppermute x1, starting transfers between devices, body(): x_far.append(lax.ppermute(x_other, 'z', ring(4, 2)))  3.88 us
  transfers between devices with their start and end apart: 13, of which 8 were waited for; matrix products, arithmetic and copies ran while one was open for 1% of the time, Pallas kernels for 5%

profile of v8, /device:TPU:0, one launch (start us, length us, event | category | flops | bytes accessed | tf_op | source)
XLA Modules:
  0.0 134.4 jit_solution(6807156685860699829)
XLA Ops:
  0.0 2.7 %slice.18 = bf16[256,3072]{1,0:T(8,128)(2,1)} slice(bf16[384,3072]{1,0:T(8,128)(2,1)} %param.4), slice={[128:384], [0:3072]} | slice | bytes 3145728 | tf_op jit(solution)/shard_map/slice | solution.py:224
  2.7 5.4 %all-to-all-start.1 = ((bf16[8,32,3072]{2,1,0:T(8,128)(2,1)}), bf16[8,32,3072]{2,1,0:T(8,128)(2,1)S(1)}, u32[]{:S(2)}, u32[]{:S(2)}) async-start(bf16[8,32,3072]{2,1,0:T(8,128)(2,1)} %bitcast.5), calls=%async_computation.1 | async-start | bytes 3145728 | tf_op jit(solution)/shard_map/all_to_all | solution.py:227
  8.1 0.0 copy-start
  8.1 0.0 slice-start
  8.1 0.9 copy-done
  9.1 0.3 slice-done
  9.4 1.1 pad_maximum_fusion
  10.5 21.4 %all-to-all-done.1.own = bf16[8,32,3072]{2,1,0:T(8,128)(2,1)S(1)} async-done(((bf16[8,32,3072]{2,1,0:T(8,128)(2,1)}), bf16[8,32,3072]{2,1,0:T(8,128)(2,1)S(1)}, u32[]{:S(2)}, u32[]{:S(2)}) %all-to-all-start.1) | async-done | bytes 1572896 | tf_op jit(solution)/shard_map/all_to_all | solution.py:227
  31.9 3.6 %all-to-all-start = ((bf16[8,16,4608]{2,1,0:T(8,128)(2,1)}), bf16[8,16,4608]{2,1,0:T(8,128)(2,1)S(1)}, u32[]{:S(2)}, u32[]{:S(2)}) async-start(bf16[8,16,4608]{2,1,0:T(8,128)(2,1)} %pad_maximum_fusion), calls=%async_computation | async-start | bytes 2359296 | tf_op jit(solution)/shard_map/all_to_all | solution.py:227
  35.4 0.1 collective-permute-start.6
  35.5 16.5 %all-to-all-done.own = bf16[8,16,4608]{2,1,0:T(8,128)(2,1)S(1)} async-done(((bf16[8,16,4608]{2,1,0:T(8,128)(2,1)}), bf16[8,16,4608]{2,1,0:T(8,128)(2,1)S(1)}, u32[]{:S(2)}, u32[]{:S(2)}) %all-to-all-start) | async-done | bytes 1179680 | tf_op jit(solution)/shard_map/all_to_all | solution.py:227
  52.1 0.0 collective-permute-start.5
  52.1 0.6 collective-permute-start
  52.7 2.9 %collective-permute-start.2 = (bf16[8,16,768]{2,1,0:T(8,128)(2,1)S(1)}, bf16[8,16,768]{2,1,0:T(8,128)(2,1)S(1)}, u32[]{:S(2)}, u32[]{:S(2)}) collective-permute-start(bf16[8,16,768]{2,1,0:T(8,128)(2,1)S(1)} %get-tuple-element.9), channel_id=1, source_target_pairs={{0,4},{4,0},{1,5},{5,1},{2,6},{6,2},{3,7},{7,3},{8,12},{12,8},{9,1... | collective-permute-start | bytes 589832 | tf_op jit(solution)/shard_map/ppermute | solution.py:234
  55.6 0.0 collective-permute-done
  55.6 2.0 %collective-permute-start.1 = (bf16[16,16,768]{2,1,0:T(8,128)(2,1)S(1)}, bf16[16,16,768]{2,1,0:T(8,128)(2,1)S(1)}, u32[]{:S(2)}, u32[]{:S(2)}) collective-permute-start(bf16[16,16,768]{2,1,0:T(8,128)(2,1)S(1)} %pad_maximum_fusion.1.x_a), channel_id=1, source_target_pairs={{0,1},{1,2},{2,3},{3,0},{4,5},{5,6},{6,7},{7,4},{8,9},{9,10},{10,1... | collective-permute-start | bytes 1179656 | tf_op jit(solution)/shard_map/ppermute | solution.py:236
  57.6 2.2 %collective-permute-start.4 = (bf16[16,16,768]{2,1,0:T(8,128)(2,1)S(1)}, bf16[16,16,768]{2,1,0:T(8,128)(2,1)S(1)}, u32[]{:S(2)}, u32[]{:S(2)}) collective-permute-start(bf16[16,16,768]{2,1,0:T(8,128)(2,1)S(1)} %pad_maximum_fusion.1.x_a), channel_id=1, source_target_pairs={{0,3},{1,0},{2,1},{3,2},{4,7},{5,4},{6,5},{7,6},{8,11},{9,8},{10,9... | collective-permute-start | bytes 1179656 | tf_op jit(solution)/shard_map/ppermute | solution.py:236
  59.8 1.3 collective-permute-done.2.x_c
  61.1 3.9 %collective-permute-start.3 = (bf16[8,16,768]{2,1,0:T(8,128)(2,1)S(1)}, bf16[8,16,768]{2,1,0:T(8,128)(2,1)S(1)}, u32[]{:S(2)}, u32[]{:S(2)}) collective-permute-start(bf16[8,16,768]{2,1,0:T(8,128)(2,1)S(1)} %collective-permute-done), channel_id=1, source_target_pairs={{0,2},{1,3},{2,0},{3,1},{4,6},{5,7},{6,4},{7,5},{8,10},{9,11},{10,... | collective-permute-start | bytes 589832 | tf_op jit(solution)/shard_map/ppermute | solution.py:235
  65.0 0.1 pad_add_fusion.1.where
  65.0 9.2 %collective-permute-done.3.x_e = bf16[8,16,768]{2,1,0:T(8,128)(2,1)S(1)} collective-permute-done((bf16[8,16,768]{2,1,0:T(8,128)(2,1)S(1)}, bf16[8,16,768]{2,1,0:T(8,128)(2,1)S(1)}, u32[]{:S(2)}, u32[]{:S(2)}) %collective-permute-start.3) | collective-permute-done | bytes 196640 | tf_op jit(solution)/shard_map/ppermute | solution.py:235
  74.2 0.0 collective-permute-done.1.x_b
  74.2 0.0 collective-permute-done.4.x_d
  74.2 0.0 collective-permute-done.5.other
  74.2 6.2 %terms_early.1 = (f32[1024,768]{1,0:T(8,128)}, bf16[16,4,16,768]{3,2,1,0:T(8,128)(2,1)S(1)}) custom-call(s32[2]{0:T(128)S(1)} %pad_add_fusion.1.where, bf16[16,16,768]{2,1,0:T(8,128)(2,1)S(1)} %pad_maximum_fusion.1.x_a, bf16[16,16,768]{2,1,0:T(8,128)(2,1)S(1)} %collective-permute-done.1.x_b, bf16[8,16,768]{2,1,0:T(8,128)(2,1)S(1)} %collective-permute-done.2.x_c, ...), custom_call_target="tpu_custom_call" | custom-call | flops 3221225472 | bytes 6291456 | tf_op jit(solution)/shard_map/terms_early/pallas_call | solution.py:157
  80.4 0.0 collective-permute-done.6.other
  80.4 10.0 %terms_late.1 = bf16[16,4,16,768]{3,2,1,0:T(8,128)(2,1)S(1)} custom-call(s32[2]{0:T(128)S(1)} %pad_add_fusion.1.where, bf16[16,4,16,768]{3,2,1,0:T(8,128)(2,1)S(1)} %get-tuple-element.7.x_in, bf16[8,32,3072]{2,1,0:T(8,128)(2,1)S(1)} %all-to-all-done.1.own, bf16[8,32,3072]{2,1,0:T(8,128)(2,1)} %collective-permute-done.6.other, ...), custom_call_target="tpu_custom_call" | custom-call | flops 6442450944 | bytes 6291456 | tf_op jit(solution)/shard_map/terms_late/pallas_call | solution.py:178
  90.5 27.9 %all_to_all.15 = bf16[64,16,768]{2,1,0:T(8,128)(2,1)S(1)} all-to-all(bf16[64,16,768]{2,1,0:T(8,128)(2,1)S(1)} %bitcast.11), channel_id=1, replica_groups=mesh['x'=4,'yl'=2,'c'=2,'yh'=2,'z'=4] {'x','yl','c','z'}, dimensions={0} | all-to-all | bytes 3145728 | tf_op jit(solution)/shard_map/all_to_all | solution.py:239
  118.4 0.0 copy-start.2
  118.4 0.0 copy-start.1
  118.4 0.2 convert_reduce_fusion
  118.6 3.0 %collective-permute-start.7 = (f32[32,768]{1,0:T(8,128)S(1)}, f32[32,768]{1,0:T(8,128)S(1)}, u32[]{:S(2)}, u32[]{:S(2)}) collective-permute-start(f32[32,768]{1,0:T(8,128)S(1)} %bitcast.14), channel_id=1, source_target_pairs={{0,4},{4,0},{1,5},{5,1},{2,6},{6,2},{3,7},{7,3},{8,12},{12,8},{9,1... | collective-permute-start | bytes 294920 | tf_op jit(solution)/shard_map/ppermute | solution.py:241
  121.6 0.0 copy-done.2
  121.6 3.2 %collective-permute-done.7 = f32[32,768]{1,0:T(8,128)S(1)} collective-permute-done((f32[32,768]{1,0:T(8,128)S(1)}, f32[32,768]{1,0:T(8,128)S(1)}, u32[]{:S(2)}, u32[]{:S(2)}) %collective-permute-start.7) | collective-permute-done | bytes 98336 | tf_op jit(solution)/shard_map/ppermute | solution.py:241
  124.9 0.8 collective-permute-start.10
  125.6 1.3 collective-permute-start.8
  127.0 1.2 collective-permute-start.9
  128.1 0.1 pad_add_fusion.where
  128.2 1.8 %collective-permute-done.10.p_d = f32[32,768]{1,0:T(8,128)S(1)} collective-permute-done((f32[32,768]{1,0:T(8,128)S(1)}, f32[32,768]{1,0:T(8,128)S(1)}, u32[]{:S(2)}, u32[]{:S(2)}) %collective-permute-start.10) | collective-permute-done | bytes 98336 | tf_op jit(solution)/shard_map/ppermute | solution.py:242
  130.1 1.5 %collective-permute-done.8.p_b = f32[32,768]{1,0:T(8,128)S(1)} collective-permute-done((f32[32,768]{1,0:T(8,128)S(1)}, f32[32,768]{1,0:T(8,128)S(1)}, u32[]{:S(2)}, u32[]{:S(2)}) %collective-permute-start.8) | collective-permute-done | bytes 98336 | tf_op jit(solution)/shard_map/ppermute | solution.py:242
  131.6 1.5 %collective-permute-done.9.p_c = f32[32,768]{1,0:T(8,128)S(1)} collective-permute-done((f32[32,768]{1,0:T(8,128)S(1)}, f32[32,768]{1,0:T(8,128)S(1)}, u32[]{:S(2)}, u32[]{:S(2)}) %collective-permute-start.9) | collective-permute-done | bytes 98336 | tf_op jit(solution)/shard_map/ppermute | solution.py:242
  133.1 0.0 copy-done.1
  133.1 1.3 %final.1 = f32[32,3072]{1,0:T(8,128)} custom-call(s32[2]{0:T(128)S(1)} %pad_add_fusion.where, f32[64]{0:T(128)S(1)} %copy-done.1, f32[1,768]{1,0:T(1,128)S(1)} %reshape.19.vir, bf16[32,3072]{1,0:T(8,128)(2,1)S(1)} %copy-done, f32[32,768]{1,0:T(8,128)S(1)} %bitcast_add_fusion.p_a, f32[32,768]{1,0:T(8,128)S(1)} %collective-permute-done.8.p_b, ...), custom_call_target="tpu_custom_call" | custom-call | tf_op jit(solution)/shard_map/final/pallas_call | solution.py:200
  (7 shorter events, 0.1 us)
Async XLA Ops:
  2.7 29.2 %all-to-all-start.1 = ((bf16[8,32,3072]{2,1,0:T(8,128)(2,1)}), bf16[8,32,3072]{2,1,0:T(8,128)(2,1)S(1)}, u32[]{:S(2)}, u32[]{:S(2)}) async-start(bf16[8,32,3072]{2,1,0:T(8,128)(2,1)} %bitcast.5), calls=%async_computation.1 | async-start | bytes 3145728 | tf_op jit(solution)/shard_map/all_to_all | solution.py:227
  8.1 0.9 copy-start
  8.1 1.2 slice-start
  31.9 20.2 %all-to-all-start = ((bf16[8,16,4608]{2,1,0:T(8,128)(2,1)}), bf16[8,16,4608]{2,1,0:T(8,128)(2,1)S(1)}, u32[]{:S(2)}, u32[]{:S(2)}) async-start(bf16[8,16,4608]{2,1,0:T(8,128)(2,1)} %pad_maximum_fusion), calls=%async_computation | async-start | bytes 2359296 | tf_op jit(solution)/shard_map/all_to_all | solution.py:227
  35.4 45.0 %collective-permute-start.6 = (bf16[8,32,3072]{2,1,0:T(8,128)(2,1)S(1)}, bf16[8,32,3072]{2,1,0:T(8,128)(2,1)}, u32[]{:S(2)}, u32[]{:S(2)}) collective-permute-start(bf16[8,32,3072]{2,1,0:T(8,128)(2,1)S(1)} %all-to-all-done.1.own), channel_id=1, source_target_pairs={{0,8},{8,0},{1,9},{9,1},{2,10},{10,2},{3,11},{11,3},{4,12},{12,4},... | collective-permute-start | bytes 4718600 | tf_op jit(solution)/shard_map/ppermute | solution.py:230
  52.1 22.2 %collective-permute-start.5 = (bf16[8,16,4608]{2,1,0:T(8,128)(2,1)S(1)}, bf16[8,16,4608]{2,1,0:T(8,128)(2,1)S(1)}, u32[]{:S(2)}, u32[]{:S(2)}) collective-permute-start(bf16[8,16,4608]{2,1,0:T(8,128)(2,1)S(1)} %all-to-all-done.own), channel_id=1, source_target_pairs={{0,8},{8,0},{1,9},{9,1},{2,10},{10,2},{3,11},{11,3},{4,12},{12,4},... | collective-permute-start | bytes 3538952 | tf_op jit(solution)/shard_map/ppermute | solution.py:230
  52.1 3.5 %collective-permute-start = (bf16[8,16,768]{2,1,0:T(8,128)(2,1)S(1)}, bf16[8,16,768]{2,1,0:T(8,128)(2,1)S(1)}, u32[]{:S(2)}, u32[]{:S(2)}) collective-permute-start(bf16[8,16,768]{2,1,0:T(8,128)(2,1)S(1)} %get-tuple-element.10), channel_id=1, source_target_pairs={{0,8},{8,0},{1,9},{9,1},{2,10},{10,2},{3,11},{11,3},{4,12},{12,4},... | collective-permute-start | bytes 589832 | tf_op jit(solution)/shard_map/ppermute | solution.py:232
  52.7 8.4 %collective-permute-start.2 = (bf16[8,16,768]{2,1,0:T(8,128)(2,1)S(1)}, bf16[8,16,768]{2,1,0:T(8,128)(2,1)S(1)}, u32[]{:S(2)}, u32[]{:S(2)}) collective-permute-start(bf16[8,16,768]{2,1,0:T(8,128)(2,1)S(1)} %get-tuple-element.9), channel_id=1, source_target_pairs={{0,4},{4,0},{1,5},{5,1},{2,6},{6,2},{3,7},{7,3},{8,12},{12,8},{9,1... | collective-permute-start | bytes 589832 | tf_op jit(solution)/shard_map/ppermute | solution.py:234
  55.6 18.6 %collective-permute-start.1 = (bf16[16,16,768]{2,1,0:T(8,128)(2,1)S(1)}, bf16[16,16,768]{2,1,0:T(8,128)(2,1)S(1)}, u32[]{:S(2)}, u32[]{:S(2)}) collective-permute-start(bf16[16,16,768]{2,1,0:T(8,128)(2,1)S(1)} %pad_maximum_fusion.1.x_a), channel_id=1, source_target_pairs={{0,1},{1,2},{2,3},{3,0},{4,5},{5,6},{6,7},{7,4},{8,9},{9,10},{10,1... | collective-permute-start | bytes 1179656 | tf_op jit(solution)/shard_map/ppermute | solution.py:236
  57.6 16.6 %collective-permute-start.4 = (bf16[16,16,768]{2,1,0:T(8,128)(2,1)S(1)}, bf16[16,16,768]{2,1,0:T(8,128)(2,1)S(1)}, u32[]{:S(2)}, u32[]{:S(2)}) collective-permute-start(bf16[16,16,768]{2,1,0:T(8,128)(2,1)S(1)} %pad_maximum_fusion.1.x_a), channel_id=1, source_target_pairs={{0,3},{1,0},{2,1},{3,2},{4,7},{5,4},{6,5},{7,6},{8,11},{9,8},{10,9... | collective-permute-start | bytes 1179656 | tf_op jit(solution)/shard_map/ppermute | solution.py:236
  61.1 13.1 %collective-permute-start.3 = (bf16[8,16,768]{2,1,0:T(8,128)(2,1)S(1)}, bf16[8,16,768]{2,1,0:T(8,128)(2,1)S(1)}, u32[]{:S(2)}, u32[]{:S(2)}) collective-permute-start(bf16[8,16,768]{2,1,0:T(8,128)(2,1)S(1)} %collective-permute-done), channel_id=1, source_target_pairs={{0,2},{1,3},{2,0},{3,1},{4,6},{5,7},{6,4},{7,5},{8,10},{9,11},{10,... | collective-permute-start | bytes 589832 | tf_op jit(solution)/shard_map/ppermute | solution.py:235
  118.4 3.2 %copy-start.2 = (f32[768]{0:T(1024)S(1)}, f32[768]{0:T(1024)}, u32[]{:S(2)}) copy-start(f32[768]{0:T(1024)} %param.7) | copy-start | bytes 9220
  118.4 14.7 %copy-start.1 = (f32[64]{0:T(128)S(1)}, f32[64]{0:T(128)}, u32[]{:S(2)}) copy-start(f32[64]{0:T(128)} %occ.1) | copy-start | bytes 772
  118.6 6.2 %collective-permute-start.7 = (f32[32,768]{1,0:T(8,128)S(1)}, f32[32,768]{1,0:T(8,128)S(1)}, u32[]{:S(2)}, u32[]{:S(2)}) collective-permute-start(f32[32,768]{1,0:T(8,128)S(1)} %bitcast.14), channel_id=1, source_target_pairs={{0,4},{4,0},{1,5},{5,1},{2,6},{6,2},{3,7},{7,3},{8,12},{12,8},{9,1... | collective-permute-start | bytes 294920 | tf_op jit(solution)/shard_map/ppermute | solution.py:241
  124.9 5.2 %collective-permute-start.10 = (f32[32,768]{1,0:T(8,128)S(1)}, f32[32,768]{1,0:T(8,128)S(1)}, u32[]{:S(2)}, u32[]{:S(2)}) collective-permute-start(f32[32,768]{1,0:T(8,128)S(1)} %bitcast_add_fusion.p_a), channel_id=1, source_target_pairs={{0,3},{1,0},{2,1},{3,2},{4,7},{5,4},{6,5},{7,6},{8,11},{9,8},{10,9... | collective-permute-start | bytes 294920 | tf_op jit(solution)/shard_map/ppermute | solution.py:242
  125.6 6.0 %collective-permute-start.8 = (f32[32,768]{1,0:T(8,128)S(1)}, f32[32,768]{1,0:T(8,128)S(1)}, u32[]{:S(2)}, u32[]{:S(2)}) collective-permute-start(f32[32,768]{1,0:T(8,128)S(1)} %bitcast_add_fusion.p_a), channel_id=1, source_target_pairs={{0,1},{1,2},{2,3},{3,0},{4,5},{5,6},{6,7},{7,4},{8,9},{9,10},{10,1... | collective-permute-start | bytes 294920 | tf_op jit(solution)/shard_map/ppermute | solution.py:242
  127.0 6.1 %collective-permute-start.9 = (f32[32,768]{1,0:T(8,128)S(1)}, f32[32,768]{1,0:T(8,128)S(1)}, u32[]{:S(2)}, u32[]{:S(2)}) collective-permute-start(f32[32,768]{1,0:T(8,128)S(1)} %bitcast_add_fusion.p_a), channel_id=1, source_target_pairs={{0,2},{1,3},{2,0},{3,1},{4,6},{5,7},{6,4},{7,5},{8,10},{9,11},{10,... | collective-permute-start | bytes 294920 | tf_op jit(solution)/shard_map/ppermute | solution.py:242

commit v9 on v8

--- a/solution.py
+++ b/solution.py
@@ -12,7 +12,7 @@
 OCC_DEV = 4
 PAIRS = OCC_DEV * NVIR
 HALF = 16
-STEPS = (1, 2)
+STEPS = (2, 1)
 ROWS = NOCC * HALF
 
 F32 = jnp.float32
@@ -44,11 +44,21 @@
     return ref[start // 64 : (start + count) // 64].reshape(count, NVIR)
 
 
-def take_rows(b2, own, other, step):
+def get_rows(b2, own, other, step, sems):
+    copies = []
+    for rel, src in enumerate((own, other)):
+        for q in range(OCC_DEV):
+            there = b2.at[pl.ds(rel * NCHIP, NCHIP), q]
+            here = src.at[:, pl.ds(step * HALF, HALF), pl.ds(q * NVIR, NVIR)]
+            copies.append(pltpu.make_async_copy(here, there, sems.at[step, rel, q]))
+    return copies
+
+
+def take_rows(b2, own, other):
     for rel, src in enumerate((own, other)):
         for chip in range(NCHIP):
             for q in range(OCC_DEV):
-                b2[rel * NCHIP + chip, q] = src[chip, step * HALF : (step + 1) * HALF, q * NVIR : (q + 1) * NVIR]
+                b2[rel * NCHIP + chip, q] = src[chip, :, q * NVIR : (q + 1) * NVIR]
 
 
 def contract_first(x2, b2, d, diag):
@@ -87,21 +97,33 @@
     return acc[g * 128 : (g + 1) * 128, :] - jnp.dot(fit, rows_of(b2, g * 128, 128), preferred_element_type=F32)
 
 
-def early_kernel(where, x_a, x_b, x_c, x_e, x_d, own, other, out, x_out, x2, b2, d, acc, diag, xs, os):
-    for s, low, high in ((0, x_a, x_a), (1, x_b, x_b), (2, x_c, x_e), (3, x_d, x_d)):
+def early_kernel(where, x_a, x_b, x_c, x_d, own, other, out, x_out, x2, b_a, b_b, d, acc, diag, xs, bs, os):
+    rows0 = get_rows(b_a, own, other, 0, bs)
+    rows1 = get_rows(b_b, own, other, 1, bs)
+    for cp in rows0:
+        cp.start()
+    for s, ref in enumerate((x_a, x_b, x_c, x_d)):
         q = (where[1] - s) & 3
-        for k in range(NCHIP):
-            x2[k, q] = low[k]
-            x2[NCHIP + k, q] = high[high.shape[0] - NCHIP + k]
+        for k in range(16):
+            x2[k, q] = ref[k]
+    for cp in rows0:
+        cp.wait()
+    for cp in rows1:
+        cp.start()
     keep_x = pltpu.make_async_copy(x2, x_out, xs.at[0])
     keep_x.start()
-    take_rows(b2, own, other, 0)
-    fit = contract_first(x2, b2, d, diag)
-    contract_second(b2, d, acc, True)
+    fit = contract_first(x2, b_a, d, diag)
+    contract_second(b_a, d, acc, True)
+    for g in range(8):
+        acc[g * 128 : (g + 1) * 128, :] = less_coulomb(b_a, acc, fit, g)
+    for cp in rows1:
+        cp.wait()
+    fit = contract_first(x2, b_b, d, diag)
+    contract_second(b_b, d, acc, False)
     puts = []
     for half in range(2):
         for g in range(half * 4, half * 4 + 4):
-            acc[g * 128 : (g + 1) * 128, :] = less_coulomb(b2, acc, fit, g)
+            acc[g * 128 : (g + 1) * 128, :] = less_coulomb(b_b, acc, fit, g)
         rows = pl.ds(half * 512, 512)
         puts.append(pltpu.make_async_copy(acc.at[rows], out.at[rows], os.at[half]))
         puts[-1].start()
@@ -110,24 +132,19 @@
         cp.wait()
 
 
-def late_kernel(where, x_in, own, other, acc_in, out, x2, b_a, b_b, d, acc, diag, xs, os):
+def late_kernel(where, x_in, own, other, acc_in, out, x2, b2, d, acc, diag, xs, os):
     c = where[0]
     get_x = pltpu.make_async_copy(x_in, x2, xs.at[0])
     get_x.start()
-    take_rows(b_a, own, other, 0)
-    take_rows(b_b, own, other, 1)
+    take_rows(b2, own, other)
     get_x.wait()
     get_acc = pltpu.make_async_copy(acc_in, acc, os.at[0])
     get_acc.start()
-    fit_a = contract_first(x2, b_a, d, diag)
+    fit = contract_first(x2, b2, d, diag)
     get_acc.wait()
-    contract_second(b_a, d, acc, False)
+    contract_second(b2, d, acc, False)
     for g in range(8):
-        acc[g * 128 : (g + 1) * 128, :] = less_coulomb(b_a, acc, fit_a, g)
-    fit_b = contract_first(x2, b_b, d, diag)
-    contract_second(b_b, d, acc, False)
-    for g in range(8):
-        value = less_coulomb(b_b, acc, fit_b, g).astype(BF16).reshape(2, OCC_DEV, HALF, NVIR)
+        value = less_coulomb(b2, acc, fit, g).astype(BF16).reshape(2, OCC_DEV, HALF, NVIR)
         for k in range(2):
             rel, chip = g // 4, (g % 4) * 2 + k
             out[chip * 2 + (c ^ rel)] = value[k]
@@ -142,8 +159,8 @@
 
 
 VMEM = pl.BlockSpec(memory_space=pltpu.VMEM)
-LATE_MIB = 46
-EARLY_MIB = 46
+LATE_MIB = 50
+EARLY_MIB = 50
 SMEM = pl.BlockSpec(memory_space=pltpu.SMEM)
 ANY = pl.BlockSpec(memory_space=pl.ANY)
 BLOCK = (16, OCC_DEV, HALF, NVIR)
@@ -157,18 +174,20 @@
     return pl.pallas_call(
         early_kernel,
         out_shape=[jax.ShapeDtypeStruct((ROWS, NVIR), F32), jax.ShapeDtypeStruct(BLOCK, BF16)],
-        in_specs=[SMEM] + [VMEM] * 7,
+        in_specs=[SMEM] + [VMEM] * 4 + [ANY] * 2,
         out_specs=[ANY, ANY],
         scratch_shapes=[
+            pltpu.VMEM(BLOCK, BF16),
             pltpu.VMEM(BLOCK, BF16),
             pltpu.VMEM(BLOCK, BF16),
             pltpu.VMEM((ROWS, ROWS), BF16),
             pltpu.VMEM((ROWS, NVIR), F32),
             pltpu.VMEM((8, 128, 128), F32),
             pltpu.SemaphoreType.DMA((1,)),
+            pltpu.SemaphoreType.DMA((2, 2, 4)),
             pltpu.SemaphoreType.DMA((2,)),
         ],
-        cost_estimate=cost(1),
+        cost_estimate=cost(2),
         compiler_params=pltpu.CompilerParams(vmem_limit_bytes=EARLY_MIB << 20),
         name="terms_early",
     )(where, *x, own[0], other[0])
@@ -183,14 +202,13 @@
         scratch_shapes=[
             pltpu.VMEM(BLOCK, BF16),
             pltpu.VMEM(BLOCK, BF16),
-            pltpu.VMEM(BLOCK, BF16),
             pltpu.VMEM((ROWS, ROWS), BF16),
             pltpu.VMEM((ROWS, NVIR), F32),
             pltpu.VMEM((8, 128, 128), F32),
             pltpu.SemaphoreType.DMA((1,)),
             pltpu.SemaphoreType.DMA((1,)),
         ],
-        cost_estimate=cost(2),
+        cost_estimate=cost(1),
         compiler_params=pltpu.CompilerParams(vmem_limit_bytes=LATE_MIB << 20),
         name="terms_late",
     )(where, x2, own[1], other[1], acc).reshape(16 * OCC_DEV, HALF, NVIR)
@@ -213,27 +231,24 @@
 
 def body(fit_rows, trials, occ_energy, vir_energy):
     core = lax.axis_index("c").astype(jnp.int32)
-    z = (lax.axis_index("z") + 2 * lax.axis_index("yh")).astype(jnp.int32) & 3
+    z = lax.axis_index("z").astype(jnp.int32)
     where = jnp.stack([core, z])
     mine = [lax.dynamic_slice(trials, (half * HALF, z * NVIR), (HALF, NVIR)) for half in (core, 1 - core)]
     mine = jnp.broadcast_to(jnp.concatenate(mine, 1)[None], (NCHIP, HALF, 2 * NVIR))
+    both = lax.all_to_all(mine, CHIPS, 0, 0, tiled=True)
     own, other, rows = [], [], fit_rows
     first = 0
     for t, steps in enumerate(STEPS):
         count = steps * HALF
         send = rows[first : first + NCHIP * count].reshape(NCHIP, count, PAIRS)
-        if t == 0:
-            send = jnp.concatenate([send, mine], 2)
         own.append(lax.all_to_all(send, CHIPS, 0, 0, tiled=True))
         first += NCHIP * count
         rows = lax.optimization_barrier(rows)
         other.append(lax.ppermute(own[t], "c", ring(2, 1)))
-    x_own, x_send = own[0][:, :, PAIRS : PAIRS + NVIR], own[0][:, :, PAIRS + NVIR :]
+    x_own, x_send = both[:, :, :NVIR], both[:, :, NVIR:]
     x_other = lax.ppermute(x_send, "c", ring(2, 1))
-    x = jnp.concatenate([x_own, x_other])
-    x_far = [lax.ppermute(x_own, "yh", ring(2, 1))]
-    x_far.append(lax.ppermute(x_other, "z", ring(4, 2)))
-    x = [x, lax.ppermute(x, "z", ring(4, 1)), *x_far, lax.ppermute(x, "z", ring(4, 3))]
+    x = [jnp.concatenate([x_own, x_other])]
+    x = x + [lax.ppermute(x[0], "z", ring(4, s)) for s in (1, 2, 3)]
     acc, x2 = early(where, x, own, other)
     acc = late(where, x2, own, other, acc)
     parts = lax.all_to_all(acc, MOST, 0, 0, tiled=True)

time: 135 us -> 141 us (1.044)
  blocking collectives: 27.9 us -> 31.7 us
  local copies, waits for them, and re-layouts: 3.92 us -> 6.72 us
  Pallas kernels: 17.6 us -> 19.4 us
    all_to_all x2, waiting for transfers between devices: 37.9 us -> 28.1 us  [body(): own.append(lax.all_to_all(send, CHIPS, 0, 0, tiled=True))]
    all_to_all x0 -> x1, waiting for transfers between devices: none -> 6.86 us  [body(): both = lax.all_to_all(mine, CHIPS, 0, 0, tiled=True)]
    pallas_call x1, Pallas kernels: 6.2 us -> 11.6 us  [early(): pl.pallas_call(early_kernel, out_shape=[jax.ShapeDtypeStruct((ROWS, NVIR)...]
    ppermute x4 -> x3, starting transfers between devices: 11 us -> 6.58 us  [body(): x = x + [lax.ppermute(x[0], 'z', ring(4, s)) for s in (1, 2, 3)]]
    all_to_all x1, blocking collectives: 27.9 us -> 31.7 us  [body(): parts = lax.all_to_all(acc, MOST, 0, 0, tiled=True)]
    pallas_call x1, Pallas kernels: 10 us -> 6.41 us  [late(): pl.pallas_call(late_kernel, out_shape=jax.ShapeDtypeStruct(BLOCK, BF16),...]
    all_to_all x0 -> x1, starting transfers between devices: none -> 3.45 us  [body(): both = lax.all_to_all(mine, CHIPS, 0, 0, tiled=True)]
    ppermute x4 -> x3, waiting for transfers between devices: 10.5 us -> 12.3 us  [body(): x = x + [lax.ppermute(x[0], 'z', ring(4, s)) for s in (1, 2, 3)]]
  transfers between devices with their start and end apart: 13 -> 13, of which waited for: 8 -> 10; matrix products, arithmetic and copies ran while one was open for 1% -> 2% of each run, Pallas kernels for 5% -> 8%
where the time goes in v9:
time: 141 us; the launch traced here: 140 us
  waiting for transfers between devices  55.7 us (40%)
  blocking collectives  31.7 us (22%)
  starting transfers between devices  26.1 us (19%)
  Pallas kernels  19.4 us (14%)
  local copies, waits for them, and re-layouts  6.72 us (5%)
    all_to_all x1, blocking collectives, body(): parts = lax.all_to_all(acc, MOST, 0, 0, tiled=True)  31.7 us
    all_to_all x2, waiting for transfers between devices, body(): own.append(lax.all_to_all(send, CHIPS, 0, 0, tiled=True))  28.1 us
    ppermute x3, waiting for transfers between devices, body(): x = x + [lax.ppermute(x[0], 'z', ring(4, s)) for s in (1, 2, 3)]  12.3 us
    pallas_call x1, Pallas kernels, early(): pl.pallas_call(early_kernel, out_shape=[jax.ShapeDtypeStruct((ROWS, NVIR)...  11.6 us
    all_to_all x2, starting transfers between devices, body(): own.append(lax.all_to_all(send, CHIPS, 0, 0, tiled=True))  9.1 us
    all_to_all x1, waiting for transfers between devices, body(): both = lax.all_to_all(mine, CHIPS, 0, 0, tiled=True)  6.86 us
    ppermute x3, starting transfers between devices, body(): x = x + [lax.ppermute(x[0], 'z', ring(4, s)) for s in (1, 2, 3)]  6.58 us
    pallas_call x1, Pallas kernels, late(): pl.pallas_call(late_kernel, out_shape=jax.ShapeDtypeStruct(BLOCK, BF16),...  6.41 us
  transfers between devices with their start and end apart: 13, of which 10 were waited for; matrix products, arithmetic and copies ran while one was open for 2% of the time, Pallas kernels for 8%

profile of v9, /device:TPU:0, one launch (start us, length us, event | category | flops | bytes accessed | tf_op | source)
XLA Modules:
  0.0 140.1 jit_solution(5253298360827240424)
XLA Ops:
  0.0 2.7 %slice.14 = bf16[256,3072]{1,0:T(8,128)(2,1)} slice(bf16[384,3072]{1,0:T(8,128)(2,1)} %param.4), slice={[0:256], [0:3072]} | slice | bytes 3145728 | tf_op jit(solution)/shard_map/slice | solution.py:243
  2.7 0.0 copy-start
  2.7 5.6 %all-to-all-start.1 = ((bf16[8,32,3072]{2,1,0:T(8,128)(2,1)}), bf16[8,32,3072]{2,1,0:T(8,128)(2,1)}, u32[]{:S(2)}, u32[]{:S(2)}) async-start(bf16[8,32,3072]{2,1,0:T(8,128)(2,1)} %bitcast.3), calls=%async_computation.1 | async-start | bytes 3145728 | tf_op jit(solution)/shard_map/all_to_all | solution.py:244
  8.2 23.9 %all-to-all-done.1.own = bf16[8,32,3072]{2,1,0:T(8,128)(2,1)} async-done(((bf16[8,32,3072]{2,1,0:T(8,128)(2,1)}), bf16[8,32,3072]{2,1,0:T(8,128)(2,1)}, u32[]{:S(2)}, u32[]{:S(2)}) %all-to-all-start.1) | async-done | bytes 1572896 | tf_op jit(solution)/shard_map/all_to_all | solution.py:244
  32.1 0.0 collective-permute-start.4
  32.1 0.0 copy-done
  32.1 0.8 broadcast_in_dim.2
  32.9 3.5 %all-to-all-start = ((bf16[8,16,1536]{2,1,0:T(8,128)(2,1)}), bf16[8,16,1536]{2,1,0:T(8,128)(2,1)S(1)}, u32[]{:S(2)}, u32[]{:S(2)}) async-start(bf16[8,16,1536]{2,1,0:T(8,128)(2,1)} %broadcast_in_dim.2), calls=%async_computation | async-start | bytes 786432 | tf_op jit(solution)/shard_map/all_to_all | solution.py:238
  36.4 2.1 %slice.18 = bf16[128,3072]{1,0:T(8,128)(2,1)} slice(bf16[384,3072]{1,0:T(8,128)(2,1)} %param.4), slice={[256:384], [0:3072]} | slice | bytes 1572864 | tf_op jit(solution)/shard_map/slice | solution.py:243
  38.4 6.9 %all-to-all-done = bf16[8,16,1536]{2,1,0:T(8,128)(2,1)S(1)} async-done(((bf16[8,16,1536]{2,1,0:T(8,128)(2,1)}), bf16[8,16,1536]{2,1,0:T(8,128)(2,1)S(1)}, u32[]{:S(2)}, u32[]{:S(2)}) %all-to-all-start) | async-done | bytes 393248 | tf_op jit(solution)/shard_map/all_to_all | solution.py:238
  45.3 3.5 %all-to-all-start.2 = ((bf16[8,16,3072]{2,1,0:T(8,128)(2,1)}), bf16[8,16,3072]{2,1,0:T(8,128)(2,1)S(1)}, u32[]{:S(2)}, u32[]{:S(2)}) async-start(bf16[8,16,3072]{2,1,0:T(8,128)(2,1)} %bitcast.4), calls=%async_computation.2 | async-start | bytes 1572864 | tf_op jit(solution)/shard_map/all_to_all | solution.py:244
  48.9 0.1 collective-permute-start
  49.0 1.4 %collective-permute-done = bf16[8,16,768]{2,1,0:T(8,128)(2,1)S(1)} collective-permute-done((bf16[8,16,768]{2,1,0:T(8,128)(2,1)S(1)}, bf16[8,16,768]{2,1,0:T(8,128)(2,1)S(1)}, u32[]{:S(2)}, u32[]{:S(2)}) %collective-permute-start) | collective-permute-done | bytes 196640 | tf_op jit(solution)/shard_map/ppermute | solution.py:249
  50.5 2.0 %collective-permute-start.1 = (bf16[16,16,768]{2,1,0:T(8,128)(2,1)S(1)}, bf16[16,16,768]{2,1,0:T(8,128)(2,1)S(1)}, u32[]{:S(2)}, u32[]{:S(2)}) collective-permute-start(bf16[16,16,768]{2,1,0:T(8,128)(2,1)S(1)} %pad_maximum_fusion.x_a), channel_id=1, source_target_pairs={{0,1},{1,2},{2,3},{3,0},{4,5},{5,6},{6,7},{7,4},{8,9},{9,10},{10,1... | collective-permute-start | bytes 1179656 | tf_op jit(solution)/shard_map/ppermute | solution.py:251
  52.4 3.6 %collective-permute-start.2 = (bf16[16,16,768]{2,1,0:T(8,128)(2,1)S(1)}, bf16[16,16,768]{2,1,0:T(8,128)(2,1)S(1)}, u32[]{:S(2)}, u32[]{:S(2)}) collective-permute-start(bf16[16,16,768]{2,1,0:T(8,128)(2,1)S(1)} %pad_maximum_fusion.x_a), channel_id=1, source_target_pairs={{0,2},{1,3},{2,0},{3,1},{4,6},{5,7},{6,4},{7,5},{8,10},{9,11},{10,... | collective-permute-start | bytes 1179656 | tf_op jit(solution)/shard_map/ppermute | solution.py:251
  56.0 1.0 collective-permute-start.3
  57.0 4.2 %all-to-all-done.2.own = bf16[8,16,3072]{2,1,0:T(8,128)(2,1)S(1)} async-done(((bf16[8,16,3072]{2,1,0:T(8,128)(2,1)}), bf16[8,16,3072]{2,1,0:T(8,128)(2,1)S(1)}, u32[]{:S(2)}, u32[]{:S(2)}) %all-to-all-start.2) | async-done | bytes 786464 | tf_op jit(solution)/shard_map/all_to_all | solution.py:244
  61.2 0.0 collective-permute-start.5
  61.2 0.1 pad_add_fusion.1.where
  61.3 2.7 %collective-permute-done.1.x_b = bf16[16,16,768]{2,1,0:T(8,128)(2,1)S(1)} collective-permute-done((bf16[16,16,768]{2,1,0:T(8,128)(2,1)S(1)}, bf16[16,16,768]{2,1,0:T(8,128)(2,1)S(1)}, u32[]{:S(2)}, u32[]{:S(2)}) %collective-permute-start.1) | collective-permute-done | bytes 393248 | tf_op jit(solution)/shard_map/ppermute | solution.py:251
  64.0 9.6 %collective-permute-done.2.x_c = bf16[16,16,768]{2,1,0:T(8,128)(2,1)S(1)} collective-permute-done((bf16[16,16,768]{2,1,0:T(8,128)(2,1)S(1)}, bf16[16,16,768]{2,1,0:T(8,128)(2,1)S(1)}, u32[]{:S(2)}, u32[]{:S(2)}) %collective-permute-start.2) | collective-permute-done | bytes 393248 | tf_op jit(solution)/shard_map/ppermute | solution.py:251
  73.6 0.0 collective-permute-done.3.x_d
  73.6 0.0 collective-permute-done.4.other
  73.6 11.6 %terms_early.1 = (f32[1024,768]{1,0:T(8,128)}, bf16[16,4,16,768]{3,2,1,0:T(8,128)(2,1)S(1)}) custom-call(s32[2]{0:T(128)S(1)} %pad_add_fusion.1.where, bf16[16,16,768]{2,1,0:T(8,128)(2,1)S(1)} %pad_maximum_fusion.x_a, bf16[16,16,768]{2,1,0:T(8,128)(2,1)S(1)} %collective-permute-done.1.x_b, bf16[16,16,768]{2,1,0:T(8,128)(2,1)S(1)} %collective-permute-done.2.x_c, ...), custom_call_target="tpu_custom_call" | custom-call | flops 6442450944 | bytes 6291456 | tf_op jit(solution)/shard_map/terms_early/pallas_call | solution.py:174
  85.2 0.0 copy-start.2
  85.2 1.1 copy-done.2
  86.4 0.0 collective-permute-done.5.other
  86.4 6.4 %terms_late.1 = bf16[16,4,16,768]{3,2,1,0:T(8,128)(2,1)S(1)} custom-call(s32[2]{0:T(128)S(1)} %pad_add_fusion.1.where, bf16[16,4,16,768]{3,2,1,0:T(8,128)(2,1)} %copy-done.2, bf16[8,16,3072]{2,1,0:T(8,128)(2,1)S(1)} %all-to-all-done.2.own, bf16[8,16,3072]{2,1,0:T(8,128)(2,1)S(1)} %collective-permute-done.5.other, f32[1024,768]{1,0:T(8,128)} %get-tuple-element.8.acc_in), custom_call_target="tpu_custom_call" | custom-call | flops 3221225472 | bytes 6291456 | tf_op jit(solution)/shard_map/terms_late/pallas_call | solution.py:197
  92.8 31.7 %all_to_all.20 = bf16[64,16,768]{2,1,0:T(8,128)(2,1)S(1)} all-to-all(bf16[64,16,768]{2,1,0:T(8,128)(2,1)S(1)} %bitcast.10), channel_id=1, replica_groups=mesh['x'=4,'yl'=2,'c'=2,'yh'=2,'z'=4] {'x','yl','c','z'}, dimensions={0} | all-to-all | bytes 3145728 | tf_op jit(solution)/shard_map/all_to_all | solution.py:254
  124.5 0.0 copy-start.3
  124.5 0.0 copy-start.1
  124.5 0.2 convert_reduce_fusion
  124.7 3.0 %collective-permute-start.6 = (f32[32,768]{1,0:T(8,128)S(1)}, f32[32,768]{1,0:T(8,128)S(1)}, u32[]{:S(2)}, u32[]{:S(2)}) collective-permute-start(f32[32,768]{1,0:T(8,128)S(1)} %bitcast.12), channel_id=1, source_target_pairs={{0,4},{4,0},{1,5},{5,1},{2,6},{6,2},{3,7},{7,3},{8,12},{12,8},{9,1... | collective-permute-start | bytes 294920 | tf_op jit(solution)/shard_map/ppermute | solution.py:256
  127.7 0.0 copy-done.3
  127.7 3.2 %collective-permute-done.6 = f32[32,768]{1,0:T(8,128)S(1)} collective-permute-done((f32[32,768]{1,0:T(8,128)S(1)}, f32[32,768]{1,0:T(8,128)S(1)}, u32[]{:S(2)}, u32[]{:S(2)}) %collective-permute-start.6) | collective-permute-done | bytes 98336 | tf_op jit(solution)/shard_map/ppermute | solution.py:256
  130.9 0.7 collective-permute-start.7
  131.7 1.5 %collective-permute-start.8 = (f32[32,768]{1,0:T(8,128)S(1)}, f32[32,768]{1,0:T(8,128)S(1)}, u32[]{:S(2)}, u32[]{:S(2)}) collective-permute-start(f32[32,768]{1,0:T(8,128)S(1)} %bitcast_add_fusion.p_a), channel_id=1, source_target_pairs={{0,2},{1,3},{2,0},{3,1},{4,6},{5,7},{6,4},{7,5},{8,10},{9,11},{10,... | collective-permute-start | bytes 294920 | tf_op jit(solution)/shard_map/ppermute | solution.py:257
  133.2 1.7 %collective-permute-start.9 = (f32[32,768]{1,0:T(8,128)S(1)}, f32[32,768]{1,0:T(8,128)S(1)}, u32[]{:S(2)}, u32[]{:S(2)}) collective-permute-start(f32[32,768]{1,0:T(8,128)S(1)} %bitcast_add_fusion.p_a), channel_id=1, source_target_pairs={{0,3},{1,0},{2,1},{3,2},{4,7},{5,4},{6,5},{7,6},{8,11},{9,8},{10,9... | collective-permute-start | bytes 294920 | tf_op jit(solution)/shard_map/ppermute | solution.py:257
  134.8 0.1 pad_add_fusion.where
  134.9 1.9 %collective-permute-done.7.p_b = f32[32,768]{1,0:T(8,128)S(1)} collective-permute-done((f32[32,768]{1,0:T(8,128)S(1)}, f32[32,768]{1,0:T(8,128)S(1)}, u32[]{:S(2)}, u32[]{:S(2)}) %collective-permute-start.7) | collective-permute-done | bytes 98336 | tf_op jit(solution)/shard_map/ppermute | solution.py:257
  136.8 1.0 collective-permute-done.8.p_c
  137.9 0.9 collective-permute-done.9.p_d
  138.7 0.0 copy-done.1
  138.7 1.3 final.1
  (6 shorter events, 0.1 us)
Async XLA Ops:
  2.7 29.4 %copy-start = (bf16[32,3072]{1,0:T(8,128)(2,1)S(1)}, bf16[32,3072]{1,0:T(8,128)(2,1)}, u32[]{:S(2)}) copy-start(bf16[32,3072]{1,0:T(8,128)(2,1)} %trials.1) | copy-start | bytes 589828
  2.7 29.4 %all-to-all-start.1 = ((bf16[8,32,3072]{2,1,0:T(8,128)(2,1)}), bf16[8,32,3072]{2,1,0:T(8,128)(2,1)}, u32[]{:S(2)}, u32[]{:S(2)}) async-start(bf16[8,32,3072]{2,1,0:T(8,128)(2,1)} %bitcast.3), calls=%async_computation.1 | async-start | bytes 3145728 | tf_op jit(solution)/shard_map/all_to_all | solution.py:244
  32.1 41.5 %collective-permute-start.4 = (bf16[8,32,3072]{2,1,0:T(8,128)(2,1)}, bf16[8,32,3072]{2,1,0:T(8,128)(2,1)}, u32[]{:S(2)}, u32[]{:S(2)}) collective-permute-start(bf16[8,32,3072]{2,1,0:T(8,128)(2,1)} %all-to-all-done.1.own), channel_id=1, source_target_pairs={{0,8},{8,0},{1,9},{9,1},{2,10},{10,2},{3,11},{11,3},{4,12},{12,4},... | collective-permute-start | bytes 4718600 | tf_op jit(solution)/shard_map/ppermute | solution.py:247
  32.9 12.4 %all-to-all-start = ((bf16[8,16,1536]{2,1,0:T(8,128)(2,1)}), bf16[8,16,1536]{2,1,0:T(8,128)(2,1)S(1)}, u32[]{:S(2)}, u32[]{:S(2)}) async-start(bf16[8,16,1536]{2,1,0:T(8,128)(2,1)} %broadcast_in_dim.2), calls=%async_computation | async-start | bytes 786432 | tf_op jit(solution)/shard_map/all_to_all | solution.py:238
  45.3 15.9 %all-to-all-start.2 = ((bf16[8,16,3072]{2,1,0:T(8,128)(2,1)}), bf16[8,16,3072]{2,1,0:T(8,128)(2,1)S(1)}, u32[]{:S(2)}, u32[]{:S(2)}) async-start(bf16[8,16,3072]{2,1,0:T(8,128)(2,1)} %bitcast.4), calls=%async_computation.2 | async-start | bytes 1572864 | tf_op jit(solution)/shard_map/all_to_all | solution.py:244
  48.9 1.5 %collective-permute-start = (bf16[8,16,768]{2,1,0:T(8,128)(2,1)S(1)}, bf16[8,16,768]{2,1,0:T(8,128)(2,1)S(1)}, u32[]{:S(2)}, u32[]{:S(2)}) collective-permute-start(bf16[8,16,768]{2,1,0:T(8,128)(2,1)S(1)} %get-tuple-element.10), channel_id=1, source_target_pairs={{0,8},{8,0},{1,9},{9,1},{2,10},{10,2},{3,11},{11,3},{4,12},{12,4},... | collective-permute-start | bytes 589832 | tf_op jit(solution)/shard_map/ppermute | solution.py:249
  50.5 13.5 %collective-permute-start.1 = (bf16[16,16,768]{2,1,0:T(8,128)(2,1)S(1)}, bf16[16,16,768]{2,1,0:T(8,128)(2,1)S(1)}, u32[]{:S(2)}, u32[]{:S(2)}) collective-permute-start(bf16[16,16,768]{2,1,0:T(8,128)(2,1)S(1)} %pad_maximum_fusion.x_a), channel_id=1, source_target_pairs={{0,1},{1,2},{2,3},{3,0},{4,5},{5,6},{6,7},{7,4},{8,9},{9,10},{10,1... | collective-permute-start | bytes 1179656 | tf_op jit(solution)/shard_map/ppermute | solution.py:251
  52.4 21.1 %collective-permute-start.2 = (bf16[16,16,768]{2,1,0:T(8,128)(2,1)S(1)}, bf16[16,16,768]{2,1,0:T(8,128)(2,1)S(1)}, u32[]{:S(2)}, u32[]{:S(2)}) collective-permute-start(bf16[16,16,768]{2,1,0:T(8,128)(2,1)S(1)} %pad_maximum_fusion.x_a), channel_id=1, source_target_pairs={{0,2},{1,3},{2,0},{3,1},{4,6},{5,7},{6,4},{7,5},{8,10},{9,11},{10,... | collective-permute-start | bytes 1179656 | tf_op jit(solution)/shard_map/ppermute | solution.py:251
  56.0 17.6 %collective-permute-start.3 = (bf16[16,16,768]{2,1,0:T(8,128)(2,1)S(1)}, bf16[16,16,768]{2,1,0:T(8,128)(2,1)S(1)}, u32[]{:S(2)}, u32[]{:S(2)}) collective-permute-start(bf16[16,16,768]{2,1,0:T(8,128)(2,1)S(1)} %pad_maximum_fusion.x_a), channel_id=1, source_target_pairs={{0,3},{1,0},{2,1},{3,2},{4,7},{5,4},{6,5},{7,6},{8,11},{9,8},{10,9... | collective-permute-start | bytes 1179656 | tf_op jit(solution)/shard_map/ppermute | solution.py:251
  61.2 25.1 %collective-permute-start.5 = (bf16[8,16,3072]{2,1,0:T(8,128)(2,1)S(1)}, bf16[8,16,3072]{2,1,0:T(8,128)(2,1)S(1)}, u32[]{:S(2)}, u32[]{:S(2)}) collective-permute-start(bf16[8,16,3072]{2,1,0:T(8,128)(2,1)S(1)} %all-to-all-done.2.own), channel_id=1, source_target_pairs={{0,8},{8,0},{1,9},{9,1},{2,10},{10,2},{3,11},{11,3},{4,12},{12,4},... | collective-permute-start | bytes 2359304 | tf_op jit(solution)/shard_map/ppermute | solution.py:247
  85.2 1.2 copy-start.2
  124.5 3.2 %copy-start.3 = (f32[768]{0:T(1024)S(1)}, f32[768]{0:T(1024)}, u32[]{:S(2)}) copy-start(f32[768]{0:T(1024)} %param.7) | copy-start | bytes 9220
  124.5 14.2 %copy-start.1 = (f32[64]{0:T(128)S(1)}, f32[64]{0:T(128)}, u32[]{:S(2)}) copy-start(f32[64]{0:T(128)} %occ.1) | copy-start | bytes 772
  124.7 6.2 %collective-permute-start.6 = (f32[32,768]{1,0:T(8,128)S(1)}, f32[32,768]{1,0:T(8,128)S(1)}, u32[]{:S(2)}, u32[]{:S(2)}) collective-permute-start(f32[32,768]{1,0:T(8,128)S(1)} %bitcast.12), channel_id=1, source_target_pairs={{0,4},{4,0},{1,5},{5,1},{2,6},{6,2},{3,7},{7,3},{8,12},{12,8},{9,1... | collective-permute-start | bytes 294920 | tf_op jit(solution)/shard_map/ppermute | solution.py:256
  130.9 5.9 %collective-permute-start.7 = (f32[32,768]{1,0:T(8,128)S(1)}, f32[32,768]{1,0:T(8,128)S(1)}, u32[]{:S(2)}, u32[]{:S(2)}) collective-permute-start(f32[32,768]{1,0:T(8,128)S(1)} %bitcast_add_fusion.p_a), channel_id=1, source_target_pairs={{0,1},{1,2},{2,3},{3,0},{4,5},{5,6},{6,7},{7,4},{8,9},{9,10},{10,1... | collective-permute-start | bytes 294920 | tf_op jit(solution)/shard_map/ppermute | solution.py:257
  131.7 6.2 %collective-permute-start.8 = (f32[32,768]{1,0:T(8,128)S(1)}, f32[32,768]{1,0:T(8,128)S(1)}, u32[]{:S(2)}, u32[]{:S(2)}) collective-permute-start(f32[32,768]{1,0:T(8,128)S(1)} %bitcast_add_fusion.p_a), channel_id=1, source_target_pairs={{0,2},{1,3},{2,0},{3,1},{4,6},{5,7},{6,4},{7,5},{8,10},{9,11},{10,... | collective-permute-start | bytes 294920 | tf_op jit(solution)/shard_map/ppermute | solution.py:257
  133.2 5.6 %collective-permute-start.9 = (f32[32,768]{1,0:T(8,128)S(1)}, f32[32,768]{1,0:T(8,128)S(1)}, u32[]{:S(2)}, u32[]{:S(2)}) collective-permute-start(f32[32,768]{1,0:T(8,128)S(1)} %bitcast_add_fusion.p_a), channel_id=1, source_target_pairs={{0,3},{1,0},{2,1},{3,2},{4,7},{5,4},{6,5},{7,6},{8,11},{9,8},{10,9... | collective-permute-start | bytes 294920 | tf_op jit(solution)/shard_map/ppermute | solution.py:257

commit v10 on v9

--- a/solution.py
+++ b/solution.py
@@ -105,7 +105,9 @@
     for s, ref in enumerate((x_a, x_b, x_c, x_d)):
         q = (where[1] - s) & 3
         for k in range(16):
-            x2[k, q] = ref[k]
+            rel, cross, back = k // 8, (k // 4) % 2, k % 4
+            chip = ((where[2] - back) & 3) * 2 + (where[3] ^ cross)
+            x2[rel * NCHIP + chip, q] = ref[k]
     for cp in rows0:
         cp.wait()
     for cp in rows1:
@@ -160,7 +162,7 @@
 
 VMEM = pl.BlockSpec(memory_space=pltpu.VMEM)
 LATE_MIB = 50
-EARLY_MIB = 50
+EARLY_MIB = 52
 SMEM = pl.BlockSpec(memory_space=pltpu.SMEM)
 ANY = pl.BlockSpec(memory_space=pl.ANY)
 BLOCK = (16, OCC_DEV, HALF, NVIR)
@@ -232,10 +234,13 @@
 def body(fit_rows, trials, occ_energy, vir_energy):
     core = lax.axis_index("c").astype(jnp.int32)
     z = lax.axis_index("z").astype(jnp.int32)
-    where = jnp.stack([core, z])
+    where = jnp.stack([core, z, lax.axis_index("x").astype(jnp.int32), lax.axis_index("yl").astype(jnp.int32)])
     mine = [lax.dynamic_slice(trials, (half * HALF, z * NVIR), (HALF, NVIR)) for half in (core, 1 - core)]
-    mine = jnp.broadcast_to(jnp.concatenate(mine, 1)[None], (NCHIP, HALF, 2 * NVIR))
-    both = lax.all_to_all(mine, CHIPS, 0, 0, tiled=True)
+    x = jnp.concatenate(mine, 1)[None]
+    x = jnp.concatenate([x] + [lax.ppermute(x, "x", ring(4, s)) for s in (1, 2, 3)])
+    x = jnp.concatenate([x, lax.ppermute(x, "yl", ring(2, 1))])
+    x = jnp.concatenate([x[:, :, :NVIR], lax.ppermute(x[:, :, NVIR:], "c", ring(2, 1))])
+    x = [x] + [lax.ppermute(x, "z", ring(4, s)) for s in (1, 2, 3)]
     own, other, rows = [], [], fit_rows
     first = 0
     for t, steps in enumerate(STEPS):
@@ -245,10 +250,6 @@
         first += NCHIP * count
         rows = lax.optimization_barrier(rows)
         other.append(lax.ppermute(own[t], "c", ring(2, 1)))
-    x_own, x_send = both[:, :, :NVIR], both[:, :, NVIR:]
-    x_other = lax.ppermute(x_send, "c", ring(2, 1))
-    x = [jnp.concatenate([x_own, x_other])]
-    x = x + [lax.ppermute(x[0], "z", ring(4, s)) for s in (1, 2, 3)]
     acc, x2 = early(where, x, own, other)
     acc = late(where, x2, own, other, acc)
     parts = lax.all_to_all(acc, MOST, 0, 0, tiled=True)

time: 141 us -> 131 us (0.929)
  waiting for transfers between devices: 55.7 us -> 45.1 us
  starting transfers between devices: 26.1 us -> 29 us
  local copies, waits for them, and re-layouts: 6.72 us -> 4.82 us
    all_to_all x2, waiting for transfers between devices: 28.1 us -> 0.84 us  [body(): own.append(lax.all_to_all(send, CHIPS, 0, 0, tiled=True))]
    ppermute x4 -> x8, waiting for transfers between devices: 13.7 us -> 37.3 us  [the longest x3 17.6 us: body(): lax.ppermute(x, 'x', ring(4, s))]
    all_to_all x1 -> x0, waiting for transfers between devices: 6.86 us -> none  [body(): both = lax.all_to_all(mine, CHIPS, 0, 0, tiled=True)]
    ppermute x4 -> x8, starting transfers between devices: 6.66 us -> 13 us  [the longest x3 6.58 us: body(): x = [x] + [lax.ppermute(x, 'z', ring(4, s)) for s in (1, 2, 3)]]
    all_to_all x1 -> x0, starting transfers between devices: 3.45 us -> none  [body(): both = lax.all_to_all(mine, CHIPS, 0, 0, tiled=True)]
  transfers between devices with their start and end apart: 13 -> 16, of which waited for: 10 -> 11; matrix products, arithmetic and copies ran while one was open for 2% -> 2% of each run, Pallas kernels for 8% -> 9%
where the time goes in v10:
time: 131 us; the launch traced here: 130 us
  waiting for transfers between devices  45.1 us (34%)
  blocking collectives  31.2 us (24%)
  starting transfers between devices  29 us (22%)
  Pallas kernels  19.3 us (15%)
  local copies, waits for them, and re-layouts  4.82 us (4%)
    all_to_all x1, blocking collectives, body(): parts = lax.all_to_all(acc, MOST, 0, 0, tiled=True)  31.2 us
    ppermute x3, waiting for transfers between devices, body(): lax.ppermute(x, 'x', ring(4, s))  17.6 us
    ppermute x3, waiting for transfers between devices, body(): x = [x] + [lax.ppermute(x, 'z', ring(4, s)) for s in (1, 2, 3)]  15.6 us
    pallas_call x1, Pallas kernels, early(): pl.pallas_call(early_kernel, out_shape=[jax.ShapeDtypeStruct((ROWS, NVIR)...  11.5 us
    all_to_all x2, starting transfers between devices, body(): own.append(lax.all_to_all(send, CHIPS, 0, 0, tiled=True))  9.11 us
    ppermute x3, starting transfers between devices, body(): x = [x] + [lax.ppermute(x, 'z', ring(4, s)) for s in (1, 2, 3)]  6.58 us
    pallas_call x1, Pallas kernels, late(): pl.pallas_call(late_kernel, out_shape=jax.ShapeDtypeStruct(BLOCK, BF16),...  6.41 us
    ppermute x3, starting transfers between devices, body(): lax.ppermute(x, 'x', ring(4, s))  6.21 us
  transfers between devices with their start and end apart: 16, of which 11 were waited for; matrix products, arithmetic and copies ran while one was open for 2% of the time, Pallas kernels for 9%

profile of v10, /device:TPU:0, one launch (start us, length us, event | category | flops | bytes accessed | tf_op | source)
XLA Modules:
  0.0 130.1 jit_solution(15174571591650988490)
XLA Ops:
  0.0 2.7 %slice.14 = bf16[256,3072]{1,0:T(8,128)(2,1)} slice(bf16[384,3072]{1,0:T(8,128)(2,1)} %param.4), slice={[0:256], [0:3072]} | slice | bytes 3145728 | tf_op jit(solution)/shard_map/slice | solution.py:248
  2.7 0.0 copy-start
  2.7 5.6 %all-to-all-start = ((bf16[8,32,3072]{2,1,0:T(8,128)(2,1)}), bf16[8,32,3072]{2,1,0:T(8,128)(2,1)}, u32[]{:S(2)}, u32[]{:S(2)}) async-start(bf16[8,32,3072]{2,1,0:T(8,128)(2,1)} %bitcast.6), calls=%async_computation | async-start | bytes 3145728 | tf_op jit(solution)/shard_map/all_to_all | solution.py:249
  8.2 0.0 copy-done
  8.3 2.1 %collective-permute-start = (bf16[1,16,1536]{2,1,0:T(8,128)(2,1)S(1)}, bf16[1,16,1536]{2,1,0:T(8,128)(2,1)S(1)}, u32[]{:S(2)}, u32[]{:S(2)}) collective-permute-start(bf16[1,16,1536]{2,1,0:T(8,128)(2,1)S(1)} %maximum_bitcast_fusion), channel_id=1, source_target_pairs={{0,32},{32,64},{64,96},{96,0},{1,33},{33,65},{65,97},{97,1},{2,34}... | collective-permute-start | bytes 147464 | tf_op jit(solution)/shard_map/ppermute | solution.py:240
  10.4 2.7 %collective-permute-start.1 = (bf16[1,16,1536]{2,1,0:T(8,128)(2,1)S(1)}, bf16[1,16,1536]{2,1,0:T(8,128)(2,1)S(1)}, u32[]{:S(2)}, u32[]{:S(2)}) collective-permute-start(bf16[1,16,1536]{2,1,0:T(8,128)(2,1)S(1)} %maximum_bitcast_fusion), channel_id=1, source_target_pairs={{0,64},{32,96},{64,0},{96,32},{1,65},{33,97},{65,1},{97,33},{2,66}... | collective-permute-start | bytes 147464 | tf_op jit(solution)/shard_map/ppermute | solution.py:240
  13.0 1.5 %collective-permute-start.2 = (bf16[1,16,1536]{2,1,0:T(8,128)(2,1)S(1)}, bf16[1,16,1536]{2,1,0:T(8,128)(2,1)S(1)}, u32[]{:S(2)}, u32[]{:S(2)}) collective-permute-start(bf16[1,16,1536]{2,1,0:T(8,128)(2,1)S(1)} %maximum_bitcast_fusion), channel_id=1, source_target_pairs={{0,96},{32,0},{64,32},{96,64},{1,97},{33,1},{65,33},{97,65},{2,98}... | collective-permute-start | bytes 147464 | tf_op jit(solution)/shard_map/ppermute | solution.py:240
  14.5 2.1 %slice.18 = bf16[128,3072]{1,0:T(8,128)(2,1)} slice(bf16[384,3072]{1,0:T(8,128)(2,1)} %param.4), slice={[256:384], [0:3072]} | slice | bytes 1572864 | tf_op jit(solution)/shard_map/slice | solution.py:248
  16.6 11.3 %collective-permute-done = bf16[1,16,1536]{2,1,0:T(8,128)(2,1)S(1)} collective-permute-done((bf16[1,16,1536]{2,1,0:T(8,128)(2,1)S(1)}, bf16[1,16,1536]{2,1,0:T(8,128)(2,1)S(1)}, u32[]{:S(2)}, u32[]{:S(2)}) %collective-permute-start) | collective-permute-done | bytes 49184 | tf_op jit(solution)/shard_map/ppermute | solution.py:240
  27.9 6.2 %collective-permute-done.1 = bf16[1,16,1536]{2,1,0:T(8,128)(2,1)S(1)} collective-permute-done((bf16[1,16,1536]{2,1,0:T(8,128)(2,1)S(1)}, bf16[1,16,1536]{2,1,0:T(8,128)(2,1)S(1)}, u32[]{:S(2)}, u32[]{:S(2)}) %collective-permute-start.1) | collective-permute-done | bytes 49184 | tf_op jit(solution)/shard_map/ppermute | solution.py:240
  34.1 0.0 collective-permute-done.2
  34.1 0.1 collective-permute-start.3
  34.3 0.0 all-to-all-done.own
  34.3 3.6 %all-to-all-start.1 = ((bf16[8,16,3072]{2,1,0:T(8,128)(2,1)}), bf16[8,16,3072]{2,1,0:T(8,128)(2,1)S(1)}, u32[]{:S(2)}, u32[]{:S(2)}) async-start(bf16[8,16,3072]{2,1,0:T(8,128)(2,1)} %bitcast.7), calls=%async_computation.1 | async-start | bytes 1572864 | tf_op jit(solution)/shard_map/all_to_all | solution.py:249
  37.8 0.1 collective-permute-start.8
  38.0 2.6 %collective-permute-done.3 = bf16[4,16,1536]{2,1,0:T(8,128)(2,1)S(1)} collective-permute-done((bf16[4,16,1536]{2,1,0:T(8,128)(2,1)S(1)}, bf16[4,16,1536]{2,1,0:T(8,128)(2,1)S(1)}, u32[]{:S(2)}, u32[]{:S(2)}) %collective-permute-start.3) | collective-permute-done | bytes 196640 | tf_op jit(solution)/shard_map/ppermute | solution.py:241
  40.6 0.1 collective-permute-start.4
  40.7 1.4 %collective-permute-done.4 = bf16[8,16,768]{2,1,0:T(8,128)(2,1)S(1)} collective-permute-done((bf16[8,16,768]{2,1,0:T(8,128)(2,1)S(1)}, bf16[8,16,768]{2,1,0:T(8,128)(2,1)S(1)}, u32[]{:S(2)}, u32[]{:S(2)}) %collective-permute-start.4) | collective-permute-done | bytes 196640 | tf_op jit(solution)/shard_map/ppermute | solution.py:242
  42.2 2.0 %collective-permute-start.5 = (bf16[16,16,768]{2,1,0:T(8,128)(2,1)S(1)}, bf16[16,16,768]{2,1,0:T(8,128)(2,1)S(1)}, u32[]{:S(2)}, u32[]{:S(2)}) collective-permute-start(bf16[16,16,768]{2,1,0:T(8,128)(2,1)S(1)} %pad_maximum_fusion.x_a), channel_id=1, source_target_pairs={{0,1},{1,2},{2,3},{3,0},{4,5},{5,6},{6,7},{7,4},{8,9},{9,10},{10,1... | collective-permute-start | bytes 1179656 | tf_op jit(solution)/shard_map/ppermute | solution.py:243
  44.2 3.6 %collective-permute-start.6 = (bf16[16,16,768]{2,1,0:T(8,128)(2,1)S(1)}, bf16[16,16,768]{2,1,0:T(8,128)(2,1)S(1)}, u32[]{:S(2)}, u32[]{:S(2)}) collective-permute-start(bf16[16,16,768]{2,1,0:T(8,128)(2,1)S(1)} %pad_maximum_fusion.x_a), channel_id=1, source_target_pairs={{0,2},{1,3},{2,0},{3,1},{4,6},{5,7},{6,4},{7,5},{8,10},{9,11},{10,... | collective-permute-start | bytes 1179656 | tf_op jit(solution)/shard_map/ppermute | solution.py:243
  47.8 1.0 collective-permute-start.7
  48.8 0.8 all-to-all-done.1.own
  49.6 0.0 collective-permute-start.9
  49.6 0.1 pad_add_fusion.1.where
  49.7 6.0 %collective-permute-done.5.x_b = bf16[16,16,768]{2,1,0:T(8,128)(2,1)S(1)} collective-permute-done((bf16[16,16,768]{2,1,0:T(8,128)(2,1)S(1)}, bf16[16,16,768]{2,1,0:T(8,128)(2,1)S(1)}, u32[]{:S(2)}, u32[]{:S(2)}) %collective-permute-start.5) | collective-permute-done | bytes 393248 | tf_op jit(solution)/shard_map/ppermute | solution.py:243
  55.7 9.6 %collective-permute-done.6.x_c = bf16[16,16,768]{2,1,0:T(8,128)(2,1)S(1)} collective-permute-done((bf16[16,16,768]{2,1,0:T(8,128)(2,1)S(1)}, bf16[16,16,768]{2,1,0:T(8,128)(2,1)S(1)}, u32[]{:S(2)}, u32[]{:S(2)}) %collective-permute-start.6) | collective-permute-done | bytes 393248 | tf_op jit(solution)/shard_map/ppermute | solution.py:243
  65.3 0.0 collective-permute-done.7.x_d
  65.3 0.0 collective-permute-done.8.other
  65.3 11.5 %terms_early.1 = (f32[1024,768]{1,0:T(8,128)}, bf16[16,4,16,768]{3,2,1,0:T(8,128)(2,1)}) custom-call(s32[4]{0:T(128)S(1)} %pad_add_fusion.1.where, bf16[16,16,768]{2,1,0:T(8,128)(2,1)S(1)} %pad_maximum_fusion.x_a, bf16[16,16,768]{2,1,0:T(8,128)(2,1)S(1)} %collective-permute-done.5.x_b, bf16[16,16,768]{2,1,0:T(8,128)(2,1)S(1)} %collective-permute-done.6.x_c, ...), custom_call_target="tpu_custom_call" | custom-call | flops 6442450944 | bytes 6291456 | tf_op jit(solution)/shard_map/terms_early/pallas_call | solution.py:176
  76.9 0.0 collective-permute-done.9.other
  76.9 6.4 %terms_late.1 = bf16[16,4,16,768]{3,2,1,0:T(8,128)(2,1)S(1)} custom-call(s32[4]{0:T(128)S(1)} %pad_add_fusion.1.where, bf16[16,4,16,768]{3,2,1,0:T(8,128)(2,1)} %get-tuple-element.7.x_in, bf16[8,16,3072]{2,1,0:T(8,128)(2,1)S(1)} %all-to-all-done.1.own, bf16[8,16,3072]{2,1,0:T(8,128)(2,1)S(1)} %collective-permute-done.9.other, ...), custom_call_target="tpu_custom_call" | custom-call | flops 3221225472 | bytes 6291456 | tf_op jit(solution)/shard_map/terms_late/pallas_call | solution.py:199
  83.3 31.2 %all_to_all.15 = bf16[64,16,768]{2,1,0:T(8,128)(2,1)S(1)} all-to-all(bf16[64,16,768]{2,1,0:T(8,128)(2,1)S(1)} %bitcast.16), channel_id=1, replica_groups=mesh['x'=4,'yl'=2,'c'=2,'yh'=2,'z'=4] {'x','yl','c','z'}, dimensions={0} | all-to-all | bytes 3145728 | tf_op jit(solution)/shard_map/all_to_all | solution.py:255
  114.5 0.0 copy-start.2
  114.5 0.0 copy-start.1
  114.5 0.2 convert_reduce_fusion
  114.8 3.0 %collective-permute-start.10 = (f32[32,768]{1,0:T(8,128)S(1)}, f32[32,768]{1,0:T(8,128)S(1)}, u32[]{:S(2)}, u32[]{:S(2)}) collective-permute-start(f32[32,768]{1,0:T(8,128)S(1)} %bitcast.18), channel_id=1, source_target_pairs={{0,4},{4,0},{1,5},{5,1},{2,6},{6,2},{3,7},{7,3},{8,12},{12,8},{9,1... | collective-permute-start | bytes 294920 | tf_op jit(solution)/shard_map/ppermute | solution.py:257
  117.7 0.0 copy-done.2
  117.8 3.2 %collective-permute-done.10 = f32[32,768]{1,0:T(8,128)S(1)} collective-permute-done((f32[32,768]{1,0:T(8,128)S(1)}, f32[32,768]{1,0:T(8,128)S(1)}, u32[]{:S(2)}, u32[]{:S(2)}) %collective-permute-start.10) | collective-permute-done | bytes 98336 | tf_op jit(solution)/shard_map/ppermute | solution.py:257
  121.0 0.7 collective-permute-start.11
  121.7 1.5 %collective-permute-start.12 = (f32[32,768]{1,0:T(8,128)S(1)}, f32[32,768]{1,0:T(8,128)S(1)}, u32[]{:S(2)}, u32[]{:S(2)}) collective-permute-start(f32[32,768]{1,0:T(8,128)S(1)} %bitcast_add_fusion.p_a), channel_id=1, source_target_pairs={{0,2},{1,3},{2,0},{3,1},{4,6},{5,7},{6,4},{7,5},{8,10},{9,11},{10,... | collective-permute-start | bytes 294920 | tf_op jit(solution)/shard_map/ppermute | solution.py:258
  123.2 1.7 %collective-permute-start.13 = (f32[32,768]{1,0:T(8,128)S(1)}, f32[32,768]{1,0:T(8,128)S(1)}, u32[]{:S(2)}, u32[]{:S(2)}) collective-permute-start(f32[32,768]{1,0:T(8,128)S(1)} %bitcast_add_fusion.p_a), channel_id=1, source_target_pairs={{0,3},{1,0},{2,1},{3,2},{4,7},{5,4},{6,5},{7,6},{8,11},{9,8},{10,9... | collective-permute-start | bytes 294920 | tf_op jit(solution)/shard_map/ppermute | solution.py:258
  124.9 0.1 pad_add_fusion.where
  125.0 1.9 %collective-permute-done.11.p_b = f32[32,768]{1,0:T(8,128)S(1)} collective-permute-done((f32[32,768]{1,0:T(8,128)S(1)}, f32[32,768]{1,0:T(8,128)S(1)}, u32[]{:S(2)}, u32[]{:S(2)}) %collective-permute-start.11) | collective-permute-done | bytes 98336 | tf_op jit(solution)/shard_map/ppermute | solution.py:258
  126.9 1.0 collective-permute-done.12.p_c
  127.9 0.9 collective-permute-done.13.p_d
  128.8 0.0 copy-done.1
  128.8 1.3 %final.1 = f32[32,3072]{1,0:T(8,128)} custom-call(s32[2]{0:T(128)S(1)} %pad_add_fusion.where, f32[64]{0:T(128)S(1)} %copy-done.1, f32[1,768]{1,0:T(1,128)S(1)} %reshape.18.vir, bf16[32,3072]{1,0:T(8,128)(2,1)S(1)} %copy-done, f32[32,768]{1,0:T(8,128)S(1)} %bitcast_add_fusion.p_a, f32[32,768]{1,0:T(8,128)S(1)} %collective-permute-done.11.p_b, ...), custom_call_target="tpu_custom_call" | custom-call | tf_op jit(solution)/shard_map/final/pallas_call | solution.py:220
  (12 shorter events, 0.2 us)
Async XLA Ops:
  2.7 5.6 %copy-start = (bf16[32,3072]{1,0:T(8,128)(2,1)S(1)}, bf16[32,3072]{1,0:T(8,128)(2,1)}, u32[]{:S(2)}) copy-start(bf16[32,3072]{1,0:T(8,128)(2,1)} %trials.1) | copy-start | bytes 589828
  2.7 31.6 %all-to-all-start = ((bf16[8,32,3072]{2,1,0:T(8,128)(2,1)}), bf16[8,32,3072]{2,1,0:T(8,128)(2,1)}, u32[]{:S(2)}, u32[]{:S(2)}) async-start(bf16[8,32,3072]{2,1,0:T(8,128)(2,1)} %bitcast.6), calls=%async_computation | async-start | bytes 3145728 | tf_op jit(solution)/shard_map/all_to_all | solution.py:249
  8.3 19.6 %collective-permute-start = (bf16[1,16,1536]{2,1,0:T(8,128)(2,1)S(1)}, bf16[1,16,1536]{2,1,0:T(8,128)(2,1)S(1)}, u32[]{:S(2)}, u32[]{:S(2)}) collective-permute-start(bf16[1,16,1536]{2,1,0:T(8,128)(2,1)S(1)} %maximum_bitcast_fusion), channel_id=1, source_target_pairs={{0,32},{32,64},{64,96},{96,0},{1,33},{33,65},{65,97},{97,1},{2,34}... | collective-permute-start | bytes 147464 | tf_op jit(solution)/shard_map/ppermute | solution.py:240
  10.4 23.8 %collective-permute-start.1 = (bf16[1,16,1536]{2,1,0:T(8,128)(2,1)S(1)}, bf16[1,16,1536]{2,1,0:T(8,128)(2,1)S(1)}, u32[]{:S(2)}, u32[]{:S(2)}) collective-permute-start(bf16[1,16,1536]{2,1,0:T(8,128)(2,1)S(1)} %maximum_bitcast_fusion), channel_id=1, source_target_pairs={{0,64},{32,96},{64,0},{96,32},{1,65},{33,97},{65,1},{97,33},{2,66}... | collective-permute-start | bytes 147464 | tf_op jit(solution)/shard_map/ppermute | solution.py:240
  13.0 21.1 %collective-permute-start.2 = (bf16[1,16,1536]{2,1,0:T(8,128)(2,1)S(1)}, bf16[1,16,1536]{2,1,0:T(8,128)(2,1)S(1)}, u32[]{:S(2)}, u32[]{:S(2)}) collective-permute-start(bf16[1,16,1536]{2,1,0:T(8,128)(2,1)S(1)} %maximum_bitcast_fusion), channel_id=1, source_target_pairs={{0,96},{32,0},{64,32},{96,64},{1,97},{33,1},{65,33},{97,65},{2,98}... | collective-permute-start | bytes 147464 | tf_op jit(solution)/shard_map/ppermute | solution.py:240
  34.1 6.4 %collective-permute-start.3 = (bf16[4,16,1536]{2,1,0:T(8,128)(2,1)S(1)}, bf16[4,16,1536]{2,1,0:T(8,128)(2,1)S(1)}, u32[]{:S(2)}, u32[]{:S(2)}) collective-permute-start(bf16[4,16,1536]{2,1,0:T(8,128)(2,1)S(1)} %pad_maximum_fusion.1), channel_id=1, source_target_pairs={{0,16},{16,0},{1,17},{17,1},{2,18},{18,2},{3,19},{19,3},{4,20},{20... | collective-permute-start | bytes 589832 | tf_op jit(solution)/shard_map/ppermute | solution.py:241
  34.3 15.4 %all-to-all-start.1 = ((bf16[8,16,3072]{2,1,0:T(8,128)(2,1)}), bf16[8,16,3072]{2,1,0:T(8,128)(2,1)S(1)}, u32[]{:S(2)}, u32[]{:S(2)}) async-start(bf16[8,16,3072]{2,1,0:T(8,128)(2,1)} %bitcast.7), calls=%async_computation.1 | async-start | bytes 1572864 | tf_op jit(solution)/shard_map/all_to_all | solution.py:249
  37.8 27.5 %collective-permute-start.8 = (bf16[8,32,3072]{2,1,0:T(8,128)(2,1)}, bf16[8,32,3072]{2,1,0:T(8,128)(2,1)}, u32[]{:S(2)}, u32[]{:S(2)}) collective-permute-start(bf16[8,32,3072]{2,1,0:T(8,128)(2,1)} %all-to-all-done.own), channel_id=1, source_target_pairs={{0,8},{8,0},{1,9},{9,1},{2,10},{10,2},{3,11},{11,3},{4,12},{12,4},... | collective-permute-start | bytes 4718600 | tf_op jit(solution)/shard_map/ppermute | solution.py:252
  40.6 1.5 %collective-permute-start.4 = (bf16[8,16,768]{2,1,0:T(8,128)(2,1)S(1)}, bf16[8,16,768]{2,1,0:T(8,128)(2,1)S(1)}, u32[]{:S(2)}, u32[]{:S(2)}) collective-permute-start(bf16[8,16,768]{2,1,0:T(8,128)(2,1)S(1)} %get-tuple-element.10), channel_id=1, source_target_pairs={{0,8},{8,0},{1,9},{9,1},{2,10},{10,2},{3,11},{11,3},{4,12},{12,4},... | collective-permute-start | bytes 589832 | tf_op jit(solution)/shard_map/ppermute | solution.py:242
  42.2 13.5 %collective-permute-start.5 = (bf16[16,16,768]{2,1,0:T(8,128)(2,1)S(1)}, bf16[16,16,768]{2,1,0:T(8,128)(2,1)S(1)}, u32[]{:S(2)}, u32[]{:S(2)}) collective-permute-start(bf16[16,16,768]{2,1,0:T(8,128)(2,1)S(1)} %pad_maximum_fusion.x_a), channel_id=1, source_target_pairs={{0,1},{1,2},{2,3},{3,0},{4,5},{5,6},{6,7},{7,4},{8,9},{9,10},{10,1... | collective-permute-start | bytes 1179656 | tf_op jit(solution)/shard_map/ppermute | solution.py:243
  44.2 21.1 %collective-permute-start.6 = (bf16[16,16,768]{2,1,0:T(8,128)(2,1)S(1)}, bf16[16,16,768]{2,1,0:T(8,128)(2,1)S(1)}, u32[]{:S(2)}, u32[]{:S(2)}) collective-permute-start(bf16[16,16,768]{2,1,0:T(8,128)(2,1)S(1)} %pad_maximum_fusion.x_a), channel_id=1, source_target_pairs={{0,2},{1,3},{2,0},{3,1},{4,6},{5,7},{6,4},{7,5},{8,10},{9,11},{10,... | collective-permute-start | bytes 1179656 | tf_op jit(solution)/shard_map/ppermute | solution.py:243
  47.8 17.6 %collective-permute-start.7 = (bf16[16,16,768]{2,1,0:T(8,128)(2,1)S(1)}, bf16[16,16,768]{2,1,0:T(8,128)(2,1)S(1)}, u32[]{:S(2)}, u32[]{:S(2)}) collective-permute-start(bf16[16,16,768]{2,1,0:T(8,128)(2,1)S(1)} %pad_maximum_fusion.x_a), channel_id=1, source_target_pairs={{0,3},{1,0},{2,1},{3,2},{4,7},{5,4},{6,5},{7,6},{8,11},{9,8},{10,9... | collective-permute-start | bytes 1179656 | tf_op jit(solution)/shard_map/ppermute | solution.py:243
  49.6 27.3 %collective-permute-start.9 = (bf16[8,16,3072]{2,1,0:T(8,128)(2,1)S(1)}, bf16[8,16,3072]{2,1,0:T(8,128)(2,1)S(1)}, u32[]{:S(2)}, u32[]{:S(2)}) collective-permute-start(bf16[8,16,3072]{2,1,0:T(8,128)(2,1)S(1)} %all-to-all-done.1.own), channel_id=1, source_target_pairs={{0,8},{8,0},{1,9},{9,1},{2,10},{10,2},{3,11},{11,3},{4,12},{12,4},... | collective-permute-start | bytes 2359304 | tf_op jit(solution)/shard_map/ppermute | solution.py:252
  114.5 3.2 %copy-start.2 = (f32[768]{0:T(1024)S(1)}, f32[768]{0:T(1024)}, u32[]{:S(2)}) copy-start(f32[768]{0:T(1024)} %param.7) | copy-start | bytes 9220
  114.5 14.3 %copy-start.1 = (f32[64]{0:T(128)S(1)}, f32[64]{0:T(128)}, u32[]{:S(2)}) copy-start(f32[64]{0:T(128)} %occ.1) | copy-start | bytes 772
  114.8 6.2 %collective-permute-start.10 = (f32[32,768]{1,0:T(8,128)S(1)}, f32[32,768]{1,0:T(8,128)S(1)}, u32[]{:S(2)}, u32[]{:S(2)}) collective-permute-start(f32[32,768]{1,0:T(8,128)S(1)} %bitcast.18), channel_id=1, source_target_pairs={{0,4},{4,0},{1,5},{5,1},{2,6},{6,2},{3,7},{7,3},{8,12},{12,8},{9,1... | collective-permute-start | bytes 294920 | tf_op jit(solution)/shard_map/ppermute | solution.py:257
  121.0 5.9 %collective-permute-start.11 = (f32[32,768]{1,0:T(8,128)S(1)}, f32[32,768]{1,0:T(8,128)S(1)}, u32[]{:S(2)}, u32[]{:S(2)}) collective-permute-start(f32[32,768]{1,0:T(8,128)S(1)} %bitcast_add_fusion.p_a), channel_id=1, source_target_pairs={{0,1},{1,2},{2,3},{3,0},{4,5},{5,6},{6,7},{7,4},{8,9},{9,10},{10,1... | collective-permute-start | bytes 294920 | tf_op jit(solution)/shard_map/ppermute | solution.py:258
  121.7 6.2 %collective-permute-start.12 = (f32[32,768]{1,0:T(8,128)S(1)}, f32[32,768]{1,0:T(8,128)S(1)}, u32[]{:S(2)}, u32[]{:S(2)}) collective-permute-start(f32[32,768]{1,0:T(8,128)S(1)} %bitcast_add_fusion.p_a), channel_id=1, source_target_pairs={{0,2},{1,3},{2,0},{3,1},{4,6},{5,7},{6,4},{7,5},{8,10},{9,11},{10,... | collective-permute-start | bytes 294920 | tf_op jit(solution)/shard_map/ppermute | solution.py:258
  123.2 5.6 %collective-permute-start.13 = (f32[32,768]{1,0:T(8,128)S(1)}, f32[32,768]{1,0:T(8,128)S(1)}, u32[]{:S(2)}, u32[]{:S(2)}) collective-permute-start(f32[32,768]{1,0:T(8,128)S(1)} %bitcast_add_fusion.p_a), channel_id=1, source_target_pairs={{0,3},{1,0},{2,1},{3,2},{4,7},{5,4},{6,5},{7,6},{8,11},{9,8},{10,9... | collective-permute-start | bytes 294920 | tf_op jit(solution)/shard_map/ppermute | solution.py:258
